TPU v7x, 128 devices: a whole 4x4x4 slice. The times are simulated.
128 devices in a mesh: row: 8 (over x_hi, y), col: 16 (over x_lo, z, core).
Axes of the slice: x: 4 (x_hi: 2, x_lo: 2; x = x_hi * 2 + x_lo), y: 4, z: 4, core: 2. Of those that a mesh axis runs over, the one named last changes fastest.
Arguments:
- activations: bfloat16 [48, 512, 2048], P('row', 'col'), may hold values from -6 to 6
- targets: int32 [48, 512], P('row', 'col'), may hold values from 0 to 255
- candidates: int32 [1024], replicated, may hold values from 0 to 24575
- mix_gain: float32 [2048], replicated, may hold values from 0.1 to 1.9
- project_weight: bfloat16 [3, 2048, 2048], P(None, None, 'col'), may hold values from -0.1875 to 0.1875
- output_weight: bfloat16 [2048, 2048], P('col'), may hold values from -0.25 to 0.25
- up_weight: bfloat16 [2048, 8192], P(None, 'col'), as said below
- down_weight: bfloat16 [8192, 2048], P('col'), as said below
- pattern_bias: float32 [16], P('col'), may hold values from 1 to 5
- head_gain: float32 [2048], replicated, may hold values from 0.1 to 1.9
- head_weight: bfloat16 [2048, 256], replicated, may hold values from -0.375 to 0.375
Outputs:
- layer_out: bfloat16 [48, 512, 2048], P('row', 'col')
- chosen: float32 [1024], replicated
Inputs may be any that keep to these rules, and one draw needn't show every extreme that they name: `up_weight`: Real-valued weights of fan-in scale. `down_weight`: Real-valued weights of fan-in scale.
All inputs are finite; a program needn't handle non-finite values.
Results may differ from a plain program's by a relative error of at most 0.018.
Values may be sent and summed in bfloat16 or wider, within the bound.
No kernel may reach another device: no remote copies, remote signals or barrier semaphores. Data moves between devices by JAX's collectives and lax.ppermute only.
A program may use at most 128 MiB of HBM per device.

v0:
```python
import math

import jax
import jax.numpy as jnp
from jax import lax
from jax.experimental import pallas as pl
from jax.experimental.pallas import tpu as pltpu
from jax.sharding import Mesh
from jax.sharding import PartitionSpec as P

COL = ("col_0", "col_1", "col_2")
ROW = ("row_0", "row_1")
ALL = ("row_0", "row_1", "col_0", "col_1", "col_2")
XL, Z, CORE = COL

EPS = 1e-06
F32 = jnp.float32
BF16 = jnp.bfloat16


def permuted(array, axis, by):
    n = lax.axis_size(axis)
    return lax.ppermute(array, axis, [(i, (i + by) % n) for i in range(n)])


def up_z(array):
    return permuted(array, Z, 1)


def down_z(array):
    return permuted(array, Z, -1)


def swap_x(array):
    return permuted(array, XL, 1)


def swap_core(array):
    return permuted(array, CORE, 1)


def next_row(array):
    n = lax.axis_size(ROW)
    return lax.ppermute(array, ROW, [(i, i + 1) for i in range(n - 1)])


def dot(a, b):
    return jnp.dot(a, b, preferred_element_type=F32)


def dot_t(a, b):
    return lax.dot_general(a, b, (((1,), (1,)), ((), ())), preferred_element_type=F32)


def cost(flops, bytes_accessed, exps=0):
    return pl.CostEstimate(flops=flops, bytes_accessed=bytes_accessed, transcendentals=exps)


VMEM = pl.BlockSpec(memory_space=pltpu.VMEM)
SMEM = pl.BlockSpec(memory_space=pltpu.SMEM)
HALF = 16


def laid(column, lanes=256):
    shape = (column.shape[0], lanes)
    hit = lax.broadcasted_iota(jnp.int32, shape, 1) == lax.broadcasted_iota(jnp.int32, shape, 0)
    return jnp.sum(jnp.where(hit, column, 0.0), axis=0, keepdims=True)


def norm_body(x, gain, out):
    v = x[...].astype(F32)
    scale = lax.rsqrt(jnp.sum(v * v, axis=-1, keepdims=True) / v.shape[1] + EPS)
    out[...] = (v * scale * gain[...]).astype(BF16)


def normalize(x, gain):
    return pl.pallas_call(
        norm_body,
        in_specs=[VMEM, VMEM],
        out_specs=VMEM,
        out_shape=jax.ShapeDtypeStruct(x.shape, BF16),
        cost_estimate=cost(5 * x.size, 4 * x.size),
        name="normalize",
    )(x, gain)


def stacked(refs):
    return jnp.concatenate([ref[...] for ref in refs], axis=0)


def project_body(rows, n, *refs):
    mine, theirs, out = refs[n:]
    x = stacked(refs[:n])
    w = jnp.concatenate([mine[0], theirs[0]], axis=1)
    y = dot(x, w).astype(BF16).reshape(4, rows, 2, HALF, w.shape[1])
    for g in range(2):
        out[:, g] = y[:, :, g]


def project(shards, mine, theirs, rows):
    n = len(shards)
    total = sum(v.shape[0] for v in shards)
    _, width, hs = mine.shape
    whole = [pl.BlockSpec(v.shape, lambda j: (0, 0)) for v in shards]
    weight = pl.BlockSpec((1, width, hs), lambda j: (j, 0, 0))
    return pl.pallas_call(
        lambda *refs: project_body(rows, n, *refs),
        grid=(3,),
        in_specs=whole + [weight] * 2,
        out_specs=pl.BlockSpec((4, 2, rows, HALF, 2 * hs), lambda j: (0, 0, 0, 0, j)),
        out_shape=jax.ShapeDtypeStruct((4, 2, rows, HALF, 6 * hs), BF16),
        cost_estimate=cost(2 * total * width * 6 * hs, 2 * total * width + 12 * width * hs),
        name="project",
    )(*shards, mine, theirs)


def forward_body(n, *refs):
    up, their_up, down, their_down = refs[n : n + 4]
    outs, (acc, sums) = refs[n + 4 : -2], refs[-2:]
    step = pl.program_id(0)
    x = stacked(refs[:n])
    h = dot(x, jnp.concatenate([up[...], their_up[...]], axis=1))
    h = jax.nn.gelu(h, approximate=True).astype(BF16)
    h_f = h.astype(F32)
    part = jnp.sum(h_f * h_f, axis=-1, keepdims=True)
    term = dot(h, jnp.concatenate([down[...], their_down[...]], axis=0))

    @pl.when(step == 0)
    def _():
        acc[...] = term
        sums[...] = jnp.broadcast_to(part, sums.shape)

    @pl.when(step == 1)
    def _():
        width = acc.shape[1]
        total = (acc[...] + term).astype(BF16)
        squares = (sums[...] + part).astype(BF16)
        tokens = outs[0].shape[0]
        for i, out in enumerate(outs):
            at = slice(tokens * i, tokens * (i + 1))
            out[:, 0:width] = total[at]
            out[:, width : width + 128] = squares[at]


def feed_forward(shards, slots, up, their_up, down, their_down):
    n = len(shards)
    total = sum(v.shape[0] for v in shards)
    tokens, width = total // slots, shards[0].shape[1]
    units = up.shape[1] // 2
    whole = [pl.BlockSpec(v.shape, lambda j: (0, 0)) for v in shards]
    rise = pl.BlockSpec((width, units), lambda j: (0, j))
    fall = pl.BlockSpec((units, width), lambda j: (j, 0))
    return pl.pallas_call(
        lambda *refs: forward_body(n, *refs),
        grid=(2,),
        in_specs=whole + [rise, rise, fall, fall],
        out_specs=[pl.BlockSpec((tokens, width + 128), lambda j: (0, 0))] * slots,
        out_shape=[jax.ShapeDtypeStruct((tokens, width + 128), BF16)] * slots,
        scratch_shapes=[pltpu.VMEM((total, width), F32), pltpu.VMEM((total, 128), F32)],
        cost_estimate=cost(16 * total * width * units, 4 * total * width + 16 * width * units),
        name="feed_forward",
    )(*shards, up, their_up, down, their_down)


def row_body(inv_root, hs, top_ref, qcol, kcol, *refs):
    (cur0, cur1, prv0, prv1, pcur0, pcur1, pprv0, pprv1) = refs[:8]
    (edge0, edge1, pedge0, pedge1) = refs[8:12]
    accs, dens = refs[12:14], refs[14:16]
    r = pl.program_id(0)
    first = r == 0
    n = qcol.shape[0] // 2
    mask = kcol[...] <= qcol[...]
    open_prev = jnp.logical_not(jnp.logical_and(first, top_ref[0] == 1))
    used = jnp.logical_or(mask, jnp.broadcast_to(open_prev, mask.shape))

    def part(ref, at):
        return ref[:, :, 0, :, at : at + hs].reshape(n, hs)

    def edge_part(ref, at):
        return ref[:, :, :, at : at + hs].reshape(n, hs)

    def either(prv, edge, at):
        return jnp.where(first, edge_part(edge, at), part(prv, 2 * hs + at))

    for h in range(2):
        q = jnp.concatenate([part(cur0, h * hs), part(cur1, h * hs)], axis=0)

        def pair(base):
            a, b = base + hs * h, base + hs * (1 - h)
            same = [part(cur0, 2 * hs + a), part(cur1, 2 * hs + a)]
            same += [part(pcur0, 2 * hs + b), part(pcur1, 2 * hs + b)]
            prev = [either(prv0, edge0, a), either(prv1, edge1, a)]
            prev += [either(pprv0, pedge0, b), either(pprv1, pedge1, b)]
            return jnp.concatenate(same, axis=0), jnp.concatenate(prev, axis=0)

        k_same, k_prev = pair(0)
        v_same, v_prev = pair(2 * hs)
        scores = jnp.where(mask, dot_t(q, k_same), dot_t(q, k_prev)) * inv_root
        w = jnp.where(used, jnp.exp(scores), 0.0)
        total = jnp.sum(w, axis=-1, keepdims=True)
        w_same = jnp.where(mask, w, 0.0).astype(BF16)
        w_prev = jnp.where(mask, 0.0, w).astype(BF16)
        out = dot(w_same, v_same) + dot(w_prev, v_prev)
        total = jnp.broadcast_to(total, out.shape)
        for i in range(2):
            at = slice(h * hs, (h + 1) * hs)
            shape = (4, 2, HALF, hs)
            accs[i][:, :, 0, :, at] = out[n * i : n * (i + 1)].reshape(shape)
            dens[i][:, :, 0, :, at] = total[n * i : n * (i + 1)].reshape(shape)


def row_attention(top, qcol, kcol, qkv, their_qkv, edge, their_edge, hs, inv_root):
    rows = qkv[0].shape[2]
    width = 6 * hs
    now = pl.BlockSpec((4, 2, 1, HALF, width), lambda r: (0, 0, r, 0, 0))
    before = pl.BlockSpec(
        (4, 2, 1, HALF, width), lambda r: (0, 0, jnp.maximum(r - 1, 0), 0, 0)
    )
    whole = lambda a: pl.BlockSpec(a.shape, lambda r: (0,) * a.ndim)
    out = jax.ShapeDtypeStruct((4, 2, rows, HALF, 2 * hs), F32)
    out_spec = pl.BlockSpec((4, 2, 1, HALF, 2 * hs), lambda r: (0, 0, r, 0, 0))
    n = qcol.shape[0]
    outs = pl.pallas_call(
        lambda *refs: row_body(inv_root, hs, *refs),
        grid=(rows,),
        in_specs=[SMEM, whole(qcol), whole(kcol)]
        + [now, now, before, before] * 2
        + [whole(e) for e in (*edge, *their_edge)],
        out_specs=[out_spec] * 4,
        out_shape=[out] * 4,
        cost_estimate=cost(rows * 32 * n * n * hs, rows * 32 * n * hs, rows * 4 * n * n),
        name="row_attention",
    )(top, qcol, kcol, *qkv, *qkv, *their_qkv, *their_qkv, *edge, *their_edge)
    return outs[:2], outs[2:]


def col_body(inv_root, hs, own_rows, bias, x, *refs):
    out = refs[-1]
    rows, cols, _ = x.shape
    chunk = 16
    spots = rows * cols
    step = chunk * cols
    den_rows = jnp.zeros((rows, 128), F32)
    lane = lax.broadcasted_iota(jnp.int32, (spots, 128), 1)
    spot = lax.broadcasted_iota(jnp.int32, (spots, 128), 0)
    for h in range(2):

        def part(at):
            return x[:, :, at * hs : (at + 1) * hs].reshape(spots, hs)

        q, k, v = part(h), part(2 + h), part(4 + h)
        accs, sums = [], []
        for i in range(rows // chunk):
            n = step * (i + 1)
            s = dot_t(q[step * i : step * (i + 1)], k[:n]) * inv_root + bias[h]
            qi = lax.broadcasted_iota(jnp.int32, s.shape, 0) + step * i
            ki = lax.broadcasted_iota(jnp.int32, s.shape, 1)
            keep = jnp.logical_and(((qi - ki) & (cols - 1)) == 0, ki < qi)
            w = jnp.where(keep, jnp.exp(s), 0.0)
            accs.append(dot(w.astype(BF16), v[:n]))
            sums.append(jnp.sum(w, axis=-1, keepdims=True))
        a = jnp.concatenate(accs, axis=0).astype(BF16).reshape(rows, cols, hs)
        d = jnp.concatenate(sums, axis=0)
        spread = jnp.where(lane == (spot & (cols - 1)) + cols * h, d, 0.0)
        den_rows = den_rows + jnp.sum(spread.reshape(rows, cols, 128), axis=1)
        for r in range(rows):
            out[r // own_rows, 0, r % own_rows, :, h * hs : (h + 1) * hs] = a[r]
    fill = jnp.zeros((cols - own_rows, 128), F32)
    for b in range(rows // own_rows):
        block = jnp.concatenate([den_rows[own_rows * b : own_rows * (b + 1)], fill], axis=0)
        out[b, 0, own_rows, :, 0:128] = block.astype(BF16)
        out[b, 0, own_rows, :, 128:256] = jnp.zeros((cols, 128), BF16)


def column_attention(group, bias, x, own_rows, hs, inv_root, earlier=()):
    rows, cols, _ = x.shape
    spots = rows * cols
    peers = rows // own_rows
    return pl.pallas_call(
        lambda *refs: col_body(inv_root, hs, own_rows, *refs),
        grid=(1,),
        in_specs=[SMEM, pl.BlockSpec(x.shape, lambda i: (0, 0, 0))]
        + [pl.BlockSpec(memory_space=pl.ANY)] * len(earlier),
        out_specs=pl.BlockSpec(
            (peers, 1, own_rows + 1, cols, 2 * hs), lambda i: (0, group, 0, 0, 0)
        ),
        out_shape=jax.ShapeDtypeStruct((peers, 2, own_rows + 1, cols, 2 * hs), BF16),
        input_output_aliases={2: 0} if earlier else {},
        cost_estimate=cost(6 * spots * spots * hs, 16 * spots * hs, 2 * spots * spots),
        name="column_attention",
    )(bias, x, *earlier)


def term_body(hs, rows, group, splits, got, acc, den, f0, f1, f2, f3, w_mine, w_their, *outs):
    spots = 8 * rows * HALF
    unit = lax.broadcasted_iota(jnp.int32, (spots, 128), 0) // HALF
    line = lax.broadcasted_iota(jnp.int32, (spots, 128), 1)
    hit = jnp.logical_and(unit == (line // HALF) * rows + line % HALF, line % HALF < rows)
    table = got[:, group, rows, :, 0:128].reshape(128, 128)
    table = dot(jnp.where(hit, 1.0, 0.0).astype(BF16), table)
    spot = lax.broadcasted_iota(jnp.int32, (spots, 128), 0) % HALF
    ones = jnp.ones((128, 128), BF16)
    parts = []
    for h in range(2):
        at = slice(h * hs, (h + 1) * hs)
        col_den = dot(jnp.where(line == spot + HALF * h, table, 0.0).astype(BF16), ones)
        total = acc[:, :, :, :, at].reshape(spots, hs)
        total = total + got[:, group, 0:rows, :, at].reshape(spots, hs).astype(F32)
        parts.append((total / (den[:, :, :, :, at].reshape(spots, hs) + col_den)).astype(BF16))
    halves = jnp.concatenate(parts, axis=1).reshape(4, 2, rows, HALF, 2 * hs)
    blocks = [halves[s, g, r] for s in range(4) for r in range(rows) for g in range(2)]
    attended = jnp.concatenate(blocks, axis=0)
    att_f = attended.astype(F32)
    squares = jnp.sum(att_f * att_f, axis=-1, keepdims=True)
    weight = jnp.concatenate([w_mine[...], w_their[...]], axis=0)
    term = dot(attended, weight)
    width = term.shape[1]
    for out, (slot, low, high) in zip(outs, splits):
        f = (f0, f1, f2, f3)[slot]
        tokens = f.shape[0]
        at = slice(tokens * slot + low, tokens * slot + high)
        out[:, 0:width] = (f[low:high, 0:width].astype(F32) + term[at]).astype(BF16)
        out[:, width:] = (f[low:high, width:].astype(F32) + squares[at]).astype(BF16)


def terms(group, got, acc, den, ff, w_mine, w_their, hs, rows, splits):
    tokens, full = ff[0].shape
    return pl.pallas_call(
        lambda *refs: term_body(hs, rows, group, splits, *refs),
        in_specs=[VMEM] * 9,
        out_specs=[VMEM] * len(splits),
        out_shape=[jax.ShapeDtypeStruct((b - a, full), BF16) for _, a, b in splits],
        cost_estimate=cost(16 * tokens * hs * full, 20 * tokens * full),
        name="terms",
    )(got, acc, den, *ff, w_mine, w_their)


def thirds_body(t0, t1, t2, o0, o1, o2):
    o0[...] = t0[...]
    o1[...] = t1[...]
    o2[...] = t2[...]


def thirds_of(arrays):
    rows, width = arrays[0].shape
    third = rows // 3
    block = lambda at: pl.BlockSpec((third, width), lambda i: (at, 0))
    return pl.pallas_call(
        thirds_body,
        grid=(1,),
        in_specs=[block(0), block(1), block(2)],
        out_specs=[block(0)] * 3,
        out_shape=[jax.ShapeDtypeStruct((third, width), BF16)] * 3,
        cost_estimate=cost(0, 4 * rows * width),
        name="thirds",
    )(*arrays)


def far_body(t0, t1, t2, g0, g1, g2, o0, o1, o2):
    for t, g, o in ((t0, g0, o0), (t1, g1, o1), (t2, g2, o2)):
        o[...] = (t[...].astype(F32) + g[...].astype(F32)).astype(BF16)


def add_far(arrays, parts):
    third, width = parts[0].shape
    block = lambda at: pl.BlockSpec((third, width), lambda i: (at, 0))
    spread = [block(0), block(1), block(2)]
    return pl.pallas_call(
        far_body,
        grid=(1,),
        in_specs=spread + [block(0)] * 3,
        out_specs=spread,
        out_shape=[jax.ShapeDtypeStruct(arrays[0].shape, BF16)] * 3,
        input_output_aliases={0: 0, 1: 1, 2: 2},
        cost_estimate=cost(6 * third * width, 18 * third * width),
        name="add_far",
    )(*arrays, *parts)


def near_body(t0, t1, r0, r1, r2, o0, o1):
    o0[...] = (t0[...].astype(F32) + r0[...].astype(F32) + r1[...].astype(F32)).astype(BF16)
    o1[...] = (t1[...].astype(F32) + r2[...].astype(F32)).astype(BF16)


def add_near(*arrays):
    rows, width = arrays[0].shape
    block = pl.BlockSpec((rows // 3, width), lambda i: (i, 0))
    return pl.pallas_call(
        near_body,
        grid=(3,),
        in_specs=[block] * 5,
        out_specs=[block] * 2,
        out_shape=[jax.ShapeDtypeStruct((rows, width), BF16)] * 2,
        cost_estimate=cost(3 * rows * width, 14 * rows * width),
        name="add_near",
    )(*arrays)


def head_body(x, mine, m0, m1, m2, targets, gain, weight, layer_out, line):
    width = x.shape[1]
    mixed, spread = 0.0, 0.0
    for m in (mine, m0, m1, m2):
        mixed = mixed + m[:, :width].astype(F32)
        spread = spread + m[:, width : width + 1].astype(F32)
    lo = (x[...].astype(F32) + mixed).astype(BF16)
    layer_out[...] = lo
    back = lo.astype(F32)
    inv_norm = lax.rsqrt(jnp.sum(back * back, axis=-1, keepdims=True) / width + EPS)
    head_in = (back * inv_norm * gain[...]).astype(BF16)
    raised = jnp.exp(dot(head_in, weight[...]))
    prob = raised / jnp.sum(raised, axis=-1, keepdims=True)
    levels = lax.broadcasted_iota(jnp.int32, prob.shape, 1)
    grad = prob - jnp.where(levels == targets[...], 1.0, 0.0)
    scaled = gain[...] * dot_t(grad.astype(BF16), weight[...])
    lean = jnp.sum(back * scaled, axis=-1, keepdims=True) / width
    layer_grad = inv_norm * scaled - back * (inv_norm * inv_norm * inv_norm) * lean
    head_f = head_in.astype(F32)
    out_sq = jnp.sum(head_f * head_f, axis=-1, keepdims=True) * jnp.sum(
        grad * grad, axis=-1, keepdims=True
    )
    layer_sq = jnp.sum(layer_grad * layer_grad, axis=-1, keepdims=True)
    norm = jnp.sqrt(laid(out_sq + spread * layer_sq))
    line[...] = jnp.broadcast_to(norm[None], line.shape)


def head(x, mine, m0, m1, m2, targets, gain, weight, devices):
    return pl.pallas_call(
        head_body,
        in_specs=[VMEM] * 8,
        out_specs=[pl.BlockSpec(memory_space=pltpu.VMEM)] * 2,
        out_shape=[
            jax.ShapeDtypeStruct(x.shape, BF16),
            jax.ShapeDtypeStruct((devices, 1, 256), F32),
        ],
        name="head",
    )(x, mine, m0, m1, m2, targets, gain, weight)


def pick_body(table, where, spot, out):
    devices = table.shape[0]
    count = where.shape[1]
    hit = lax.broadcasted_iota(jnp.int32, (devices, count), 0) == where[...]
    hot = jnp.where(hit, 1.0, 0.0).astype(BF16)

    def take(part):
        return lax.dot_general(part, hot, (((0,), (0,)), ((), ())), preferred_element_type=F32)

    full = table[...]
    high = full.astype(BF16)
    rest = full - high.astype(F32)
    mid = rest.astype(BF16)
    low = (rest - mid.astype(F32)).astype(BF16)
    lines = take(high) + take(mid) + take(low)
    mine = lax.broadcasted_iota(jnp.int32, lines.shape, 0) == spot[...]
    picked = jnp.sum(jnp.where(mine, lines, 0.0), axis=0, keepdims=True)
    out[...] = count * picked / jnp.sum(picked, axis=-1, keepdims=True)


def pick(table, where, spot):
    return pl.pallas_call(
        pick_body,
        in_specs=[pl.BlockSpec(memory_space=pltpu.VMEM)] * 3,
        out_specs=pl.BlockSpec(memory_space=pltpu.VMEM),
        out_shape=jax.ShapeDtypeStruct(where.shape, F32),
        name="pick",
    )(table, where, spot)


def per_device(
    activations,
    targets,
    candidates,
    mix_gain,
    project_weight,
    output_weight,
    up_weight,
    down_weight,
    pattern_bias,
    head_gain,
    head_weight,
):
    rows, cols, width = activations.shape
    hs = project_weight.shape[2]
    tokens = rows * cols
    row_peers = lax.axis_size(ROW)
    inv_root = 1.0 / math.sqrt(hs)
    third = tokens // 3

    devices = lax.axis_size(ALL)

    their_project = swap_core(project_weight)
    their_up = swap_core(up_weight)
    their_down = swap_core(down_weight)
    their_output = swap_core(output_weight)
    bias = jnp.concatenate([pattern_bias, swap_core(pattern_bias)])

    x = activations.reshape(tokens, width)
    own = normalize(x, mix_gain[None, :])

    def after(first, values):
        return lax.optimization_barrier((first, values))[1]

    def ffn(shards, slots):
        return feed_forward(shards, slots, up_weight, their_up, down_weight, their_down)

    near = (up_z(own), down_z(own), swap_x(own))
    (ff_own,) = ffn((own,), 1)
    s_a, s_b, s_p = after((ff_own, their_project), near)
    s_aa, s_pb, s_pa = up_z(s_a), down_z(s_p), swap_x(s_a)

    def columns(shards):
        qkv = project(shards, project_weight, their_project, rows)
        got = lax.all_to_all(
            qkv.reshape(row_peers, rows * HALF, 6 * hs), ROW, split_axis=0, concat_axis=0, tiled=True
        )
        return qkv, got

    def attend_columns(group, got, *earlier):
        x = got.reshape(row_peers * rows, HALF, 6 * hs)
        return column_attention(group, bias, x, rows, hs, inv_root, earlier)

    def edge_of(qkv):
        return next_row(qkv[:, :, -1, :, 2 * hs :])

    qkv0, got0 = columns((own, s_a, s_b, s_p))
    their_qkv0 = swap_core(qkv0)
    edge0 = edge_of(qkv0)
    their_edge0 = swap_core(edge0)
    s_aa, s_pa, s_pb = after(qkv0, (s_aa, s_pa, s_pb))
    h_aa, h_pa, h_pb = thirds_of((s_aa, s_pa, s_pb))
    far = (swap_x(h_aa), up_z(h_pa), down_z(h_pb))
    back = attend_columns(0, after((s_aa, s_pa, s_pb), got0))
    away = after((back, their_qkv0), (s_aa, s_pa, s_pb, *far))
    qkv1, got1 = columns(away)
    their_qkv1 = swap_core(qkv1)
    edge1 = edge_of(qkv1)
    their_edge1 = swap_core(edge1)
    ff1 = ffn(after(qkv1, away), 4)
    back = attend_columns(1, after((ff1, their_qkv1), got1), back)
    again = lax.all_to_all(back, ROW, split_axis=0, concat_axis=0, tiled=True)

    xl, z, core = lax.axis_index(XL), lax.axis_index(Z), lax.axis_index(CORE)
    n_z = lax.axis_size(Z)
    shift_x = jnp.array([0, 0, 0, 1, 0, 1, 1, 1], jnp.int32)
    shift_z = jnp.array([0, 3, 1, 0, 2, 3, 1, 2], jnp.int32)
    chip = ((xl + shift_x) % 2) * n_z + (z + shift_z) % n_z
    starts = chip * 2 * cols
    offs = jnp.arange(cols, dtype=jnp.int32)
    mine = (starts[:, None] + core * cols + offs[None, :]).reshape(-1)
    theirs = (starts[:, None] + (1 - core) * cols + offs[None, :]).reshape(-1)
    top = (lax.axis_index(ROW) == 0).astype(jnp.int32)[None]
    acc, den = row_attention(
        after(back, top),
        mine[:, None],
        jnp.concatenate([mine, theirs])[None, :],
        (qkv0, qkv1),
        (their_qkv0, their_qkv1),
        (edge0, edge1),
        (their_edge0, their_edge1),
        hs,
        inv_root,
    )
    thirds = [(3, third * i, third * (i + 1)) for i in range(3)]
    t_aa, t_pa, t_pb, f0, f1, f2 = terms(
        1, again, acc[1], den[1], ff1, output_weight, their_output, hs, rows,
        [(i, 0, tokens) for i in range(3)] + thirds,
    )

    t_aa, t_pa, t_pb = add_far((t_aa, t_pa, t_pb), (swap_x(f0), down_z(f1), up_z(f2)))
    r_aa, r_pa, r_pb = down_z(t_aa), swap_x(t_pa), up_z(t_pb)
    ff0 = ffn(after(t_pb, (s_a, s_b, s_p)), 3)
    t_own, t_a, t_b, t_p = terms(
        0, again, acc[0], den[0], (ff_own, *ff0), output_weight, their_output, hs, rows,
        [(i, 0, tokens) for i in range(4)],
    )
    from_b = up_z(t_b)
    t_a, t_p = add_near(t_a, t_p, r_aa, r_pa, r_pb)
    from_a, from_p = down_z(t_a), swap_x(t_p)

    layer_out, line = head(
        x,
        t_own,
        from_a,
        from_b,
        from_p,
        targets.reshape(tokens, 1),
        head_gain[None, :],
        head_weight,
        devices,
    )
    table = lax.all_to_all(
        line,
        ALL,
        split_axis=0,
        concat_axis=0,
        tiled=True,
    ).reshape(devices, 256)
    full_cols = cols * lax.axis_size(COL)
    c_row, c_col = candidates // full_cols, candidates % full_cols
    where = (c_row // rows) * lax.axis_size(COL) + c_col // cols
    spot = (c_row % rows) * cols + c_col % cols
    chosen = pick(table, where[None, :], spot[None, :])
    return (layer_out.reshape(rows, cols, width), chosen.reshape(-1))


def solution(mesh):
    split = Mesh(mesh.devices.reshape(2, 4, 2, 4, 2), ("row_0", "row_1", "col_0", "col_1", "col_2"))

    return jax.shard_map(
        per_device,
        mesh=split,
        in_specs=(
            P(ROW, COL, None),
            P(ROW, COL),
            P(),
            P(),
            P(None, None, COL),
            P(COL, None),
            P(None, COL),
            P(COL, None),
            P(COL),
            P(),
            P(),
        ),
        out_specs=(P(ROW, COL, None), P()),
        check_vma=False,
    )
```

profile of v0, /device:TPU:1, one launch (start us, length us, event | category | flops | bytes accessed | tf_op | source)
XLA Modules:
  0.0 255.0 jit_solution(5881174955588139900)
XLA Ops:
  0.6 1.5 collective-permute-start.1
  2.6 2.3 normalize.1.refs_0_
  4.9 1.7 collective-permute-start.4
  6.7 2.1 collective-permute-start.5
  8.8 1.2 collective-permute-start.6
  10.1 6.6 %feed_forward.3.refs_3_ = bf16[192,2176]{1,0:T(8,128)(2,1)} custom-call(bf16[192,2048]{1,0:T(8,128)(2,1)} %normalize.1.refs_0_, bf16[2048,512]{1,0:T(8,128)(2,1)} %refs_3_.3, bf16[2048,512]{1,0:T(8,128)(2,1)} %copy-done.4, bf16[512,2048]{1,0:T(8,128)(2,1)} %refs_5_.1, bf16[512,2048]{1,0:T(8,128)(2,1)} %collective-permute-done.2.refs_4_.refs_9_.refs_6_), custom_call_target="tpu_custom_call" | custom-call | flops 1610612736 | bytes 9961472 | tf_op jit(solution)/shard_map/feed_forward/pallas_call | solution.py:153
  16.7 10.1 %collective-permute-done.4.refs_1_.refs_0_ = bf16[192,2048]{1,0:T(8,128)(2,1)S(1)} collective-permute-done((bf16[192,2048]{1,0:T(8,128)(2,1)}, bf16[192,2048]{1,0:T(8,128)(2,1)S(1)}, u32[]{:S(2)}, u32[]{:S(2)}) %collective-permute-start.4) | collective-permute-done | bytes 786464 | tf_op jit(solution)/shard_map/ppermute | solution.py:23
  27.8 6.3 %project.2.refs_3_.refs_5_ = bf16[4,2,6,16,768]{4,3,2,1,0:T(8,128)(2,1)} custom-call(bf16[192,2048]{1,0:T(8,128)(2,1)} %normalize.1.refs_0_, bf16[192,2048]{1,0:T(8,128)(2,1)} %copy-done.25, bf16[192,2048]{1,0:T(8,128)(2,1)} %collective-permute-done.5.refs_2_.refs_1_, bf16[192,2048]{1,0:T(8,128)(2,1)} %collective-permute-done.6.refs_3_.refs_2_, ...), custom_call_target="tpu_custom_call" | custom-call | flops 2415919104 | bytes 6291456 | tf_op jit(solution)/shard_map/project/pallas_call | solution.py:106
  34.2 1.2 collective-permute-start.10
  35.4 6.7 %all-to-all-start = ((bf16[8,96,768]{2,1,0:T(8,128)(2,1)}), bf16[8,96,768]{2,1,0:T(8,128)(2,1)S(1)}, u32[]{:S(2)}, u32[]{:S(2)}) async-start(bf16[8,96,768]{2,1,0:T(8,128)(2,1)} %bitcast.24), calls=%async_computation | async-start | bytes 2359296 | tf_op jit(solution)/shard_map/all_to_all | solution.py:513
  42.5 2.6 %collective-permute-start.9 = (bf16[192,2048]{1,0:T(8,128)(2,1)}, bf16[192,2048]{1,0:T(8,128)(2,1)}, u32[]{:S(2)}, u32[]{:S(2)}) collective-permute-start(bf16[192,2048]{1,0:T(8,128)(2,1)} %collective-permute-done.6.refs_3_.refs_2_), channel_id=1, source_target_pairs={{0,6},{2,0},{4,2},{6,4},{1,7},{3,1},{5,3},{7,5},{8,14},{10,8},{12,... | collective-permute-start | bytes 2359304 | tf_op jit(solution)/shard_map/ppermute | solution.py:23
  45.1 17.4 %collective-permute-done.7.t0.refs_0_ = bf16[192,2048]{1,0:T(8,128)(2,1)} collective-permute-done((bf16[192,2048]{1,0:T(8,128)(2,1)}, bf16[192,2048]{1,0:T(8,128)(2,1)}, u32[]{:S(2)}, u32[]{:S(2)}) %collective-permute-start.7) | collective-permute-done | bytes 786464 | tf_op jit(solution)/shard_map/ppermute | solution.py:23
  62.5 10.5 %collective-permute-done.8.t1.refs_1_ = bf16[192,2048]{1,0:T(8,128)(2,1)} collective-permute-done((bf16[192,2048]{1,0:T(8,128)(2,1)}, bf16[192,2048]{1,0:T(8,128)(2,1)}, u32[]{:S(2)}, u32[]{:S(2)}) %collective-permute-start.8) | collective-permute-done | bytes 786464 | tf_op jit(solution)/shard_map/ppermute | solution.py:23
  73.0 2.0 thirds.1
  75.0 1.2 collective-permute-start.11
  76.1 2.7 %collective-permute-start.13 = (bf16[64,2048]{1,0:T(8,128)(2,1)}, bf16[64,2048]{1,0:T(8,128)(2,1)}, u32[]{:S(2)}, u32[]{:S(2)}) collective-permute-start(bf16[64,2048]{1,0:T(8,128)(2,1)} %get-tuple-element.66), channel_id=1, source_target_pairs={{0,6},{2,0},{4,2},{6,4},{1,7},{3,1},{5,3},{7,5},{8,14},{10,8},{12,... | collective-permute-start | bytes 786440 | tf_op jit(solution)/shard_map/ppermute | solution.py:23
  78.8 1.7 collective-permute-start
  81.8 1.3 pad_maximum_fusion.refs_0_
  84.1 3.8 %column_attention.2.refs_2_ = bf16[8,2,7,16,256]{4,3,2,1,0:T(8,128)(2,1)} custom-call(f32[2]{0:T(128)} %pad_maximum_fusion.refs_0_, bf16[48,16,768]{2,1,0:T(8,128)(2,1)} %bitcast.29), custom_call_target="tpu_custom_call" | custom-call | flops 452984832 | bytes 1572864 | tf_op jit(solution)/shard_map/column_attention/pallas_call | solution.py:279
  88.0 6.7 %project.3.refs_4_.refs_6_ = bf16[4,2,6,16,768]{4,3,2,1,0:T(8,128)(2,1)} custom-call(bf16[192,2048]{1,0:T(8,128)(2,1)} %collective-permute-done.7.t0.refs_0_, bf16[192,2048]{1,0:T(8,128)(2,1)} %collective-permute-done.8.t1.refs_1_, bf16[192,2048]{1,0:T(8,128)(2,1)} %collective-permute-done.9.t2.refs_2_, bf16[64,2048]{1,0:T(8,128)(2,1)} %collective-permute-done.11.refs_3_, ...), custom_call_target="tpu_custom_call" | custom-call | flops 2415919104 | bytes 6291456 | tf_op jit(solution)/shard_map/project/pallas_call | solution.py:106
  94.9 6.7 %all-to-all-start.1 = ((bf16[8,96,768]{2,1,0:T(8,128)(2,1)}), bf16[8,96,768]{2,1,0:T(8,128)(2,1)S(1)}, u32[]{:S(2)}, u32[]{:S(2)}) async-start(bf16[8,96,768]{2,1,0:T(8,128)(2,1)} %bitcast.25), calls=%async_computation.1 | async-start | bytes 2359296 | tf_op jit(solution)/shard_map/all_to_all | solution.py:513
  101.5 1.6 slice_bitcast_fusion.1
  103.1 3.5 %collective-permute-start.15 = (bf16[4,2,16,512]{3,2,1,0:T(8,128)(2,1)}, bf16[4,2,16,512]{3,2,1,0:T(8,128)(2,1)S(1)}, u32[]{:S(2)}, u32[]{:S(2)}) collective-permute-start(bf16[4,2,16,512]{3,2,1,0:T(8,128)(2,1)} %slice_bitcast_fusion.1), channel_id=1, source_target_pairs={{0,16},{16,32},{32,48},{48,64},{64,80},{80,96},{96,112},{1,17},{17... | collective-permute-start | bytes 393224 | tf_op jit(solution)/shard_map/ppermute | solution.py:44
  106.7 13.6 %feed_forward.4 = (bf16[192,2176]{1,0:T(8,128)(2,1)}, bf16[192,2176]{1,0:T(8,128)(2,1)}, bf16[192,2176]{1,0:T(8,128)(2,1)}, bf16[192,2176]{1,0:T(8,128)(2,1)}) custom-call(bf16[192,2048]{1,0:T(8,128)(2,1)} %collective-permute-done.7.t0.refs_0_, bf16[192,2048]{1,0:T(8,128)(2,1)} %collective-permute-done.8.t1.refs_1_, ...), custom_call_target="tpu_custom_call" | custom-call | flops 6442450944 | bytes 14680064 | tf_op jit(solution)/shard_map/feed_forward/pallas_call | solution.py:153
  121.2 3.8 %column_attention.3 = bf16[8,2,7,16,256]{4,3,2,1,0:T(8,128)(2,1)} custom-call(f32[2]{0:T(128)} %pad_maximum_fusion.refs_0_, bf16[48,16,768]{2,1,0:T(8,128)(2,1)} %bitcast.26, bf16[8,2,7,16,256]{4,3,2,1,0:T(8,128)(2,1)} %column_attention.2.refs_2_), custom_call_target="tpu_custom_call", output_to_operand_aliasing={{}: (2, {})} | custom-call | flops 452984832 | bytes 1572864 | tf_op jit(solution)/shard_map/column_attention/pallas_call | solution.py:279
  125.0 6.1 %all-to-all-start.2 = ((bf16[8,2,7,16,256]{4,3,2,1,0:T(8,128)(2,1)}), bf16[8,2,7,16,256]{4,3,2,1,0:T(8,128)(2,1)S(1)}, u32[]{:S(2)}, u32[]{:S(2)}) async-start(bf16[8,2,7,16,256]{4,3,2,1,0:T(8,128)(2,1)} %column_attention.3), calls=%async_computation.2 | async-start | bytes 1835008 | tf_op jit(solution)/shard_map/all_to_all | solution.py:540
  132.0 3.4 %collective-permute-start.16 = (bf16[4,2,16,512]{3,2,1,0:T(8,128)(2,1)S(1)}, bf16[4,2,16,512]{3,2,1,0:T(8,128)(2,1)S(1)}, u32[]{:S(2)}, u32[]{:S(2)}) collective-permute-start(bf16[4,2,16,512]{3,2,1,0:T(8,128)(2,1)S(1)} %slice_bitcast_fusion), channel_id=1, source_target_pairs={{0,16},{16,32},{32,48},{48,64},{64,80},{80,96},{96,112},{1,17},{17... | collective-permute-start | bytes 393224 | tf_op jit(solution)/shard_map/ppermute | solution.py:44
  135.5 2.0 collective-permute-start.17
  137.5 5.9 %collective-permute-done.16.refs_12_ = bf16[4,2,16,512]{3,2,1,0:T(8,128)(2,1)S(1)} collective-permute-done((bf16[4,2,16,512]{3,2,1,0:T(8,128)(2,1)S(1)}, bf16[4,2,16,512]{3,2,1,0:T(8,128)(2,1)S(1)}, u32[]{:S(2)}, u32[]{:S(2)}) %collective-permute-start.16) | collective-permute-done | bytes 131104 | tf_op jit(solution)/shard_map/ppermute | solution.py:44
  143.4 1.4 collective-permute-start.18
  147.2 10.3 %row_attention.1 = (f32[4,2,6,16,256]{4,3,2,1,0:T(8,128)}, f32[4,2,6,16,256]{4,3,2,1,0:T(8,128)}, f32[4,2,6,16,256]{4,3,2,1,0:T(8,128)}, f32[4,2,6,16,256]{4,3,2,1,0:T(8,128)}) custom-call(s32[1]{0:T(128)} %bitcast.6.refs_0_, s32[256,1]{1,0:T(8,128)} %add.135.refs_1_, s32[1,512]{1,0:T(1,128)} %bitcast.35, ...), custom_call_target="tpu_custom_call" | custom-call | flops 1610612736 | bytes 6291456 | tf_op jit(solution)/shard_map/row_attention/pallas_call | solution.py:223
  158.6 5.8 %terms.2 = (bf16[192,2176]{1,0:T(8,128)(2,1)}, bf16[192,2176]{1,0:T(8,128)(2,1)}, bf16[192,2176]{1,0:T(8,128)(2,1)}, bf16[64,2176]{1,0:T(8,128)(2,1)}, bf16[64,2...) custom-call(bf16[8,2,7,16,256]{4,3,2,1,0:T(8,128)(2,1)} %copy-done, f32[4,2,6,16,256]{4,3,2,1,0:T(8,128)} %get-tuple-element.87.refs_1_, ...), custom_call_target="tpu_custom_call" | custom-call | flops 855638016 | bytes 8355840 | tf_op jit(solution)/shard_map/terms/pallas_call | solution.py:328
  166.3 6.6 %collective-permute-done.20.g0 = bf16[64,2176]{1,0:T(8,128)(2,1)S(1)} collective-permute-done((bf16[64,2176]{1,0:T(8,128)(2,1)}, bf16[64,2176]{1,0:T(8,128)(2,1)S(1)}, u32[]{:S(2)}, u32[]{:S(2)}) %collective-permute-start.20) | collective-permute-done | bytes 278560 | tf_op jit(solution)/shard_map/ppermute | solution.py:23
  172.9 1.5 collective-permute-done.22.g2
  175.2 2.4 add_far.1
  178.0 1.1 collective-permute-start.24
  180.1 11.1 %feed_forward.5 = (bf16[192,2176]{1,0:T(8,128)(2,1)}, bf16[192,2176]{1,0:T(8,128)(2,1)}, bf16[192,2176]{1,0:T(8,128)(2,1)}) custom-call(bf16[192,2048]{1,0:T(8,128)(2,1)} %copy-done.25, bf16[192,2048]{1,0:T(8,128)(2,1)} %collective-permute-done.5.refs_2_.refs_1_, bf16[192,2048]{1,0:T(8,128)(2,1)} %collective-permute-done.6.refs_3_.refs_2_, ...), custom_call_target="tpu_custom_call" | custom-call | flops 4831838208 | bytes 13107200 | tf_op jit(solution)/shard_map/feed_forward/pallas_call | solution.py:153
  191.2 5.9 %terms.3 = (bf16[192,2176]{1,0:T(8,128)(2,1)}, bf16[192,2176]{1,0:T(8,128)(2,1)}, bf16[192,2176]{1,0:T(8,128)(2,1)}, bf16[192,2176]{1,0:T(8,128)(2,1)}) custom-call(bf16[8,2,7,16,256]{4,3,2,1,0:T(8,128)(2,1)} %copy-done, f32[4,2,6,16,256]{4,3,2,1,0:T(8,128)} %get-tuple-element.85.refs_1_, f32[4,2,6,16,256]{4,3,2,1,0:T(8,128)} %get-tuple-element.86.refs_2_, ...), custom_call_target="tpu_custom_call" | custom-call | flops 855638016 | bytes 8355840 | tf_op jit(solution)/shard_map/terms/pallas_call | solution.py:328
  197.1 1.8 collective-permute-done.25.r2
  199.8 4.1 %add_near.1 = (bf16[192,2176]{1,0:T(8,128)(2,1)}, bf16[192,2176]{1,0:T(8,128)(2,1)}) custom-call(bf16[192,2176]{1,0:T(8,128)(2,1)} %get-tuple-element.103.t0, bf16[192,2176]{1,0:T(8,128)(2,1)} %get-tuple-element.104.t1, bf16[192,2176]{1,0:T(8,128)(2,1)} %copy-done.11, bf16[192,2176]{1,0:T(8,128)(2,1)} %copy-done.12, bf16[192,2176]{1,0:T(8,128)(2,1)} %copy-done.13), custom_call_target="tpu_custom_call" | custom-call | flops 1253376 | bytes 5849088 | tf_op jit(solution)/shard_map/add_near/pallas_call | solution.py:388
  203.9 1.4 collective-permute-start.26
  206.5 10.0 %collective-permute-done.27.m1 = bf16[192,2176]{1,0:T(8,128)(2,1)S(1)} collective-permute-done((bf16[192,2176]{1,0:T(8,128)(2,1)}, bf16[192,2176]{1,0:T(8,128)(2,1)S(1)}, u32[]{:S(2)}, u32[]{:S(2)}) %collective-permute-start.27) | collective-permute-done | bytes 835616 | tf_op jit(solution)/shard_map/ppermute | solution.py:23
  216.4 5.3 %collective-permute-done.26.m0 = bf16[192,2176]{1,0:T(8,128)(2,1)S(1)} collective-permute-done((bf16[192,2176]{1,0:T(8,128)(2,1)}, bf16[192,2176]{1,0:T(8,128)(2,1)S(1)}, u32[]{:S(2)}, u32[]{:S(2)}) %collective-permute-start.26) | collective-permute-done | bytes 835616 | tf_op jit(solution)/shard_map/ppermute | solution.py:23
  221.8 1.2 collective-permute-done.28.m2
  223.8 5.7 %head.1 = (bf16[192,2048]{1,0:T(8,128)(2,1)}, f32[128,1,256]{2,1,0:T(1,128)}) custom-call(bf16[192,2048]{1,0:T(8,128)(2,1)} %bitcast.28, bf16[192,2176]{1,0:T(8,128)(2,1)} %get-tuple-element.102.mine, bf16[192,2176]{1,0:T(8,128)(2,1)} %copy-done.9, bf16[192,2176]{1,0:T(8,128)(2,1)} %copy-done.8, bf16[192,2176]{1,0:T(8,128)(2,1)} %copy-done.10, ...), custom_call_target="tpu_custom_call" | custom-call | tf_op jit(solution)/shard_map/head/pallas_call | solution.py:427
  229.5 12.5 %all-to-all-start.3 = ((f32[128,1,256]{2,1,0:T(1,128)}), f32[128,1,256]{2,1,0:T(1,128)S(1)}, u32[]{:S(2)}, u32[]{:S(2)}) async-start(f32[128,1,256]{2,1,0:T(1,128)} %get-tuple-element.111), calls=%async_computation.3 | async-start | bytes 262144 | tf_op jit(solution)/shard_map/all_to_all | solution.py:591
  242.6 9.6 %all-to-all-done.3 = f32[128,1,256]{2,1,0:T(1,128)S(1)} async-done(((f32[128,1,256]{2,1,0:T(1,128)}), f32[128,1,256]{2,1,0:T(1,128)S(1)}, u32[]{:S(2)}, u32[]{:S(2)}) %all-to-all-start.3) | async-done | bytes 131104 | tf_op jit(solution)/shard_map/all_to_all | solution.py:591
  252.9 2.2 pick.1
  (100 shorter events, 17.7 us)
Async XLA Ops:
  0.6 8.2 %collective-permute-start.1 = (bf16[2048,512]{1,0:T(8,128)(2,1)}, bf16[2048,512]{1,0:T(8,128)(2,1)S(1)}, u32[]{:S(2)}, u32[]{:S(2)}) collective-permute-start(bf16[2048,512]{1,0:T(8,128)(2,1)} %refs_3_.3), channel_id=1, source_target_pairs={{0,1},{1,0},{2,3},{3,2},{4,5},{5,4},{6,7},{7,6},{8,9},{9,8},{10,11... | collective-permute-start | bytes 6291464 | tf_op jit(solution)/shard_map/ppermute | solution.py:23
  2.1 7.9 %collective-permute-start.2 = (bf16[512,2048]{1,0:T(8,128)(2,1)}, bf16[512,2048]{1,0:T(8,128)(2,1)}, u32[]{:S(2)}, u32[]{:S(2)}) collective-permute-start(bf16[512,2048]{1,0:T(8,128)(2,1)} %refs_5_.1), channel_id=1, source_target_pairs={{0,1},{1,0},{2,3},{3,2},{4,5},{5,4},{6,7},{7,6},{8,9},{9,8},{10,11... | collective-permute-start | bytes 6291464 | tf_op jit(solution)/shard_map/ppermute | solution.py:23
  2.2 25.7 %collective-permute-start.3 = (bf16[3,2048,128]{2,1,0:T(8,128)(2,1)}, bf16[3,2048,128]{2,1,0:T(8,128)(2,1)}, u32[]{:S(2)}, u32[]{:S(2)}) collective-permute-start(bf16[3,2048,128]{2,1,0:T(8,128)(2,1)} %refs_6_.2), channel_id=1, source_target_pairs={{0,1},{1,0},{2,3},{3,2},{4,5},{5,4},{6,7},{7,6},{8,9},{9,8},{10,11... | collective-permute-start | bytes 4718600 | tf_op jit(solution)/shard_map/ppermute | solution.py:23
  4.9 21.9 %collective-permute-start.4 = (bf16[192,2048]{1,0:T(8,128)(2,1)}, bf16[192,2048]{1,0:T(8,128)(2,1)S(1)}, u32[]{:S(2)}, u32[]{:S(2)}) collective-permute-start(bf16[192,2048]{1,0:T(8,128)(2,1)} %normalize.1.refs_0_), channel_id=1, source_target_pairs={{0,2},{2,4},{4,6},{6,0},{1,3},{3,5},{5,7},{7,1},{8,10},{10,12},{12... | collective-permute-start | bytes 2359304 | tf_op jit(solution)/shard_map/ppermute | solution.py:23
  6.7 20.2 %collective-permute-start.5 = (bf16[192,2048]{1,0:T(8,128)(2,1)}, bf16[192,2048]{1,0:T(8,128)(2,1)}, u32[]{:S(2)}, u32[]{:S(2)}) collective-permute-start(bf16[192,2048]{1,0:T(8,128)(2,1)} %normalize.1.refs_0_), channel_id=1, source_target_pairs={{0,6},{2,0},{4,2},{6,4},{1,7},{3,1},{5,3},{7,5},{8,14},{10,8},{12,... | collective-permute-start | bytes 2359304 | tf_op jit(solution)/shard_map/ppermute | solution.py:23
  8.8 1.3 copy-start.4
  8.8 19.0 %collective-permute-start.6 = (bf16[192,2048]{1,0:T(8,128)(2,1)}, bf16[192,2048]{1,0:T(8,128)(2,1)}, u32[]{:S(2)}, u32[]{:S(2)}) collective-permute-start(bf16[192,2048]{1,0:T(8,128)(2,1)} %normalize.1.refs_0_), channel_id=1, source_target_pairs={{0,8},{8,0},{1,9},{9,1},{2,10},{10,2},{3,11},{11,3},{4,12},{12,4},... | collective-permute-start | bytes 2359304 | tf_op jit(solution)/shard_map/ppermute | solution.py:23
  34.2 53.8 %collective-permute-start.10 = (bf16[4,2,6,16,768]{4,3,2,1,0:T(8,128)(2,1)}, bf16[4,2,6,16,768]{4,3,2,1,0:T(8,128)(2,1)S(1)}, u32[]{:S(2)}, u32[]{:S(2)}) collective-permute-start(bf16[4,2,6,16,768]{4,3,2,1,0:T(8,128)(2,1)} %project.2.refs_3_.refs_5_), channel_id=1, source_target_pairs={{0,1},{1,0},{2,3},{3,2},{4,5},{5,4},{6,7},{7,6},{8,9},{9,8},{10,11... | collective-permute-start | bytes 3538952 | tf_op jit(solution)/shard_map/ppermute | solution.py:23
  35.4 47.7 %all-to-all-start = ((bf16[8,96,768]{2,1,0:T(8,128)(2,1)}), bf16[8,96,768]{2,1,0:T(8,128)(2,1)S(1)}, u32[]{:S(2)}, u32[]{:S(2)}) async-start(bf16[8,96,768]{2,1,0:T(8,128)(2,1)} %bitcast.24), calls=%async_computation | async-start | bytes 2359296 | tf_op jit(solution)/shard_map/all_to_all | solution.py:513
  42.1 39.4 %copy-start.5 = (bf16[128,2048]{1,0:T(8,128)(2,1)S(1)}, bf16[128,2048]{1,0:T(8,128)(2,1)}, u32[]{:S(2)}) copy-start(bf16[128,2048]{1,0:T(8,128)(2,1)} %refs_7_.3) | copy-start | bytes 1572868
  42.1 20.4 %collective-permute-start.7 = (bf16[192,2048]{1,0:T(8,128)(2,1)}, bf16[192,2048]{1,0:T(8,128)(2,1)}, u32[]{:S(2)}, u32[]{:S(2)}) collective-permute-start(bf16[192,2048]{1,0:T(8,128)(2,1)} %copy-done.25), channel_id=1, source_target_pairs={{0,2},{2,4},{4,6},{6,0},{1,3},{3,5},{5,7},{7,1},{8,10},{10,12},{12... | collective-permute-start | bytes 2359304 | tf_op jit(solution)/shard_map/ppermute | solution.py:23
  42.1 30.8 %collective-permute-start.8 = (bf16[192,2048]{1,0:T(8,128)(2,1)}, bf16[192,2048]{1,0:T(8,128)(2,1)}, u32[]{:S(2)}, u32[]{:S(2)}) collective-permute-start(bf16[192,2048]{1,0:T(8,128)(2,1)} %copy-done.25), channel_id=1, source_target_pairs={{0,8},{8,0},{1,9},{9,1},{2,10},{10,2},{3,11},{11,3},{4,12},{12,4},... | collective-permute-start | bytes 2359304 | tf_op jit(solution)/shard_map/ppermute | solution.py:23
  42.5 30.4 %collective-permute-start.9 = (bf16[192,2048]{1,0:T(8,128)(2,1)}, bf16[192,2048]{1,0:T(8,128)(2,1)}, u32[]{:S(2)}, u32[]{:S(2)}) collective-permute-start(bf16[192,2048]{1,0:T(8,128)(2,1)} %collective-permute-done.6.refs_3_.refs_2_), channel_id=1, source_target_pairs={{0,6},{2,0},{4,2},{6,4},{1,7},{3,1},{5,3},{7,5},{8,14},{10,8},{12,... | collective-permute-start | bytes 2359304 | tf_op jit(solution)/shard_map/ppermute | solution.py:23
  75.0 13.0 %collective-permute-start.11 = (bf16[64,2048]{1,0:T(8,128)(2,1)}, bf16[64,2048]{1,0:T(8,128)(2,1)}, u32[]{:S(2)}, u32[]{:S(2)}) collective-permute-start(bf16[64,2048]{1,0:T(8,128)(2,1)} %get-tuple-element.64), channel_id=1, source_target_pairs={{0,8},{8,0},{1,9},{9,1},{2,10},{10,2},{3,11},{11,3},{4,12},{12,4},... | collective-permute-start | bytes 786440 | tf_op jit(solution)/shard_map/ppermute | solution.py:23
  76.1 11.8 %collective-permute-start.12 = (bf16[64,2048]{1,0:T(8,128)(2,1)}, bf16[64,2048]{1,0:T(8,128)(2,1)}, u32[]{:S(2)}, u32[]{:S(2)}) collective-permute-start(bf16[64,2048]{1,0:T(8,128)(2,1)} %get-tuple-element.65), channel_id=1, source_target_pairs={{0,2},{2,4},{4,6},{6,0},{1,3},{3,5},{5,7},{7,1},{8,10},{10,12},{12... | collective-permute-start | bytes 786440 | tf_op jit(solution)/shard_map/ppermute | solution.py:23
  76.1 11.8 %collective-permute-start.13 = (bf16[64,2048]{1,0:T(8,128)(2,1)}, bf16[64,2048]{1,0:T(8,128)(2,1)}, u32[]{:S(2)}, u32[]{:S(2)}) collective-permute-start(bf16[64,2048]{1,0:T(8,128)(2,1)} %get-tuple-element.66), channel_id=1, source_target_pairs={{0,6},{2,0},{4,2},{6,4},{1,7},{3,1},{5,3},{7,5},{8,14},{10,8},{12,... | collective-permute-start | bytes 786440 | tf_op jit(solution)/shard_map/ppermute | solution.py:23
  78.8 2.7 %collective-permute-start = (f32[1]{0:T(128)}, f32[1]{0:T(128)}, u32[]{:S(2)}, u32[]{:S(2)}) collective-permute-start(f32[1]{0:T(128)} %param.21), channel_id=1, source_target_pairs={{0,1},{1,0},{2,3},{3,2},{4,5},{5,4},{6,7},{7,6},{8,9},{9,8},{10,11... | collective-permute-start | bytes 20 | tf_op jit(solution)/shard_map/ppermute | solution.py:23
  81.5 76.0 %collective-permute-start.19 = (bf16[128,2048]{1,0:T(8,128)(2,1)S(1)}, bf16[128,2048]{1,0:T(8,128)(2,1)S(1)}, u32[]{:S(2)}, u32[]{:S(2)}) collective-permute-start(bf16[128,2048]{1,0:T(8,128)(2,1)S(1)} %copy-done.5), channel_id=1, source_target_pairs={{0,1},{1,0},{2,3},{3,2},{4,5},{5,4},{6,7},{7,6},{8,9},{9,8},{10,11... | collective-permute-start | bytes 1572872 | tf_op jit(solution)/shard_map/ppermute | solution.py:23
  87.9 6.9 %copy-start.23 = (s32[8]{0:T(128)S(1)}, s32[8]{0:T(128)}, u32[]{:S(2)}) copy-start(s32[8]{0:T(128)} %constant.117.clone) | copy-start | bytes 100
  87.9 6.9 %copy-start.24 = (s32[8]{0:T(128)S(1)}, s32[8]{0:T(128)}, u32[]{:S(2)}) copy-start(s32[8]{0:T(128)} %constant.118.clone) | copy-start | bytes 100
  88.0 6.7 %copy-start.2 = (bf16[4,2,6,16,768]{4,3,2,1,0:T(8,128)(2,1)}, bf16[4,2,6,16,768]{4,3,2,1,0:T(8,128)(2,1)S(1)}, u32[]{:S(2)}) copy-start(bf16[4,2,6,16,768]{4,3,2,1,0:T(8,128)(2,1)S(1)} %collective-permute-done.10.refs_7_.refs_9_) | copy-start | bytes 3538948
  94.7 25.6 %collective-permute-start.14 = (bf16[4,2,6,16,768]{4,3,2,1,0:T(8,128)(2,1)}, bf16[4,2,6,16,768]{4,3,2,1,0:T(8,128)(2,1)S(1)}, u32[]{:S(2)}, u32[]{:S(2)}) collective-permute-start(bf16[4,2,6,16,768]{4,3,2,1,0:T(8,128)(2,1)} %project.3.refs_4_.refs_6_), channel_id=1, source_target_pairs={{0,1},{1,0},{2,3},{3,2},{4,5},{5,4},{6,7},{7,6},{8,9},{9,8},{10,11... | collective-permute-start | bytes 3538952 | tf_op jit(solution)/shard_map/ppermute | solution.py:23
  94.9 25.3 %all-to-all-start.1 = ((bf16[8,96,768]{2,1,0:T(8,128)(2,1)}), bf16[8,96,768]{2,1,0:T(8,128)(2,1)S(1)}, u32[]{:S(2)}, u32[]{:S(2)}) async-start(bf16[8,96,768]{2,1,0:T(8,128)(2,1)} %bitcast.25), calls=%async_computation.1 | async-start | bytes 2359296 | tf_op jit(solution)/shard_map/all_to_all | solution.py:513
  103.1 32.4 %collective-permute-start.15 = (bf16[4,2,16,512]{3,2,1,0:T(8,128)(2,1)}, bf16[4,2,16,512]{3,2,1,0:T(8,128)(2,1)S(1)}, u32[]{:S(2)}, u32[]{:S(2)}) collective-permute-start(bf16[4,2,16,512]{3,2,1,0:T(8,128)(2,1)} %slice_bitcast_fusion.1), channel_id=1, source_target_pairs={{0,16},{16,32},{32,48},{48,64},{64,80},{80,96},{96,112},{1,17},{17... | collective-permute-start | bytes 393224 | tf_op jit(solution)/shard_map/ppermute | solution.py:44
  120.2 4.8 %copy-start.3 = (bf16[4,2,6,16,768]{4,3,2,1,0:T(8,128)(2,1)}, bf16[4,2,6,16,768]{4,3,2,1,0:T(8,128)(2,1)S(1)}, u32[]{:S(2)}) copy-start(bf16[4,2,6,16,768]{4,3,2,1,0:T(8,128)(2,1)S(1)} %collective-permute-done.14.refs_8_.refs_10_) | copy-start | bytes 3538948
  125.0 32.5 %all-to-all-start.2 = ((bf16[8,2,7,16,256]{4,3,2,1,0:T(8,128)(2,1)}), bf16[8,2,7,16,256]{4,3,2,1,0:T(8,128)(2,1)S(1)}, u32[]{:S(2)}, u32[]{:S(2)}) async-start(bf16[8,2,7,16,256]{4,3,2,1,0:T(8,128)(2,1)} %column_attention.3), calls=%async_computation.2 | async-start | bytes 1835008 | tf_op jit(solution)/shard_map/all_to_all | solution.py:540
  132.0 11.4 %collective-permute-start.16 = (bf16[4,2,16,512]{3,2,1,0:T(8,128)(2,1)S(1)}, bf16[4,2,16,512]{3,2,1,0:T(8,128)(2,1)S(1)}, u32[]{:S(2)}, u32[]{:S(2)}) collective-permute-start(bf16[4,2,16,512]{3,2,1,0:T(8,128)(2,1)S(1)} %slice_bitcast_fusion), channel_id=1, source_target_pairs={{0,16},{16,32},{32,48},{48,64},{64,80},{80,96},{96,112},{1,17},{17... | collective-permute-start | bytes 393224 | tf_op jit(solution)/shard_map/ppermute | solution.py:44
  135.5 11.0 %copy-start.17 = (bf16[4,2,16,512]{3,2,1,0:T(8,128)(2,1)}, bf16[4,2,16,512]{3,2,1,0:T(8,128)(2,1)S(1)}, u32[]{:S(2)}) copy-start(bf16[4,2,16,512]{3,2,1,0:T(8,128)(2,1)S(1)} %collective-permute-done.15.refs_11_) | copy-start | bytes 393220
  135.5 11.0 %collective-permute-start.17 = (bf16[4,2,16,512]{3,2,1,0:T(8,128)(2,1)S(1)}, bf16[4,2,16,512]{3,2,1,0:T(8,128)(2,1)S(1)}, u32[]{:S(2)}, u32[]{:S(2)}) collective-permute-start(bf16[4,2,16,512]{3,2,1,0:T(8,128)(2,1)S(1)} %collective-permute-done.15.refs_11_), channel_id=1, source_target_pairs={{0,1},{1,0},{2,3},{3,2},{4,5},{5,4},{6,7},{7,6},{8,9},{9,8},{10,11... | collective-permute-start | bytes 393224 | tf_op jit(solution)/shard_map/ppermute | solution.py:23
  143.4 3.1 %copy-start.18 = (bf16[4,2,16,512]{3,2,1,0:T(8,128)(2,1)}, bf16[4,2,16,512]{3,2,1,0:T(8,128)(2,1)S(1)}, u32[]{:S(2)}) copy-start(bf16[4,2,16,512]{3,2,1,0:T(8,128)(2,1)S(1)} %collective-permute-done.16.refs_12_) | copy-start | bytes 393220
  143.4 3.1 %collective-permute-start.18 = (bf16[4,2,16,512]{3,2,1,0:T(8,128)(2,1)S(1)}, bf16[4,2,16,512]{3,2,1,0:T(8,128)(2,1)S(1)}, u32[]{:S(2)}, u32[]{:S(2)}) collective-permute-start(bf16[4,2,16,512]{3,2,1,0:T(8,128)(2,1)S(1)} %collective-permute-done.16.refs_12_), channel_id=1, source_target_pairs={{0,1},{1,0},{2,3},{3,2},{4,5},{5,4},{6,7},{7,6},{8,9},{9,8},{10,11... | collective-permute-start | bytes 393224 | tf_op jit(solution)/shard_map/ppermute | solution.py:23
  164.4 8.4 %collective-permute-start.20 = (bf16[64,2176]{1,0:T(8,128)(2,1)}, bf16[64,2176]{1,0:T(8,128)(2,1)S(1)}, u32[]{:S(2)}, u32[]{:S(2)}) collective-permute-start(bf16[64,2176]{1,0:T(8,128)(2,1)} %get-tuple-element.92), channel_id=1, source_target_pairs={{0,8},{8,0},{1,9},{9,1},{2,10},{10,2},{3,11},{11,3},{4,12},{12,4},... | collective-permute-start | bytes 835592 | tf_op jit(solution)/shard_map/ppermute | solution.py:23
  164.8 8.1 %collective-permute-start.21 = (bf16[64,2176]{1,0:T(8,128)(2,1)}, bf16[64,2176]{1,0:T(8,128)(2,1)S(1)}, u32[]{:S(2)}, u32[]{:S(2)}) collective-permute-start(bf16[64,2176]{1,0:T(8,128)(2,1)} %get-tuple-element.93), channel_id=1, source_target_pairs={{0,6},{2,0},{4,2},{6,4},{1,7},{3,1},{5,3},{7,5},{8,14},{10,8},{12,... | collective-permute-start | bytes 835592 | tf_op jit(solution)/shard_map/ppermute | solution.py:23
  165.4 9.1 %collective-permute-start.22 = (bf16[64,2176]{1,0:T(8,128)(2,1)}, bf16[64,2176]{1,0:T(8,128)(2,1)S(1)}, u32[]{:S(2)}, u32[]{:S(2)}) collective-permute-start(bf16[64,2176]{1,0:T(8,128)(2,1)} %get-tuple-element.94), channel_id=1, source_target_pairs={{0,2},{2,4},{4,6},{6,0},{1,3},{3,5},{5,7},{7,1},{8,10},{10,12},{12... | collective-permute-start | bytes 835592 | tf_op jit(solution)/shard_map/ppermute | solution.py:23
  172.9 1.6 copy-start.14
  172.9 1.5 copy-start.15
  177.6 19.6 %collective-permute-start.23 = (bf16[192,2176]{1,0:T(8,128)(2,1)}, bf16[192,2176]{1,0:T(8,128)(2,1)S(1)}, u32[]{:S(2)}, u32[]{:S(2)}) collective-permute-start(bf16[192,2176]{1,0:T(8,128)(2,1)} %get-tuple-element.105), channel_id=1, source_target_pairs={{0,6},{2,0},{4,2},{6,4},{1,7},{3,1},{5,3},{7,5},{8,14},{10,8},{12,... | collective-permute-start | bytes 2506760 | tf_op jit(solution)/shard_map/ppermute | solution.py:23
  178.0 19.2 %collective-permute-start.24 = (bf16[192,2176]{1,0:T(8,128)(2,1)}, bf16[192,2176]{1,0:T(8,128)(2,1)S(1)}, u32[]{:S(2)}, u32[]{:S(2)}) collective-permute-start(bf16[192,2176]{1,0:T(8,128)(2,1)} %get-tuple-element.106), channel_id=1, source_target_pairs={{0,8},{8,0},{1,9},{9,1},{2,10},{10,2},{3,11},{11,3},{4,12},{12,4},... | collective-permute-start | bytes 2506760 | tf_op jit(solution)/shard_map/ppermute | solution.py:23
  179.1 19.9 %collective-permute-start.25 = (bf16[192,2176]{1,0:T(8,128)(2,1)}, bf16[192,2176]{1,0:T(8,128)(2,1)S(1)}, u32[]{:S(2)}, u32[]{:S(2)}) collective-permute-start(bf16[192,2176]{1,0:T(8,128)(2,1)} %get-tuple-element.95), channel_id=1, source_target_pairs={{0,2},{2,4},{4,6},{6,0},{1,3},{3,5},{5,7},{7,1},{8,10},{10,12},{12... | collective-permute-start | bytes 2506760 | tf_op jit(solution)/shard_map/ppermute | solution.py:23
  197.1 19.3 %collective-permute-start.27 = (bf16[192,2176]{1,0:T(8,128)(2,1)}, bf16[192,2176]{1,0:T(8,128)(2,1)S(1)}, u32[]{:S(2)}, u32[]{:S(2)}) collective-permute-start(bf16[192,2176]{1,0:T(8,128)(2,1)} %get-tuple-element.108), channel_id=1, source_target_pairs={{0,2},{2,4},{4,6},{6,0},{1,3},{3,5},{5,7},{7,1},{8,10},{10,12},{12... | collective-permute-start | bytes 2506760 | tf_op jit(solution)/shard_map/ppermute | solution.py:23
  197.1 1.8 copy-start.11
  197.1 1.8 copy-start.12
  199.8 5.9 %copy-start.21 = (s32[6,32]{1,0:T(8,128)S(1)}, s32[6,32]{1,0:T(8,128)}, u32[]{:S(2)}) copy-start(s32[6,32]{1,0:T(8,128)} %param.14) | copy-start | bytes 2308
  203.9 17.8 %collective-permute-start.26 = (bf16[192,2176]{1,0:T(8,128)(2,1)}, bf16[192,2176]{1,0:T(8,128)(2,1)S(1)}, u32[]{:S(2)}, u32[]{:S(2)}) collective-permute-start(bf16[192,2176]{1,0:T(8,128)(2,1)} %get-tuple-element.107), channel_id=1, source_target_pairs={{0,6},{2,0},{4,2},{6,4},{1,7},{3,1},{5,3},{7,5},{8,14},{10,8},{12,... | collective-permute-start | bytes 2506760 | tf_op jit(solution)/shard_map/ppermute | solution.py:23
  205.4 17.6 %collective-permute-start.28 = (bf16[192,2176]{1,0:T(8,128)(2,1)}, bf16[192,2176]{1,0:T(8,128)(2,1)S(1)}, u32[]{:S(2)}, u32[]{:S(2)}) collective-permute-start(bf16[192,2176]{1,0:T(8,128)(2,1)} %get-tuple-element.109), channel_id=1, source_target_pairs={{0,8},{8,0},{1,9},{9,1},{2,10},{10,2},{3,11},{11,3},{4,12},{12,4},... | collective-permute-start | bytes 2506760 | tf_op jit(solution)/shard_map/ppermute | solution.py:23
  216.4 6.5 %copy-start.8 = (bf16[192,2176]{1,0:T(8,128)(2,1)}, bf16[192,2176]{1,0:T(8,128)(2,1)S(1)}, u32[]{:S(2)}) copy-start(bf16[192,2176]{1,0:T(8,128)(2,1)S(1)} %collective-permute-done.27.m1) | copy-start | bytes 2506756
  223.8 18.2 %copy-start.22 = (s32[1024]{0:T(1024)S(1)}, s32[1024]{0:T(1024)}, u32[]{:S(2)}) copy-start(s32[1024]{0:T(1024)} %param.15) | copy-start | bytes 12292
  229.5 22.7 %all-to-all-start.3 = ((f32[128,1,256]{2,1,0:T(1,128)}), f32[128,1,256]{2,1,0:T(1,128)S(1)}, u32[]{:S(2)}, u32[]{:S(2)}) async-start(f32[128,1,256]{2,1,0:T(1,128)} %get-tuple-element.111), calls=%async_computation.3 | async-start | bytes 262144 | tf_op jit(solution)/shard_map/all_to_all | solution.py:591
  (11 other events, 10.0 us)
where the time goes:
time: 256 us; the launch traced here: 255 us
  Pallas kernels  92.5 us (36%)
  waiting for transfers between devices  81.2 us (32%)
  starting transfers between devices  65.9 us (26%)
  local copies, waits for them, and re-layouts  11.3 us (4%)
  other arithmetic  2.64 us (1%)
    ppermute x27, waiting for transfers between devices, permuted(): return lax.ppermute(array, axis, [(i, (i + by) % n) for i in range(n)])  65.7 us
    pallas_call x3, Pallas kernels, feed_forward(): pl.pallas_call(lambda *refs: forward_body(n, *refs), grid=(2,), in_specs=...  31.2 us
    ppermute x27, starting transfers between devices, permuted(): return lax.ppermute(array, axis, [(i, (i + by) % n) for i in range(n)])  27.1 us
    all_to_all x2, starting transfers between devices, columns(): lax.all_to_all(qkv.reshape(row_peers, rows * HALF, 6 * hs), ROW, split_ax...  13.3 us
    pallas_call x2, Pallas kernels, project(): pl.pallas_call(lambda *refs: project_body(rows, n, *refs), grid=(3,), in_...  13 us
    all_to_all x1, starting transfers between devices, per_device(): lax.all_to_all(line, ALL, split_axis=0, concat_axis=0, tiled=True)  12.5 us
    pallas_call x2, Pallas kernels, terms(): pl.pallas_call(lambda *refs: term_body(hs, rows, group, splits, *refs), i...  11.7 us
    pallas_call x1, Pallas kernels, row_attention(): pl.pallas_call(lambda *refs: row_body(inv_root, hs, *refs), grid=(rows,),...  10.3 us
  transfers between devices with their start and end apart: 33, of which 14 were waited for; matrix products, arithmetic and copies ran while one was open for 3% of the time, Pallas kernels for 27%

commit v1 on v0

--- a/solution.py
+++ b/solution.py
@@ -89,12 +89,13 @@
 
 
 def project_body(rows, n, *refs):
-    mine, theirs, out = refs[n:]
+    mine, theirs, out, edge = refs[n:]
     x = stacked(refs[:n])
     w = jnp.concatenate([mine[0], theirs[0]], axis=1)
     y = dot(x, w).astype(BF16).reshape(4, rows, 2, HALF, w.shape[1])
     for g in range(2):
         out[:, g] = y[:, :, g]
+        edge[:, g] = y[:, rows - 1, g]
 
 
 def project(shards, mine, theirs, rows):
@@ -107,8 +108,14 @@
         lambda *refs: project_body(rows, n, *refs),
         grid=(3,),
         in_specs=whole + [weight] * 2,
-        out_specs=pl.BlockSpec((4, 2, rows, HALF, 2 * hs), lambda j: (0, 0, 0, 0, j)),
-        out_shape=jax.ShapeDtypeStruct((4, 2, rows, HALF, 6 * hs), BF16),
+        out_specs=[
+            pl.BlockSpec((4, 2, rows, HALF, 2 * hs), lambda j: (0, 0, 0, 0, j)),
+            pl.BlockSpec((4, 2, HALF, 2 * hs), lambda j: (0, 0, 0, jnp.maximum(j - 1, 0))),
+        ],
+        out_shape=[
+            jax.ShapeDtypeStruct((4, 2, rows, HALF, 6 * hs), BF16),
+            jax.ShapeDtypeStruct((4, 2, HALF, 4 * hs), BF16),
+        ],
         cost_estimate=cost(2 * total * width * 6 * hs, 2 * total * width + 12 * width * hs),
         name="project",
     )(*shards, mine, theirs)
@@ -442,15 +449,18 @@
     hit = lax.broadcasted_iota(jnp.int32, (devices, count), 0) == where[...]
     hot = jnp.where(hit, 1.0, 0.0).astype(BF16)
 
-    def take(part):
-        return lax.dot_general(part, hot, (((0,), (0,)), ((), ())), preferred_element_type=F32)
-
     full = table[...]
     high = full.astype(BF16)
     rest = full - high.astype(F32)
     mid = rest.astype(BF16)
     low = (rest - mid.astype(F32)).astype(BF16)
-    lines = take(high) + take(mid) + take(low)
+    parts = jnp.concatenate([high, mid, low], axis=0)
+    lines = lax.dot_general(
+        parts,
+        jnp.concatenate([hot, hot, hot], axis=0),
+        (((0,), (0,)), ((), ())),
+        preferred_element_type=F32,
+    )
     mine = lax.broadcasted_iota(jnp.int32, lines.shape, 0) == spot[...]
     picked = jnp.sum(jnp.where(mine, lines, 0.0), axis=0, keepdims=True)
     out[...] = count * picked / jnp.sum(picked, axis=-1, keepdims=True)
@@ -509,31 +519,28 @@
     s_aa, s_pb, s_pa = up_z(s_a), down_z(s_p), swap_x(s_a)
 
     def columns(shards):
-        qkv = project(shards, project_weight, their_project, rows)
+        qkv, edge = project(shards, project_weight, their_project, rows)
         got = lax.all_to_all(
             qkv.reshape(row_peers, rows * HALF, 6 * hs), ROW, split_axis=0, concat_axis=0, tiled=True
         )
-        return qkv, got
+        return qkv, edge, got
 
     def attend_columns(group, got, *earlier):
         x = got.reshape(row_peers * rows, HALF, 6 * hs)
         return column_attention(group, bias, x, rows, hs, inv_root, earlier)
 
-    def edge_of(qkv):
-        return next_row(qkv[:, :, -1, :, 2 * hs :])
-
-    qkv0, got0 = columns((own, s_a, s_b, s_p))
+    qkv0, edge0, got0 = columns((own, s_a, s_b, s_p))
+    edge0 = next_row(edge0)
+    their_edge0 = swap_core(edge0)
     their_qkv0 = swap_core(qkv0)
-    edge0 = edge_of(qkv0)
-    their_edge0 = swap_core(edge0)
     s_aa, s_pa, s_pb = after(qkv0, (s_aa, s_pa, s_pb))
     h_aa, h_pa, h_pb = thirds_of((s_aa, s_pa, s_pb))
     far = (swap_x(h_aa), up_z(h_pa), down_z(h_pb))
     back = attend_columns(0, after((s_aa, s_pa, s_pb), got0))
     away = after((back, their_qkv0), (s_aa, s_pa, s_pb, *far))
-    qkv1, got1 = columns(away)
+    qkv1, edge1, got1 = columns(away)
     their_qkv1 = swap_core(qkv1)
-    edge1 = edge_of(qkv1)
+    edge1 = next_row(edge1)
     their_edge1 = swap_core(edge1)
     ff1 = ffn(after(qkv1, away), 4)
     back = attend_columns(1, after((ff1, their_qkv1), got1), back)

time: 256 us -> 256 us (level)
    unnamed x53 -> x61, local copies, waits for them, and re-layouts: 7.1 us -> 8.05 us
  transfers between devices with their start and end apart: 33 -> 33, of which waited for: 14 -> 16; matrix products, arithmetic and copies ran while one was open for 3% -> 2% of each run, Pallas kernels for 27% -> 25%
where the time goes in v1:
time: 256 us; the launch traced here: 255 us
  Pallas kernels  92.5 us (36%)
  waiting for transfers between devices  83.6 us (33%)
  starting transfers between devices  65.5 us (26%)
  local copies, waits for them, and re-layouts  9.74 us (4%)
  other arithmetic  2.64 us (1%)
    ppermute x27, waiting for transfers between devices, permuted(): return lax.ppermute(array, axis, [(i, (i + by) % n) for i in range(n)])  65.5 us
    pallas_call x3, Pallas kernels, feed_forward(): pl.pallas_call(lambda *refs: forward_body(n, *refs), grid=(2,), in_specs=...  31.2 us
    ppermute x27, starting transfers between devices, permuted(): return lax.ppermute(array, axis, [(i, (i + by) % n) for i in range(n)])  27.7 us
    all_to_all x2, starting transfers between devices, columns(): lax.all_to_all(qkv.reshape(row_peers, rows * HALF, 6 * hs), ROW, split_ax...  13.3 us
    pallas_call x2, Pallas kernels, project(): pl.pallas_call(lambda *refs: project_body(rows, n, *refs), grid=(3,), in_...  13.1 us
    all_to_all x1, starting transfers between devices, per_device(): lax.all_to_all(line, ALL, split_axis=0, concat_axis=0, tiled=True)  12.5 us
    pallas_call x2, Pallas kernels, terms(): pl.pallas_call(lambda *refs: term_body(hs, rows, group, splits, *refs), i...  11.8 us
    pallas_call x1, Pallas kernels, row_attention(): pl.pallas_call(lambda *refs: row_body(inv_root, hs, *refs), grid=(rows,),...  10.3 us
  transfers between devices with their start and end apart: 33, of which 16 were waited for; matrix products, arithmetic and copies ran while one was open for 2% of the time, Pallas kernels for 25%

profile of v1, /device:TPU:1, one launch (start us, length us, event | category | flops | bytes accessed | tf_op | source)
XLA Modules:
  0.0 255.5 jit_solution(15232191739900961235)
XLA Ops:
  0.6 1.5 collective-permute-start.1
  2.6 2.3 normalize.1.refs_0_
  4.9 1.7 collective-permute-start.4
  6.7 2.1 collective-permute-start.5
  8.8 1.2 collective-permute-start.6
  10.2 6.6 %feed_forward.3.refs_3_ = bf16[192,2176]{1,0:T(8,128)(2,1)} custom-call(bf16[192,2048]{1,0:T(8,128)(2,1)} %normalize.1.refs_0_, bf16[2048,512]{1,0:T(8,128)(2,1)} %refs_3_.3, bf16[2048,512]{1,0:T(8,128)(2,1)} %copy-done.4, bf16[512,2048]{1,0:T(8,128)(2,1)} %refs_5_.1, bf16[512,2048]{1,0:T(8,128)(2,1)} %collective-permute-done.2.refs_4_.refs_9_.refs_6_), custom_call_target="tpu_custom_call" | custom-call | flops 1610612736 | bytes 9961472 | tf_op jit(solution)/shard_map/feed_forward/pallas_call | solution.py:160
  16.8 10.1 %collective-permute-done.4.refs_1_.refs_0_ = bf16[192,2048]{1,0:T(8,128)(2,1)S(1)} collective-permute-done((bf16[192,2048]{1,0:T(8,128)(2,1)}, bf16[192,2048]{1,0:T(8,128)(2,1)S(1)}, u32[]{:S(2)}, u32[]{:S(2)}) %collective-permute-start.4) | collective-permute-done | bytes 786464 | tf_op jit(solution)/shard_map/ppermute | solution.py:23
  27.8 6.3 %project.2 = (bf16[4,2,6,16,768]{4,3,2,1,0:T(8,128)(2,1)}, bf16[4,2,16,512]{3,2,1,0:T(8,128)(2,1)}) custom-call(bf16[192,2048]{1,0:T(8,128)(2,1)} %normalize.1.refs_0_, bf16[192,2048]{1,0:T(8,128)(2,1)} %copy-done.24, bf16[192,2048]{1,0:T(8,128)(2,1)} %collective-permute-done.5.refs_2_.refs_1_, bf16[192,2048]{1,0:T(8,128)(2,1)} %collective-permute-done.6.refs_3_.refs_2_, ...), custom_call_target="tpu_custom_call" | custom-call | flops 2415919104 | bytes 6291456 | tf_op jit(solution)/shard_map/project/pallas_call | solution.py:107
  34.2 1.2 collective-permute-start.10
  35.4 6.7 %all-to-all-start = ((bf16[8,96,768]{2,1,0:T(8,128)(2,1)}), bf16[8,96,768]{2,1,0:T(8,128)(2,1)S(1)}, u32[]{:S(2)}, u32[]{:S(2)}) async-start(bf16[8,96,768]{2,1,0:T(8,128)(2,1)} %bitcast.16), calls=%async_computation | async-start | bytes 2359296 | tf_op jit(solution)/shard_map/all_to_all | solution.py:523
  42.5 2.6 %collective-permute-start.9 = (bf16[192,2048]{1,0:T(8,128)(2,1)}, bf16[192,2048]{1,0:T(8,128)(2,1)}, u32[]{:S(2)}, u32[]{:S(2)}) collective-permute-start(bf16[192,2048]{1,0:T(8,128)(2,1)} %collective-permute-done.6.refs_3_.refs_2_), channel_id=1, source_target_pairs={{0,6},{2,0},{4,2},{6,4},{1,7},{3,1},{5,3},{7,5},{8,14},{10,8},{12,... | collective-permute-start | bytes 2359304 | tf_op jit(solution)/shard_map/ppermute | solution.py:23
  45.0 17.2 %collective-permute-done.7.t0.refs_0_ = bf16[192,2048]{1,0:T(8,128)(2,1)S(1)} collective-permute-done((bf16[192,2048]{1,0:T(8,128)(2,1)}, bf16[192,2048]{1,0:T(8,128)(2,1)S(1)}, u32[]{:S(2)}, u32[]{:S(2)}) %collective-permute-start.7) | collective-permute-done | bytes 786464 | tf_op jit(solution)/shard_map/ppermute | solution.py:23
  62.3 10.7 %collective-permute-done.8.t1.refs_1_ = bf16[192,2048]{1,0:T(8,128)(2,1)} collective-permute-done((bf16[192,2048]{1,0:T(8,128)(2,1)}, bf16[192,2048]{1,0:T(8,128)(2,1)}, u32[]{:S(2)}, u32[]{:S(2)}) %collective-permute-start.8) | collective-permute-done | bytes 786464 | tf_op jit(solution)/shard_map/ppermute | solution.py:23
  72.9 2.0 thirds.1
  75.0 1.2 collective-permute-start.11
  76.2 2.7 %collective-permute-start.13 = (bf16[64,2048]{1,0:T(8,128)(2,1)}, bf16[64,2048]{1,0:T(8,128)(2,1)S(1)}, u32[]{:S(2)}, u32[]{:S(2)}) collective-permute-start(bf16[64,2048]{1,0:T(8,128)(2,1)} %get-tuple-element.71), channel_id=1, source_target_pairs={{0,6},{2,0},{4,2},{6,4},{1,7},{3,1},{5,3},{7,5},{8,14},{10,8},{12,... | collective-permute-start | bytes 786440 | tf_op jit(solution)/shard_map/ppermute | solution.py:23
  78.8 1.7 collective-permute-start
  81.5 1.3 pad_maximum_fusion.refs_0_
  82.8 1.1 copy-done.5
  83.9 3.8 %column_attention.2.refs_2_ = bf16[8,2,7,16,256]{4,3,2,1,0:T(8,128)(2,1)} custom-call(f32[2]{0:T(128)} %pad_maximum_fusion.refs_0_, bf16[48,16,768]{2,1,0:T(8,128)(2,1)} %bitcast.21), custom_call_target="tpu_custom_call" | custom-call | flops 452984832 | bytes 1572864 | tf_op jit(solution)/shard_map/column_attention/pallas_call | solution.py:286
  88.6 6.7 %project.3 = (bf16[4,2,6,16,768]{4,3,2,1,0:T(8,128)(2,1)}, bf16[4,2,16,512]{3,2,1,0:T(8,128)(2,1)}) custom-call(bf16[192,2048]{1,0:T(8,128)(2,1)} %copy-done.12, bf16[192,2048]{1,0:T(8,128)(2,1)} %collective-permute-done.8.t1.refs_1_, bf16[192,2048]{1,0:T(8,128)(2,1)} %collective-permute-done.9.t2.refs_2_, bf16[64,2048]{1,0:T(8,128)(2,1)} %copy-done.25, ...), custom_call_target="tpu_custom_call" | custom-call | flops 2415919104 | bytes 6291456 | tf_op jit(solution)/shard_map/project/pallas_call | solution.py:107
  95.7 6.6 %all-to-all-start.1 = ((bf16[8,96,768]{2,1,0:T(8,128)(2,1)}), bf16[8,96,768]{2,1,0:T(8,128)(2,1)S(1)}, u32[]{:S(2)}, u32[]{:S(2)}) async-start(bf16[8,96,768]{2,1,0:T(8,128)(2,1)} %bitcast.17), calls=%async_computation.1 | async-start | bytes 2359296 | tf_op jit(solution)/shard_map/all_to_all | solution.py:523
  102.9 13.4 %feed_forward.4 = (bf16[192,2176]{1,0:T(8,128)(2,1)}, bf16[192,2176]{1,0:T(8,128)(2,1)}, bf16[192,2176]{1,0:T(8,128)(2,1)}, bf16[192,2176]{1,0:T(8,128)(2,1)}) custom-call(bf16[192,2048]{1,0:T(8,128)(2,1)} %copy-done.12, bf16[192,2048]{1,0:T(8,128)(2,1)} %collective-permute-done.8.t1.refs_1_, bf16[192,2048]{1,0:T(8,128)(2,1)} %collective-permute-done.9.t2.refs_2_, ...), custom_call_target="tpu_custom_call" | custom-call | flops 6442450944 | bytes 14680064 | tf_op jit(solution)/shard_map/feed_forward/pallas_call | solution.py:160
  116.3 2.2 all-to-all-done.1
  119.6 3.8 %column_attention.3 = bf16[8,2,7,16,256]{4,3,2,1,0:T(8,128)(2,1)} custom-call(f32[2]{0:T(128)} %pad_maximum_fusion.refs_0_, bf16[48,16,768]{2,1,0:T(8,128)(2,1)} %bitcast.18, bf16[8,2,7,16,256]{4,3,2,1,0:T(8,128)(2,1)} %column_attention.2.refs_2_), custom_call_target="tpu_custom_call", output_to_operand_aliasing={{}: (2, {})} | custom-call | flops 452984832 | bytes 1572864 | tf_op jit(solution)/shard_map/column_attention/pallas_call | solution.py:286
  123.4 5.5 %all-to-all-start.2 = ((bf16[8,2,7,16,256]{4,3,2,1,0:T(8,128)(2,1)}), bf16[8,2,7,16,256]{4,3,2,1,0:T(8,128)(2,1)S(1)}, u32[]{:S(2)}, u32[]{:S(2)}) async-start(bf16[8,2,7,16,256]{4,3,2,1,0:T(8,128)(2,1)} %column_attention.3), calls=%async_computation.2 | async-start | bytes 1835008 | tf_op jit(solution)/shard_map/all_to_all | solution.py:547
  128.9 3.4 %collective-permute-start.15 = (bf16[4,2,16,512]{3,2,1,0:T(8,128)(2,1)S(1)}, bf16[4,2,16,512]{3,2,1,0:T(8,128)(2,1)S(1)}, u32[]{:S(2)}, u32[]{:S(2)}) collective-permute-start(bf16[4,2,16,512]{3,2,1,0:T(8,128)(2,1)S(1)} %copy-done.28), channel_id=1, source_target_pairs={{0,16},{16,32},{32,48},{48,64},{64,80},{80,96},{96,112},{1,17},{17... | collective-permute-start | bytes 393224 | tf_op jit(solution)/shard_map/ppermute | solution.py:44
  132.3 3.1 %collective-permute-start.16 = (bf16[4,2,16,512]{3,2,1,0:T(8,128)(2,1)S(1)}, bf16[4,2,16,512]{3,2,1,0:T(8,128)(2,1)S(1)}, u32[]{:S(2)}, u32[]{:S(2)}) collective-permute-start(bf16[4,2,16,512]{3,2,1,0:T(8,128)(2,1)S(1)} %copy-done.29), channel_id=1, source_target_pairs={{0,16},{16,32},{32,48},{48,64},{64,80},{80,96},{96,112},{1,17},{17... | collective-permute-start | bytes 393224 | tf_op jit(solution)/shard_map/ppermute | solution.py:44
  135.5 5.7 %collective-permute-done.15.refs_11_ = bf16[4,2,16,512]{3,2,1,0:T(8,128)(2,1)S(1)} collective-permute-done((bf16[4,2,16,512]{3,2,1,0:T(8,128)(2,1)S(1)}, bf16[4,2,16,512]{3,2,1,0:T(8,128)(2,1)S(1)}, u32[]{:S(2)}, u32[]{:S(2)}) %collective-permute-start.15) | collective-permute-done | bytes 131104 | tf_op jit(solution)/shard_map/ppermute | solution.py:44
  141.2 2.4 collective-permute-start.17
  144.1 1.3 collective-permute-start.18
  147.8 10.3 %row_attention.1 = (f32[4,2,6,16,256]{4,3,2,1,0:T(8,128)}, f32[4,2,6,16,256]{4,3,2,1,0:T(8,128)}, f32[4,2,6,16,256]{4,3,2,1,0:T(8,128)}, f32[4,2,6,16,256]{4,3,2,1,0:T(8,128)}) custom-call(s32[1]{0:T(128)} %bitcast.6.refs_0_, s32[256,1]{1,0:T(8,128)} %add.135.refs_1_, s32[1,512]{1,0:T(1,128)} %bitcast.27, ...), custom_call_target="tpu_custom_call" | custom-call | flops 1610612736 | bytes 6291456 | tf_op jit(solution)/shard_map/row_attention/pallas_call | solution.py:230
  159.1 5.9 %terms.2 = (bf16[192,2176]{1,0:T(8,128)(2,1)}, bf16[192,2176]{1,0:T(8,128)(2,1)}, bf16[192,2176]{1,0:T(8,128)(2,1)}, bf16[64,2176]{1,0:T(8,128)(2,1)}, bf16[64,2...) custom-call(bf16[8,2,7,16,256]{4,3,2,1,0:T(8,128)(2,1)} %copy-done, f32[4,2,6,16,256]{4,3,2,1,0:T(8,128)} %get-tuple-element.95.refs_1_, ...), custom_call_target="tpu_custom_call" | custom-call | flops 855638016 | bytes 8355840 | tf_op jit(solution)/shard_map/terms/pallas_call | solution.py:335
  166.8 6.6 %collective-permute-done.20.g0 = bf16[64,2176]{1,0:T(8,128)(2,1)S(1)} collective-permute-done((bf16[64,2176]{1,0:T(8,128)(2,1)}, bf16[64,2176]{1,0:T(8,128)(2,1)S(1)}, u32[]{:S(2)}, u32[]{:S(2)}) %collective-permute-start.20) | collective-permute-done | bytes 278560 | tf_op jit(solution)/shard_map/ppermute | solution.py:23
  173.5 1.5 collective-permute-done.22.g2
  175.7 2.4 add_far.1
  180.6 11.2 %feed_forward.5 = (bf16[192,2176]{1,0:T(8,128)(2,1)}, bf16[192,2176]{1,0:T(8,128)(2,1)}, bf16[192,2176]{1,0:T(8,128)(2,1)}) custom-call(bf16[192,2048]{1,0:T(8,128)(2,1)} %copy-done.24, bf16[192,2048]{1,0:T(8,128)(2,1)} %collective-permute-done.5.refs_2_.refs_1_, bf16[192,2048]{1,0:T(8,128)(2,1)} %collective-permute-done.6.refs_3_.refs_2_, ...), custom_call_target="tpu_custom_call" | custom-call | flops 4831838208 | bytes 13107200 | tf_op jit(solution)/shard_map/feed_forward/pallas_call | solution.py:160
  191.8 5.9 %terms.3 = (bf16[192,2176]{1,0:T(8,128)(2,1)}, bf16[192,2176]{1,0:T(8,128)(2,1)}, bf16[192,2176]{1,0:T(8,128)(2,1)}, bf16[192,2176]{1,0:T(8,128)(2,1)}) custom-call(bf16[8,2,7,16,256]{4,3,2,1,0:T(8,128)(2,1)} %copy-done, f32[4,2,6,16,256]{4,3,2,1,0:T(8,128)} %get-tuple-element.93.refs_1_, f32[4,2,6,16,256]{4,3,2,1,0:T(8,128)} %get-tuple-element.94.refs_2_, ...), custom_call_target="tpu_custom_call" | custom-call | flops 855638016 | bytes 8355840 | tf_op jit(solution)/shard_map/terms/pallas_call | solution.py:335
  197.7 1.7 collective-permute-done.25.r2
  200.4 4.1 %add_near.1 = (bf16[192,2176]{1,0:T(8,128)(2,1)}, bf16[192,2176]{1,0:T(8,128)(2,1)}) custom-call(bf16[192,2176]{1,0:T(8,128)(2,1)} %get-tuple-element.111.t0, bf16[192,2176]{1,0:T(8,128)(2,1)} %get-tuple-element.112.t1, bf16[192,2176]{1,0:T(8,128)(2,1)} %copy-done.9, bf16[192,2176]{1,0:T(8,128)(2,1)} %copy-done.10, bf16[192,2176]{1,0:T(8,128)(2,1)} %copy-done.11), custom_call_target="tpu_custom_call" | custom-call | flops 1253376 | bytes 5849088 | tf_op jit(solution)/shard_map/add_near/pallas_call | solution.py:395
  204.5 1.5 collective-permute-start.26
  207.0 9.9 %collective-permute-done.27.m1 = bf16[192,2176]{1,0:T(8,128)(2,1)S(1)} collective-permute-done((bf16[192,2176]{1,0:T(8,128)(2,1)}, bf16[192,2176]{1,0:T(8,128)(2,1)S(1)}, u32[]{:S(2)}, u32[]{:S(2)}) %collective-permute-start.27) | collective-permute-done | bytes 835616 | tf_op jit(solution)/shard_map/ppermute | solution.py:23
  217.0 5.3 %collective-permute-done.26.m0 = bf16[192,2176]{1,0:T(8,128)(2,1)S(1)} collective-permute-done((bf16[192,2176]{1,0:T(8,128)(2,1)}, bf16[192,2176]{1,0:T(8,128)(2,1)S(1)}, u32[]{:S(2)}, u32[]{:S(2)}) %collective-permute-start.26) | collective-permute-done | bytes 835616 | tf_op jit(solution)/shard_map/ppermute | solution.py:23
  222.3 1.2 collective-permute-done.28.m2
  224.4 5.7 %head.1 = (bf16[192,2048]{1,0:T(8,128)(2,1)}, f32[128,1,256]{2,1,0:T(1,128)}) custom-call(bf16[192,2048]{1,0:T(8,128)(2,1)} %bitcast.20, bf16[192,2176]{1,0:T(8,128)(2,1)} %get-tuple-element.110.mine, bf16[192,2176]{1,0:T(8,128)(2,1)} %copy-done.7, bf16[192,2176]{1,0:T(8,128)(2,1)} %copy-done.6, bf16[192,2176]{1,0:T(8,128)(2,1)} %copy-done.8, ...), custom_call_target="tpu_custom_call" | custom-call | tf_op jit(solution)/shard_map/head/pallas_call | solution.py:434
  230.1 12.5 %all-to-all-start.3 = ((f32[128,1,256]{2,1,0:T(1,128)}), f32[128,1,256]{2,1,0:T(1,128)S(1)}, u32[]{:S(2)}, u32[]{:S(2)}) async-start(f32[128,1,256]{2,1,0:T(1,128)} %get-tuple-element.119), calls=%async_computation.3 | async-start | bytes 262144 | tf_op jit(solution)/shard_map/all_to_all | solution.py:598
  243.2 9.6 %all-to-all-done.3 = f32[128,1,256]{2,1,0:T(1,128)S(1)} async-done(((f32[128,1,256]{2,1,0:T(1,128)}), f32[128,1,256]{2,1,0:T(1,128)S(1)}, u32[]{:S(2)}, u32[]{:S(2)}) %all-to-all-start.3) | async-done | bytes 131104 | tf_op jit(solution)/shard_map/all_to_all | solution.py:598
  253.4 2.1 pick.1
  (106 shorter events, 18.5 us)
Async XLA Ops:
  0.6 8.2 %collective-permute-start.1 = (bf16[2048,512]{1,0:T(8,128)(2,1)}, bf16[2048,512]{1,0:T(8,128)(2,1)S(1)}, u32[]{:S(2)}, u32[]{:S(2)}) collective-permute-start(bf16[2048,512]{1,0:T(8,128)(2,1)} %refs_3_.3), channel_id=1, source_target_pairs={{0,1},{1,0},{2,3},{3,2},{4,5},{5,4},{6,7},{7,6},{8,9},{9,8},{10,11... | collective-permute-start | bytes 6291464 | tf_op jit(solution)/shard_map/ppermute | solution.py:23
  2.1 7.9 %collective-permute-start.2 = (bf16[512,2048]{1,0:T(8,128)(2,1)}, bf16[512,2048]{1,0:T(8,128)(2,1)}, u32[]{:S(2)}, u32[]{:S(2)}) collective-permute-start(bf16[512,2048]{1,0:T(8,128)(2,1)} %refs_5_.1), channel_id=1, source_target_pairs={{0,1},{1,0},{2,3},{3,2},{4,5},{5,4},{6,7},{7,6},{8,9},{9,8},{10,11... | collective-permute-start | bytes 6291464 | tf_op jit(solution)/shard_map/ppermute | solution.py:23
  2.2 25.7 %collective-permute-start.3 = (bf16[3,2048,128]{2,1,0:T(8,128)(2,1)}, bf16[3,2048,128]{2,1,0:T(8,128)(2,1)}, u32[]{:S(2)}, u32[]{:S(2)}) collective-permute-start(bf16[3,2048,128]{2,1,0:T(8,128)(2,1)} %refs_6_.2), channel_id=1, source_target_pairs={{0,1},{1,0},{2,3},{3,2},{4,5},{5,4},{6,7},{7,6},{8,9},{9,8},{10,11... | collective-permute-start | bytes 4718600 | tf_op jit(solution)/shard_map/ppermute | solution.py:23
  4.9 21.9 %collective-permute-start.4 = (bf16[192,2048]{1,0:T(8,128)(2,1)}, bf16[192,2048]{1,0:T(8,128)(2,1)S(1)}, u32[]{:S(2)}, u32[]{:S(2)}) collective-permute-start(bf16[192,2048]{1,0:T(8,128)(2,1)} %normalize.1.refs_0_), channel_id=1, source_target_pairs={{0,2},{2,4},{4,6},{6,0},{1,3},{3,5},{5,7},{7,1},{8,10},{10,12},{12... | collective-permute-start | bytes 2359304 | tf_op jit(solution)/shard_map/ppermute | solution.py:23
  6.7 20.2 %collective-permute-start.5 = (bf16[192,2048]{1,0:T(8,128)(2,1)}, bf16[192,2048]{1,0:T(8,128)(2,1)}, u32[]{:S(2)}, u32[]{:S(2)}) collective-permute-start(bf16[192,2048]{1,0:T(8,128)(2,1)} %normalize.1.refs_0_), channel_id=1, source_target_pairs={{0,6},{2,0},{4,2},{6,4},{1,7},{3,1},{5,3},{7,5},{8,14},{10,8},{12,... | collective-permute-start | bytes 2359304 | tf_op jit(solution)/shard_map/ppermute | solution.py:23
  8.8 19.0 %collective-permute-start.6 = (bf16[192,2048]{1,0:T(8,128)(2,1)}, bf16[192,2048]{1,0:T(8,128)(2,1)}, u32[]{:S(2)}, u32[]{:S(2)}) collective-permute-start(bf16[192,2048]{1,0:T(8,128)(2,1)} %normalize.1.refs_0_), channel_id=1, source_target_pairs={{0,8},{8,0},{1,9},{9,1},{2,10},{10,2},{3,11},{11,3},{4,12},{12,4},... | collective-permute-start | bytes 2359304 | tf_op jit(solution)/shard_map/ppermute | solution.py:23
  34.2 53.6 %collective-permute-start.10 = (bf16[4,2,6,16,768]{4,3,2,1,0:T(8,128)(2,1)}, bf16[4,2,6,16,768]{4,3,2,1,0:T(8,128)(2,1)S(1)}, u32[]{:S(2)}, u32[]{:S(2)}) collective-permute-start(bf16[4,2,6,16,768]{4,3,2,1,0:T(8,128)(2,1)} %get-tuple-element.64.refs_3_.refs_5_), channel_id=1, source_target_pairs={{0,1},{1,0},{2,3},{3,2},{4,5},{5,4},{6,7},{7,6},{8,9},{9,8},{10,11... | collective-permute-start | bytes 3538952 | tf_op jit(solution)/shard_map/ppermute | solution.py:23
  35.4 47.4 %all-to-all-start = ((bf16[8,96,768]{2,1,0:T(8,128)(2,1)}), bf16[8,96,768]{2,1,0:T(8,128)(2,1)S(1)}, u32[]{:S(2)}, u32[]{:S(2)}) async-start(bf16[8,96,768]{2,1,0:T(8,128)(2,1)} %bitcast.16), calls=%async_computation | async-start | bytes 2359296 | tf_op jit(solution)/shard_map/all_to_all | solution.py:523
  42.1 20.2 %collective-permute-start.7 = (bf16[192,2048]{1,0:T(8,128)(2,1)}, bf16[192,2048]{1,0:T(8,128)(2,1)S(1)}, u32[]{:S(2)}, u32[]{:S(2)}) collective-permute-start(bf16[192,2048]{1,0:T(8,128)(2,1)} %copy-done.24), channel_id=1, source_target_pairs={{0,2},{2,4},{4,6},{6,0},{1,3},{3,5},{5,7},{7,1},{8,10},{10,12},{12... | collective-permute-start | bytes 2359304 | tf_op jit(solution)/shard_map/ppermute | solution.py:23
  42.1 30.9 %collective-permute-start.8 = (bf16[192,2048]{1,0:T(8,128)(2,1)}, bf16[192,2048]{1,0:T(8,128)(2,1)}, u32[]{:S(2)}, u32[]{:S(2)}) collective-permute-start(bf16[192,2048]{1,0:T(8,128)(2,1)} %copy-done.24), channel_id=1, source_target_pairs={{0,8},{8,0},{1,9},{9,1},{2,10},{10,2},{3,11},{11,3},{4,12},{12,4},... | collective-permute-start | bytes 2359304 | tf_op jit(solution)/shard_map/ppermute | solution.py:23
  42.5 30.5 %collective-permute-start.9 = (bf16[192,2048]{1,0:T(8,128)(2,1)}, bf16[192,2048]{1,0:T(8,128)(2,1)}, u32[]{:S(2)}, u32[]{:S(2)}) collective-permute-start(bf16[192,2048]{1,0:T(8,128)(2,1)} %collective-permute-done.6.refs_3_.refs_2_), channel_id=1, source_target_pairs={{0,6},{2,0},{4,2},{6,4},{1,7},{3,1},{5,3},{7,5},{8,14},{10,8},{12,... | collective-permute-start | bytes 2359304 | tf_op jit(solution)/shard_map/ppermute | solution.py:23
  62.3 10.7 %copy-start.12 = (bf16[192,2048]{1,0:T(8,128)(2,1)}, bf16[192,2048]{1,0:T(8,128)(2,1)S(1)}, u32[]{:S(2)}) copy-start(bf16[192,2048]{1,0:T(8,128)(2,1)S(1)} %collective-permute-done.7.t0.refs_0_) | copy-start | bytes 2359300
  75.0 12.7 %collective-permute-start.11 = (bf16[64,2048]{1,0:T(8,128)(2,1)}, bf16[64,2048]{1,0:T(8,128)(2,1)S(1)}, u32[]{:S(2)}, u32[]{:S(2)}) collective-permute-start(bf16[64,2048]{1,0:T(8,128)(2,1)} %get-tuple-element.69), channel_id=1, source_target_pairs={{0,8},{8,0},{1,9},{9,1},{2,10},{10,2},{3,11},{11,3},{4,12},{12,4},... | collective-permute-start | bytes 786440 | tf_op jit(solution)/shard_map/ppermute | solution.py:23
  76.2 11.5 %collective-permute-start.12 = (bf16[64,2048]{1,0:T(8,128)(2,1)}, bf16[64,2048]{1,0:T(8,128)(2,1)S(1)}, u32[]{:S(2)}, u32[]{:S(2)}) collective-permute-start(bf16[64,2048]{1,0:T(8,128)(2,1)} %get-tuple-element.70), channel_id=1, source_target_pairs={{0,2},{2,4},{4,6},{6,0},{1,3},{3,5},{5,7},{7,1},{8,10},{10,12},{12... | collective-permute-start | bytes 786440 | tf_op jit(solution)/shard_map/ppermute | solution.py:23
  76.2 11.6 %collective-permute-start.13 = (bf16[64,2048]{1,0:T(8,128)(2,1)}, bf16[64,2048]{1,0:T(8,128)(2,1)S(1)}, u32[]{:S(2)}, u32[]{:S(2)}) collective-permute-start(bf16[64,2048]{1,0:T(8,128)(2,1)} %get-tuple-element.71), channel_id=1, source_target_pairs={{0,6},{2,0},{4,2},{6,4},{1,7},{3,1},{5,3},{7,5},{8,14},{10,8},{12,... | collective-permute-start | bytes 786440 | tf_op jit(solution)/shard_map/ppermute | solution.py:23
  78.8 2.7 %collective-permute-start = (f32[1]{0:T(128)}, f32[1]{0:T(128)}, u32[]{:S(2)}, u32[]{:S(2)}) collective-permute-start(f32[1]{0:T(128)} %param.21), channel_id=1, source_target_pairs={{0,1},{1,0},{2,3},{3,2},{4,5},{5,4},{6,7},{7,6},{8,9},{9,8},{10,11... | collective-permute-start | bytes 20 | tf_op jit(solution)/shard_map/ppermute | solution.py:23
  88.6 6.8 %copy-start.2 = (bf16[4,2,6,16,768]{4,3,2,1,0:T(8,128)(2,1)}, bf16[4,2,6,16,768]{4,3,2,1,0:T(8,128)(2,1)S(1)}, u32[]{:S(2)}) copy-start(bf16[4,2,6,16,768]{4,3,2,1,0:T(8,128)(2,1)S(1)} %collective-permute-done.10.refs_7_.refs_9_) | copy-start | bytes 3538948
  95.3 7.5 %copy-start.22 = (s32[8]{0:T(128)S(1)}, s32[8]{0:T(128)}, u32[]{:S(2)}) copy-start(s32[8]{0:T(128)} %constant.117.clone) | copy-start | bytes 100
  95.3 7.5 %copy-start.23 = (s32[8]{0:T(128)S(1)}, s32[8]{0:T(128)}, u32[]{:S(2)}) copy-start(s32[8]{0:T(128)} %constant.118.clone) | copy-start | bytes 100
  95.3 23.2 %collective-permute-start.14 = (bf16[4,2,6,16,768]{4,3,2,1,0:T(8,128)(2,1)}, bf16[4,2,6,16,768]{4,3,2,1,0:T(8,128)(2,1)S(1)}, u32[]{:S(2)}, u32[]{:S(2)}) collective-permute-start(bf16[4,2,6,16,768]{4,3,2,1,0:T(8,128)(2,1)} %get-tuple-element.78.refs_4_.refs_6_), channel_id=1, source_target_pairs={{0,1},{1,0},{2,3},{3,2},{4,5},{5,4},{6,7},{7,6},{8,9},{9,8},{10,11... | collective-permute-start | bytes 3538952 | tf_op jit(solution)/shard_map/ppermute | solution.py:23
  95.7 22.8 %all-to-all-start.1 = ((bf16[8,96,768]{2,1,0:T(8,128)(2,1)}), bf16[8,96,768]{2,1,0:T(8,128)(2,1)S(1)}, u32[]{:S(2)}, u32[]{:S(2)}) async-start(bf16[8,96,768]{2,1,0:T(8,128)(2,1)} %bitcast.17), calls=%async_computation.1 | async-start | bytes 2359296 | tf_op jit(solution)/shard_map/all_to_all | solution.py:523
  102.4 55.7 %collective-permute-start.19 = (bf16[128,2048]{1,0:T(8,128)(2,1)}, bf16[128,2048]{1,0:T(8,128)(2,1)}, u32[]{:S(2)}, u32[]{:S(2)}) collective-permute-start(bf16[128,2048]{1,0:T(8,128)(2,1)} %refs_7_.3), channel_id=1, source_target_pairs={{0,1},{1,0},{2,3},{3,2},{4,5},{5,4},{6,7},{7,6},{8,9},{9,8},{10,11... | collective-permute-start | bytes 1572872 | tf_op jit(solution)/shard_map/ppermute | solution.py:23
  118.5 4.9 %copy-start.3 = (bf16[4,2,6,16,768]{4,3,2,1,0:T(8,128)(2,1)}, bf16[4,2,6,16,768]{4,3,2,1,0:T(8,128)(2,1)S(1)}, u32[]{:S(2)}) copy-start(bf16[4,2,6,16,768]{4,3,2,1,0:T(8,128)(2,1)S(1)} %collective-permute-done.14.refs_8_.refs_10_) | copy-start | bytes 3538948
  123.4 5.5 %copy-start.28 = (bf16[4,2,16,512]{3,2,1,0:T(8,128)(2,1)S(1)}, bf16[4,2,16,512]{3,2,1,0:T(8,128)(2,1)}, u32[]{:S(2)}) copy-start(bf16[4,2,16,512]{3,2,1,0:T(8,128)(2,1)} %get-tuple-element.91) | copy-start | bytes 393220
  123.4 8.9 %copy-start.29 = (bf16[4,2,16,512]{3,2,1,0:T(8,128)(2,1)S(1)}, bf16[4,2,16,512]{3,2,1,0:T(8,128)(2,1)}, u32[]{:S(2)}) copy-start(bf16[4,2,16,512]{3,2,1,0:T(8,128)(2,1)} %get-tuple-element.92) | copy-start | bytes 393220
  123.4 34.7 %all-to-all-start.2 = ((bf16[8,2,7,16,256]{4,3,2,1,0:T(8,128)(2,1)}), bf16[8,2,7,16,256]{4,3,2,1,0:T(8,128)(2,1)S(1)}, u32[]{:S(2)}, u32[]{:S(2)}) async-start(bf16[8,2,7,16,256]{4,3,2,1,0:T(8,128)(2,1)} %column_attention.3), calls=%async_computation.2 | async-start | bytes 1835008 | tf_op jit(solution)/shard_map/all_to_all | solution.py:547
  128.9 12.3 %collective-permute-start.15 = (bf16[4,2,16,512]{3,2,1,0:T(8,128)(2,1)S(1)}, bf16[4,2,16,512]{3,2,1,0:T(8,128)(2,1)S(1)}, u32[]{:S(2)}, u32[]{:S(2)}) collective-permute-start(bf16[4,2,16,512]{3,2,1,0:T(8,128)(2,1)S(1)} %copy-done.28), channel_id=1, source_target_pairs={{0,16},{16,32},{32,48},{48,64},{64,80},{80,96},{96,112},{1,17},{17... | collective-permute-start | bytes 393224 | tf_op jit(solution)/shard_map/ppermute | solution.py:44
  132.3 11.8 %collective-permute-start.16 = (bf16[4,2,16,512]{3,2,1,0:T(8,128)(2,1)S(1)}, bf16[4,2,16,512]{3,2,1,0:T(8,128)(2,1)S(1)}, u32[]{:S(2)}, u32[]{:S(2)}) collective-permute-start(bf16[4,2,16,512]{3,2,1,0:T(8,128)(2,1)S(1)} %copy-done.29), channel_id=1, source_target_pairs={{0,16},{16,32},{32,48},{48,64},{64,80},{80,96},{96,112},{1,17},{17... | collective-permute-start | bytes 393224 | tf_op jit(solution)/shard_map/ppermute | solution.py:44
  141.2 5.9 %copy-start.16 = (bf16[4,2,16,512]{3,2,1,0:T(8,128)(2,1)}, bf16[4,2,16,512]{3,2,1,0:T(8,128)(2,1)S(1)}, u32[]{:S(2)}) copy-start(bf16[4,2,16,512]{3,2,1,0:T(8,128)(2,1)S(1)} %collective-permute-done.15.refs_11_) | copy-start | bytes 393220
  141.2 5.9 %collective-permute-start.17 = (bf16[4,2,16,512]{3,2,1,0:T(8,128)(2,1)S(1)}, bf16[4,2,16,512]{3,2,1,0:T(8,128)(2,1)S(1)}, u32[]{:S(2)}, u32[]{:S(2)}) collective-permute-start(bf16[4,2,16,512]{3,2,1,0:T(8,128)(2,1)S(1)} %collective-permute-done.15.refs_11_), channel_id=1, source_target_pairs={{0,1},{1,0},{2,3},{3,2},{4,5},{5,4},{6,7},{7,6},{8,9},{9,8},{10,11... | collective-permute-start | bytes 393224 | tf_op jit(solution)/shard_map/ppermute | solution.py:23
  144.1 3.0 %copy-start.17 = (bf16[4,2,16,512]{3,2,1,0:T(8,128)(2,1)}, bf16[4,2,16,512]{3,2,1,0:T(8,128)(2,1)S(1)}, u32[]{:S(2)}) copy-start(bf16[4,2,16,512]{3,2,1,0:T(8,128)(2,1)S(1)} %collective-permute-done.16.refs_12_) | copy-start | bytes 393220
  144.1 2.9 %collective-permute-start.18 = (bf16[4,2,16,512]{3,2,1,0:T(8,128)(2,1)S(1)}, bf16[4,2,16,512]{3,2,1,0:T(8,128)(2,1)S(1)}, u32[]{:S(2)}, u32[]{:S(2)}) collective-permute-start(bf16[4,2,16,512]{3,2,1,0:T(8,128)(2,1)S(1)} %collective-permute-done.16.refs_12_), channel_id=1, source_target_pairs={{0,1},{1,0},{2,3},{3,2},{4,5},{5,4},{6,7},{7,6},{8,9},{9,8},{10,11... | collective-permute-start | bytes 393224 | tf_op jit(solution)/shard_map/ppermute | solution.py:23
  165.0 8.4 %collective-permute-start.20 = (bf16[64,2176]{1,0:T(8,128)(2,1)}, bf16[64,2176]{1,0:T(8,128)(2,1)S(1)}, u32[]{:S(2)}, u32[]{:S(2)}) collective-permute-start(bf16[64,2176]{1,0:T(8,128)(2,1)} %get-tuple-element.100), channel_id=1, source_target_pairs={{0,8},{8,0},{1,9},{9,1},{2,10},{10,2},{3,11},{11,3},{4,12},{12,4},... | collective-permute-start | bytes 835592 | tf_op jit(solution)/shard_map/ppermute | solution.py:23
  165.4 8.1 %collective-permute-start.21 = (bf16[64,2176]{1,0:T(8,128)(2,1)}, bf16[64,2176]{1,0:T(8,128)(2,1)S(1)}, u32[]{:S(2)}, u32[]{:S(2)}) collective-permute-start(bf16[64,2176]{1,0:T(8,128)(2,1)} %get-tuple-element.101), channel_id=1, source_target_pairs={{0,6},{2,0},{4,2},{6,4},{1,7},{3,1},{5,3},{7,5},{8,14},{10,8},{12,... | collective-permute-start | bytes 835592 | tf_op jit(solution)/shard_map/ppermute | solution.py:23
  165.9 9.1 %collective-permute-start.22 = (bf16[64,2176]{1,0:T(8,128)(2,1)}, bf16[64,2176]{1,0:T(8,128)(2,1)S(1)}, u32[]{:S(2)}, u32[]{:S(2)}) collective-permute-start(bf16[64,2176]{1,0:T(8,128)(2,1)} %get-tuple-element.102), channel_id=1, source_target_pairs={{0,2},{2,4},{4,6},{6,0},{1,3},{3,5},{5,7},{7,1},{8,10},{10,12},{12... | collective-permute-start | bytes 835592 | tf_op jit(solution)/shard_map/ppermute | solution.py:23
  173.4 1.5 copy-start.13
  178.0 19.6 %collective-permute-start.23 = (bf16[192,2176]{1,0:T(8,128)(2,1)}, bf16[192,2176]{1,0:T(8,128)(2,1)S(1)}, u32[]{:S(2)}, u32[]{:S(2)}) collective-permute-start(bf16[192,2176]{1,0:T(8,128)(2,1)} %get-tuple-element.113), channel_id=1, source_target_pairs={{0,6},{2,0},{4,2},{6,4},{1,7},{3,1},{5,3},{7,5},{8,14},{10,8},{12,... | collective-permute-start | bytes 2506760 | tf_op jit(solution)/shard_map/ppermute | solution.py:23
  178.4 19.3 %collective-permute-start.24 = (bf16[192,2176]{1,0:T(8,128)(2,1)}, bf16[192,2176]{1,0:T(8,128)(2,1)S(1)}, u32[]{:S(2)}, u32[]{:S(2)}) collective-permute-start(bf16[192,2176]{1,0:T(8,128)(2,1)} %get-tuple-element.114), channel_id=1, source_target_pairs={{0,8},{8,0},{1,9},{9,1},{2,10},{10,2},{3,11},{11,3},{4,12},{12,4},... | collective-permute-start | bytes 2506760 | tf_op jit(solution)/shard_map/ppermute | solution.py:23
  179.5 19.9 %collective-permute-start.25 = (bf16[192,2176]{1,0:T(8,128)(2,1)}, bf16[192,2176]{1,0:T(8,128)(2,1)S(1)}, u32[]{:S(2)}, u32[]{:S(2)}) collective-permute-start(bf16[192,2176]{1,0:T(8,128)(2,1)} %get-tuple-element.103), channel_id=1, source_target_pairs={{0,2},{2,4},{4,6},{6,0},{1,3},{3,5},{5,7},{7,1},{8,10},{10,12},{12... | collective-permute-start | bytes 2506760 | tf_op jit(solution)/shard_map/ppermute | solution.py:23
  197.6 19.3 %collective-permute-start.27 = (bf16[192,2176]{1,0:T(8,128)(2,1)}, bf16[192,2176]{1,0:T(8,128)(2,1)S(1)}, u32[]{:S(2)}, u32[]{:S(2)}) collective-permute-start(bf16[192,2176]{1,0:T(8,128)(2,1)} %get-tuple-element.116), channel_id=1, source_target_pairs={{0,2},{2,4},{4,6},{6,0},{1,3},{3,5},{5,7},{7,1},{8,10},{10,12},{12... | collective-permute-start | bytes 2506760 | tf_op jit(solution)/shard_map/ppermute | solution.py:23
  197.7 1.7 copy-start.9
  197.7 1.7 copy-start.10
  200.4 5.9 %copy-start.20 = (s32[6,32]{1,0:T(8,128)S(1)}, s32[6,32]{1,0:T(8,128)}, u32[]{:S(2)}) copy-start(s32[6,32]{1,0:T(8,128)} %param.14) | copy-start | bytes 2308
  204.5 17.8 %collective-permute-start.26 = (bf16[192,2176]{1,0:T(8,128)(2,1)}, bf16[192,2176]{1,0:T(8,128)(2,1)S(1)}, u32[]{:S(2)}, u32[]{:S(2)}) collective-permute-start(bf16[192,2176]{1,0:T(8,128)(2,1)} %get-tuple-element.115), channel_id=1, source_target_pairs={{0,6},{2,0},{4,2},{6,4},{1,7},{3,1},{5,3},{7,5},{8,14},{10,8},{12,... | collective-permute-start | bytes 2506760 | tf_op jit(solution)/shard_map/ppermute | solution.py:23
  205.9 17.5 %collective-permute-start.28 = (bf16[192,2176]{1,0:T(8,128)(2,1)}, bf16[192,2176]{1,0:T(8,128)(2,1)S(1)}, u32[]{:S(2)}, u32[]{:S(2)}) collective-permute-start(bf16[192,2176]{1,0:T(8,128)(2,1)} %get-tuple-element.117), channel_id=1, source_target_pairs={{0,8},{8,0},{1,9},{9,1},{2,10},{10,2},{3,11},{11,3},{4,12},{12,4},... | collective-permute-start | bytes 2506760 | tf_op jit(solution)/shard_map/ppermute | solution.py:23
  217.0 6.5 %copy-start.6 = (bf16[192,2176]{1,0:T(8,128)(2,1)}, bf16[192,2176]{1,0:T(8,128)(2,1)S(1)}, u32[]{:S(2)}) copy-start(bf16[192,2176]{1,0:T(8,128)(2,1)S(1)} %collective-permute-done.27.m1) | copy-start | bytes 2506756
  224.4 18.2 %copy-start.21 = (s32[1024]{0:T(1024)S(1)}, s32[1024]{0:T(1024)}, u32[]{:S(2)}) copy-start(s32[1024]{0:T(1024)} %param.15) | copy-start | bytes 12292
  230.1 22.7 %all-to-all-start.3 = ((f32[128,1,256]{2,1,0:T(1,128)}), f32[128,1,256]{2,1,0:T(1,128)S(1)}, u32[]{:S(2)}, u32[]{:S(2)}) async-start(f32[128,1,256]{2,1,0:T(1,128)} %get-tuple-element.119), calls=%async_computation.3 | async-start | bytes 262144 | tf_op jit(solution)/shard_map/all_to_all | solution.py:598
  (15 other events, 14.5 us)

commit v2 on v1

--- a/solution.py
+++ b/solution.py
@@ -121,157 +121,216 @@
     )(*shards, mine, theirs)
 
 
-def forward_body(n, *refs):
-    up, their_up, down, their_down = refs[n : n + 4]
-    outs, (acc, sums) = refs[n + 4 : -2], refs[-2:]
-    step = pl.program_id(0)
-    x = stacked(refs[:n])
-    h = dot(x, jnp.concatenate([up[...], their_up[...]], axis=1))
-    h = jax.nn.gelu(h, approximate=True).astype(BF16)
-    h_f = h.astype(F32)
-    part = jnp.sum(h_f * h_f, axis=-1, keepdims=True)
-    term = dot(h, jnp.concatenate([down[...], their_down[...]], axis=0))
-
-    @pl.when(step == 0)
-    def _():
-        acc[...] = term
-        sums[...] = jnp.broadcast_to(part, sums.shape)
-
-    @pl.when(step == 1)
-    def _():
-        width = acc.shape[1]
-        total = (acc[...] + term).astype(BF16)
-        squares = (sums[...] + part).astype(BF16)
-        tokens = outs[0].shape[0]
-        for i, out in enumerate(outs):
-            at = slice(tokens * i, tokens * (i + 1))
-            out[:, 0:width] = total[at]
-            out[:, width : width + 128] = squares[at]
+ANY = pl.BlockSpec(memory_space=pl.ANY)
+
+
+def forward_body(n, slots, unrolled, *refs):
+    shards, (up, their_up, down, their_down) = refs[:n], refs[n : n + 4]
+    outs, (x, rise, fall, hidden, done, sems, out_sems) = refs[n + 4 : -7], refs[-7:]
+    tokens = x.shape[0] // slots
+    width, units = up.shape
+    sizes = [ref.shape[0] for ref in shards]
+    starts = [sum(sizes[:i]) for i in range(n)]
+
+    def fetch(source, target, i):
+        copy = pltpu.make_async_copy(source, target, sems.at[i])
+        copy.start()
+        return copy
+
+    def shard(i):
+        return fetch(shards[i], x.at[starts[i] : starts[i] + sizes[i]], i)
+
+    x_in = [shard(0)]
+    ups = [fetch(up, rise.at[:, :units], n), fetch(their_up, rise.at[:, units:], n + 1)]
+    x_in += [shard(i) for i in range(1, n)]
+    downs = [fetch(down, fall.at[:units], n + 2), fetch(their_down, fall.at[units:], n + 3)]
+
+    def rows_of(s):
+        return pl.ds(s * tokens if unrolled else pl.multiple_of(s * tokens, tokens), tokens)
+
+    def each_slot(step):
+        if unrolled:
+            for s in range(slots):
+                step(s, 0)
+        else:
+            lax.fori_loop(0, slots, step, 0)
+
+    def ascend(s, carry):
+        at = rows_of(s)
+        for i in range(n):
+
+            @pl.when(s == starts[i] // tokens)
+            def _():
+                x_in[i].wait()
+
+        total = 0.0
+        for c in range(2):
+
+            @pl.when(s == 0)
+            def _():
+                ups[c].wait()
+
+            lanes = slice(units * c, units * (c + 1))
+            h = jax.nn.gelu(dot(x[at, :], rise[:, lanes]), approximate=True).astype(BF16)
+            hidden[at, lanes] = h
+            h_f = h.astype(F32)
+            total = total + jnp.sum(h_f * h_f, axis=-1, keepdims=True)
+        done[at, width : width + 128] = jnp.broadcast_to(total, (tokens, 128)).astype(BF16)
+        return carry
+
+    each_slot(ascend)
+    for copy in downs:
+        copy.wait()
+    copies = []
+    for s in range(slots):
+        source = done.at[tokens * s : tokens * (s + 1)]
+        copies.append(pltpu.make_async_copy(source, outs[s], out_sems.at[s]))
+
+    def descend(s, carry):
+        at = rows_of(s)
+        done[at, 0:width] = dot(hidden[at, :], fall[...]).astype(BF16)
+        for i in range(slots):
+
+            @pl.when(s == i)
+            def _():
+                copies[i].start()
+
+        return carry
+
+    each_slot(descend)
+    for copy in copies:
+        copy.wait()
 
 
 def feed_forward(shards, slots, up, their_up, down, their_down):
     n = len(shards)
     total = sum(v.shape[0] for v in shards)
     tokens, width = total // slots, shards[0].shape[1]
-    units = up.shape[1] // 2
-    whole = [pl.BlockSpec(v.shape, lambda j: (0, 0)) for v in shards]
-    rise = pl.BlockSpec((width, units), lambda j: (0, j))
-    fall = pl.BlockSpec((units, width), lambda j: (j, 0))
-    return pl.pallas_call(
-        lambda *refs: forward_body(n, *refs),
-        grid=(2,),
-        in_specs=whole + [rise, rise, fall, fall],
-        out_specs=[pl.BlockSpec((tokens, width + 128), lambda j: (0, 0))] * slots,
+    units = 2 * up.shape[1]
+    return pl.pallas_call(
+        lambda *refs: forward_body(n, slots, slots == 4, *refs),
+        in_specs=[ANY] * (n + 4),
+        out_specs=[ANY] * slots,
         out_shape=[jax.ShapeDtypeStruct((tokens, width + 128), BF16)] * slots,
-        scratch_shapes=[pltpu.VMEM((total, width), F32), pltpu.VMEM((total, 128), F32)],
-        cost_estimate=cost(16 * total * width * units, 4 * total * width + 16 * width * units),
+        scratch_shapes=[
+            pltpu.VMEM((total, width), BF16),
+            pltpu.VMEM((width, units), BF16),
+            pltpu.VMEM((units, width), BF16),
+            pltpu.VMEM((total, units), BF16),
+            pltpu.VMEM((total, width + 128), BF16),
+            pltpu.SemaphoreType.DMA((n + 4,)),
+            pltpu.SemaphoreType.DMA((slots,)),
+        ],
+        cost_estimate=cost(4 * total * width * units, 4 * total * width + 4 * width * units),
         name="feed_forward",
     )(*shards, up, their_up, down, their_down)
 
 
 def row_body(inv_root, hs, top_ref, qcol, kcol, *refs):
-    (cur0, cur1, prv0, prv1, pcur0, pcur1, pprv0, pprv1) = refs[:8]
-    (edge0, edge1, pedge0, pedge1) = refs[8:12]
-    accs, dens = refs[12:14], refs[14:16]
+    cur, theirs, edges = refs[:2], refs[2:6], refs[6:10]
+    accs, dens, above = refs[10:12], refs[12:14], refs[14:]
     r = pl.program_id(0)
     first = r == 0
     n = qcol.shape[0] // 2
     mask = kcol[...] <= qcol[...]
-    open_prev = jnp.logical_not(jnp.logical_and(first, top_ref[0] == 1))
-    used = jnp.logical_or(mask, jnp.broadcast_to(open_prev, mask.shape))
-
-    def part(ref, at):
-        return ref[:, :, 0, :, at : at + hs].reshape(n, hs)
-
-    def edge_part(ref, at):
-        return ref[:, :, :, at : at + hs].reshape(n, hs)
-
-    def either(prv, edge, at):
-        return jnp.where(first, edge_part(edge, at), part(prv, 2 * hs + at))
-
+    closed = jnp.logical_and(first, top_ref[0] == 1)
+    same_one = jnp.where(mask, 1.0, 0.0)
+    prev_one = jnp.where(closed, 0.0, 1.0 - same_one).astype(BF16)
+    same_one = same_one.astype(BF16)
+    ones = jnp.ones((kcol.shape[1], hs), BF16)
+    scale = inv_root * math.log2(math.e)
+
+    @pl.when(first)
+    def _():
+        for keep, edge in zip(above, edges):
+            keep[...] = edge[...].reshape(n, 4 * hs)
+
+    now = [ref[:, :, 0, :, 2 * hs :].reshape(n, 4 * hs) for ref in cur]
+    for i in range(2):
+        pair = [ref[:, :, 0].reshape(n, 2 * hs) for ref in theirs[2 * i : 2 * i + 2]]
+        now.append(jnp.concatenate(pair, axis=1))
+    before = [ref[...] for ref in above]
     for h in range(2):
-        q = jnp.concatenate([part(cur0, h * hs), part(cur1, h * hs)], axis=0)
-
-        def pair(base):
-            a, b = base + hs * h, base + hs * (1 - h)
-            same = [part(cur0, 2 * hs + a), part(cur1, 2 * hs + a)]
-            same += [part(pcur0, 2 * hs + b), part(pcur1, 2 * hs + b)]
-            prev = [either(prv0, edge0, a), either(prv1, edge1, a)]
-            prev += [either(pprv0, pedge0, b), either(pprv1, pedge1, b)]
-            return jnp.concatenate(same, axis=0), jnp.concatenate(prev, axis=0)
-
-        k_same, k_prev = pair(0)
-        v_same, v_prev = pair(2 * hs)
-        scores = jnp.where(mask, dot_t(q, k_same), dot_t(q, k_prev)) * inv_root
-        w = jnp.where(used, jnp.exp(scores), 0.0)
-        total = jnp.sum(w, axis=-1, keepdims=True)
-        w_same = jnp.where(mask, w, 0.0).astype(BF16)
-        w_prev = jnp.where(mask, 0.0, w).astype(BF16)
-        out = dot(w_same, v_same) + dot(w_prev, v_prev)
-        total = jnp.broadcast_to(total, out.shape)
+        at = slice(h * hs, (h + 1) * hs)
+        q = jnp.concatenate([ref[:, :, 0, :, at].reshape(n, hs) for ref in cur], axis=0)
+
+        def taken(parts, base):
+            lanes = [base + hs * h] * 2 + [base + hs * (1 - h)] * 2
+            return jnp.concatenate([p[:, m : m + hs] for p, m in zip(parts, lanes)], axis=0)
+
+        scores = jnp.where(mask, dot_t(q, taken(now, 0)), dot_t(q, taken(before, 0))) * scale
+        w = jnp.exp2(scores).astype(BF16)
+        out = dot(w * same_one, jnp.concatenate([taken(now, 2 * hs), ones], axis=1))
+        out = out + dot(w * prev_one, jnp.concatenate([taken(before, 2 * hs), ones], axis=1))
+        shape = (4, 2, HALF, hs)
         for i in range(2):
-            at = slice(h * hs, (h + 1) * hs)
-            shape = (4, 2, HALF, hs)
-            accs[i][:, :, 0, :, at] = out[n * i : n * (i + 1)].reshape(shape)
-            dens[i][:, :, 0, :, at] = total[n * i : n * (i + 1)].reshape(shape)
+            half = out[n * i : n * (i + 1)]
+            accs[i][:, :, 0, :, at] = half[:, :hs].astype(BF16).reshape(shape)
+            dens[i][:, :, 0, :, at] = half[:, hs:].reshape(shape)
+    for keep, value in zip(above, now):
+        keep[...] = value
 
 
 def row_attention(top, qcol, kcol, qkv, their_qkv, edge, their_edge, hs, inv_root):
     rows = qkv[0].shape[2]
-    width = 6 * hs
-    now = pl.BlockSpec((4, 2, 1, HALF, width), lambda r: (0, 0, r, 0, 0))
-    before = pl.BlockSpec(
-        (4, 2, 1, HALF, width), lambda r: (0, 0, jnp.maximum(r - 1, 0), 0, 0)
-    )
+    now = pl.BlockSpec((4, 2, 1, HALF, 6 * hs), lambda r: (0, 0, r, 0, 0))
+    keys = pl.BlockSpec((4, 2, 1, HALF, 2 * hs), lambda r: (0, 0, r, 0, 1))
+    values = pl.BlockSpec((4, 2, 1, HALF, 2 * hs), lambda r: (0, 0, r, 0, 2))
     whole = lambda a: pl.BlockSpec(a.shape, lambda r: (0,) * a.ndim)
-    out = jax.ShapeDtypeStruct((4, 2, rows, HALF, 2 * hs), F32)
+    out = lambda kind: jax.ShapeDtypeStruct((4, 2, rows, HALF, 2 * hs), kind)
     out_spec = pl.BlockSpec((4, 2, 1, HALF, 2 * hs), lambda r: (0, 0, r, 0, 0))
     n = qcol.shape[0]
     outs = pl.pallas_call(
         lambda *refs: row_body(inv_root, hs, *refs),
         grid=(rows,),
-        in_specs=[SMEM, whole(qcol), whole(kcol)]
-        + [now, now, before, before] * 2
+        in_specs=[SMEM, whole(qcol), whole(kcol), now, now, keys, values, keys, values]
         + [whole(e) for e in (*edge, *their_edge)],
         out_specs=[out_spec] * 4,
-        out_shape=[out] * 4,
+        out_shape=[out(BF16)] * 2 + [out(F32)] * 2,
+        scratch_shapes=[pltpu.VMEM((n // 2, 4 * hs), BF16)] * 4,
         cost_estimate=cost(rows * 32 * n * n * hs, rows * 32 * n * hs, rows * 4 * n * n),
         name="row_attention",
-    )(top, qcol, kcol, *qkv, *qkv, *their_qkv, *their_qkv, *edge, *their_edge)
+    )(
+        top, qcol, kcol, *qkv, their_qkv[0], their_qkv[0], their_qkv[1], their_qkv[1],
+        *edge, *their_edge,
+    )
     return outs[:2], outs[2:]
 
 
-def col_body(inv_root, hs, own_rows, bias, x, *refs):
+def col_body(inv_root, hs, own_rows, bias, their_bias, x, *refs):
     out = refs[-1]
     rows, cols, _ = x.shape
     chunk = 16
     spots = rows * cols
     step = chunk * cols
-    den_rows = jnp.zeros((rows, 128), F32)
-    lane = lax.broadcasted_iota(jnp.int32, (spots, 128), 1)
-    spot = lax.broadcasted_iota(jnp.int32, (spots, 128), 0)
-    for h in range(2):
-
-        def part(at):
-            return x[:, :, at * hs : (at + 1) * hs].reshape(spots, hs)
-
-        q, k, v = part(h), part(2 + h), part(4 + h)
-        accs, sums = [], []
-        for i in range(rows // chunk):
-            n = step * (i + 1)
-            s = dot_t(q[step * i : step * (i + 1)], k[:n]) * inv_root + bias[h]
-            qi = lax.broadcasted_iota(jnp.int32, s.shape, 0) + step * i
-            ki = lax.broadcasted_iota(jnp.int32, s.shape, 1)
-            keep = jnp.logical_and(((qi - ki) & (cols - 1)) == 0, ki < qi)
-            w = jnp.where(keep, jnp.exp(s), 0.0)
-            accs.append(dot(w.astype(BF16), v[:n]))
-            sums.append(jnp.sum(w, axis=-1, keepdims=True))
-        a = jnp.concatenate(accs, axis=0).astype(BF16).reshape(rows, cols, hs)
-        d = jnp.concatenate(sums, axis=0)
-        spread = jnp.where(lane == (spot & (cols - 1)) + cols * h, d, 0.0)
-        den_rows = den_rows + jnp.sum(spread.reshape(rows, cols, 128), axis=1)
-        for r in range(rows):
-            out[r // own_rows, 0, r % own_rows, :, h * hs : (h + 1) * hs] = a[r]
+    log2e = math.log2(math.e)
+    lane = lax.broadcasted_iota(jnp.int32, (step, 128), 1)
+    spot = lax.broadcasted_iota(jnp.int32, (step, 128), 0) & (cols - 1)
+    ones = jnp.ones((spots, hs), BF16)
+
+    def part(at):
+        return x[:, :, at * hs : (at + 1) * hs].reshape(spots, hs)
+
+    den_rows = []
+    for i in range(rows // chunk):
+        n = step * (i + 1)
+        qi = lax.broadcasted_iota(jnp.int32, (step, n), 0) + step * i
+        ki = lax.broadcasted_iota(jnp.int32, (step, n), 1)
+        keep = jnp.logical_and(((qi - ki) & (cols - 1)) == 0, ki < qi)
+        laid_out = 0.0
+        for h in range(2):
+            q, k, v = part(h), part(2 + h), part(4 + h)
+            s = dot_t(q[step * i : n], k[:n]) * (inv_root * log2e)
+            s = s + (bias, their_bias)[h][0] * log2e
+            w = jnp.where(keep, jnp.exp2(s), 0.0).astype(BF16)
+            a = dot(w, jnp.concatenate([v[:n], ones[:n]], axis=1))
+            laid_out = laid_out + jnp.where(lane == spot + cols * h, a[:, hs:], 0.0)
+            a = a[:, :hs].astype(BF16).reshape(chunk, cols, hs)
+            for j in range(chunk):
+                r = chunk * i + j
+                out[r // own_rows, 0, r % own_rows, :, h * hs : (h + 1) * hs] = a[j]
+        den_rows.append(jnp.sum(laid_out.reshape(chunk, cols, 128), axis=1))
+    den_rows = jnp.concatenate(den_rows, axis=0)
     fill = jnp.zeros((cols - own_rows, 128), F32)
     for b in range(rows // own_rows):
         block = jnp.concatenate([den_rows[own_rows * b : own_rows * (b + 1)], fill], axis=0)
@@ -286,58 +345,64 @@
     return pl.pallas_call(
         lambda *refs: col_body(inv_root, hs, own_rows, *refs),
         grid=(1,),
-        in_specs=[SMEM, pl.BlockSpec(x.shape, lambda i: (0, 0, 0))]
+        in_specs=[SMEM, SMEM, pl.BlockSpec(x.shape, lambda i: (0, 0, 0))]
         + [pl.BlockSpec(memory_space=pl.ANY)] * len(earlier),
         out_specs=pl.BlockSpec(
             (peers, 1, own_rows + 1, cols, 2 * hs), lambda i: (0, group, 0, 0, 0)
         ),
         out_shape=jax.ShapeDtypeStruct((peers, 2, own_rows + 1, cols, 2 * hs), BF16),
-        input_output_aliases={2: 0} if earlier else {},
+        input_output_aliases={3: 0} if earlier else {},
         cost_estimate=cost(6 * spots * spots * hs, 16 * spots * hs, 2 * spots * spots),
         name="column_attention",
-    )(bias, x, *earlier)
-
-
-def term_body(hs, rows, group, splits, got, acc, den, f0, f1, f2, f3, w_mine, w_their, *outs):
-    spots = 8 * rows * HALF
-    unit = lax.broadcasted_iota(jnp.int32, (spots, 128), 0) // HALF
-    line = lax.broadcasted_iota(jnp.int32, (spots, 128), 1)
+    )(*bias, x, *earlier)
+
+
+def term_body(hs, rows, group, base, splits, got, acc, den, *refs):
+    count = len({slot for slot, _, _ in splits})
+    ffs, (w_mine, w_their), outs = refs[:count], refs[count : count + 2], refs[count + 2 :]
+    spots = 2 * count * rows * HALF
+    lines = 2 * count * HALF
+    pairs = slice(2 * base, 2 * (base + count))
+    slots = slice(base, base + count)
+    unit = lax.broadcasted_iota(jnp.int32, (spots, lines), 0) // HALF
+    line = lax.broadcasted_iota(jnp.int32, (spots, lines), 1)
     hit = jnp.logical_and(unit == (line // HALF) * rows + line % HALF, line % HALF < rows)
-    table = got[:, group, rows, :, 0:128].reshape(128, 128)
+    table = got[pairs, group, rows, :, 0:128].reshape(lines, 128)
     table = dot(jnp.where(hit, 1.0, 0.0).astype(BF16), table)
+    lane = lax.broadcasted_iota(jnp.int32, (spots, 128), 1)
     spot = lax.broadcasted_iota(jnp.int32, (spots, 128), 0) % HALF
     ones = jnp.ones((128, 128), BF16)
     parts = []
     for h in range(2):
         at = slice(h * hs, (h + 1) * hs)
-        col_den = dot(jnp.where(line == spot + HALF * h, table, 0.0).astype(BF16), ones)
-        total = acc[:, :, :, :, at].reshape(spots, hs)
-        total = total + got[:, group, 0:rows, :, at].reshape(spots, hs).astype(F32)
-        parts.append((total / (den[:, :, :, :, at].reshape(spots, hs) + col_den)).astype(BF16))
-    halves = jnp.concatenate(parts, axis=1).reshape(4, 2, rows, HALF, 2 * hs)
-    blocks = [halves[s, g, r] for s in range(4) for r in range(rows) for g in range(2)]
+        col_den = dot(jnp.where(lane == spot + HALF * h, table, 0.0).astype(BF16), ones)
+        total = acc[slots, :, :, :, at].reshape(spots, hs).astype(F32)
+        total = total + got[pairs, group, 0:rows, :, at].reshape(spots, hs).astype(F32)
+        parts.append((total / (den[slots, :, :, :, at].reshape(spots, hs) + col_den)).astype(BF16))
+    halves = jnp.concatenate(parts, axis=1).reshape(count, 2, rows, HALF, 2 * hs)
+    blocks = [halves[s, g, r] for s in range(count) for r in range(rows) for g in range(2)]
     attended = jnp.concatenate(blocks, axis=0)
     att_f = attended.astype(F32)
     squares = jnp.sum(att_f * att_f, axis=-1, keepdims=True)
     weight = jnp.concatenate([w_mine[...], w_their[...]], axis=0)
-    term = dot(attended, weight)
+    term = dot(attended, weight).astype(BF16)
     width = term.shape[1]
     for out, (slot, low, high) in zip(outs, splits):
-        f = (f0, f1, f2, f3)[slot]
+        f = ffs[slot]
         tokens = f.shape[0]
         at = slice(tokens * slot + low, tokens * slot + high)
-        out[:, 0:width] = (f[low:high, 0:width].astype(F32) + term[at]).astype(BF16)
+        out[:, 0:width] = f[low:high, 0:width] + term[at]
         out[:, width:] = (f[low:high, width:].astype(F32) + squares[at]).astype(BF16)
 
 
-def terms(group, got, acc, den, ff, w_mine, w_their, hs, rows, splits):
+def terms(group, base, got, acc, den, ff, w_mine, w_their, hs, rows, splits):
     tokens, full = ff[0].shape
     return pl.pallas_call(
-        lambda *refs: term_body(hs, rows, group, splits, *refs),
-        in_specs=[VMEM] * 9,
+        lambda *refs: term_body(hs, rows, group, base, splits, *refs),
+        in_specs=[VMEM] * (5 + len(ff)),
         out_specs=[VMEM] * len(splits),
         out_shape=[jax.ShapeDtypeStruct((b - a, full), BF16) for _, a, b in splits],
-        cost_estimate=cost(16 * tokens * hs * full, 20 * tokens * full),
+        cost_estimate=cost(4 * len(ff) * tokens * hs * full, 5 * len(ff) * tokens * full),
         name="terms",
     )(got, acc, den, *ff, w_mine, w_their)
 
@@ -365,7 +430,7 @@
 
 def far_body(t0, t1, t2, g0, g1, g2, o0, o1, o2):
     for t, g, o in ((t0, g0, o0), (t1, g1, o1), (t2, g2, o2)):
-        o[...] = (t[...].astype(F32) + g[...].astype(F32)).astype(BF16)
+        o[...] = t[...] + g[...]
 
 
 def add_far(arrays, parts):
@@ -385,8 +450,8 @@
 
 
 def near_body(t0, t1, r0, r1, r2, o0, o1):
-    o0[...] = (t0[...].astype(F32) + r0[...].astype(F32) + r1[...].astype(F32)).astype(BF16)
-    o1[...] = (t1[...].astype(F32) + r2[...].astype(F32)).astype(BF16)
+    o0[...] = t0[...] + (r0[...] + r1[...])
+    o1[...] = t1[...] + r2[...]
 
 
 def add_near(*arrays):
@@ -502,7 +567,7 @@
     their_up = swap_core(up_weight)
     their_down = swap_core(down_weight)
     their_output = swap_core(output_weight)
-    bias = jnp.concatenate([pattern_bias, swap_core(pattern_bias)])
+    bias = (pattern_bias, swap_core(pattern_bias))
 
     x = activations.reshape(tokens, width)
     own = normalize(x, mix_gain[None, :])
@@ -567,17 +632,21 @@
         hs,
         inv_root,
     )
-    thirds = [(3, third * i, third * (i + 1)) for i in range(3)]
-    t_aa, t_pa, t_pb, f0, f1, f2 = terms(
-        1, again, acc[1], den[1], ff1, output_weight, their_output, hs, rows,
-        [(i, 0, tokens) for i in range(3)] + thirds,
-    )
-
-    t_aa, t_pa, t_pb = add_far((t_aa, t_pa, t_pb), (swap_x(f0), down_z(f1), up_z(f2)))
+    f0, f1, f2 = terms(
+        1, 3, again, acc[1], den[1], ff1[3:], output_weight, their_output, hs, rows,
+        [(0, third * i, third * (i + 1)) for i in range(3)],
+    )
+    g0, g1, g2 = swap_x(f0), down_z(f1), up_z(f2)
+    t_aa, t_pa, t_pb = terms(
+        1, 0, *after(f0, (again, acc[1], den[1])), ff1[:3], output_weight, their_output, hs, rows,
+        [(i, 0, tokens) for i in range(3)],
+    )
+
+    t_aa, t_pa, t_pb = add_far((t_aa, t_pa, t_pb), (g0, g1, g2))
     r_aa, r_pa, r_pb = down_z(t_aa), swap_x(t_pa), up_z(t_pb)
     ff0 = ffn(after(t_pb, (s_a, s_b, s_p)), 3)
     t_own, t_a, t_b, t_p = terms(
-        0, again, acc[0], den[0], (ff_own, *ff0), output_weight, their_output, hs, rows,
+        0, 0, again, acc[0], den[0], (ff_own, *ff0), output_weight, their_output, hs, rows,
         [(i, 0, tokens) for i in range(4)],
     )
     from_b = up_z(t_b)

time: 256 us -> 253 us (0.988)
    pallas_call x5 -> x6, Pallas kernels: 43 us -> 42.1 us  [the longest x3 27.8 us: feed_forward(): pl.pallas_call(lambda *refs: forward_body(n, slots, slots == 4, *refs), i...]
    unnamed x61 -> x63, local copies, waits for them, and re-layouts: 8.05 us -> 7.61 us
  transfers between devices with their start and end apart: 33 -> 33, of which waited for: 16 -> 18; matrix products, arithmetic and copies ran while one was open for 2% -> 1% of each run, Pallas kernels for 25% -> 26%
where the time goes in v2:
time: 253 us; the launch traced here: 252 us
  Pallas kernels  91.3 us (36%)
  waiting for transfers between devices  82.7 us (33%)
  starting transfers between devices  65.6 us (26%)
  local copies, waits for them, and re-layouts  9.29 us (4%)
    ppermute x27, waiting for transfers between devices, permuted(): return lax.ppermute(array, axis, [(i, (i + by) % n) for i in range(n)])  63.4 us
    pallas_call x3, Pallas kernels, feed_forward(): pl.pallas_call(lambda *refs: forward_body(n, slots, slots == 4, *refs), i...  27.8 us
    ppermute x27, starting transfers between devices, permuted(): return lax.ppermute(array, axis, [(i, (i + by) % n) for i in range(n)])  27.7 us
    pallas_call x3, Pallas kernels, terms(): pl.pallas_call(lambda *refs: term_body(hs, rows, group, base, splits, *re...  14.3 us
    all_to_all x2, starting transfers between devices, columns(): lax.all_to_all(qkv.reshape(row_peers, rows * HALF, 6 * hs), ROW, split_ax...  13.4 us
    pallas_call x2, Pallas kernels, project(): pl.pallas_call(lambda *refs: project_body(rows, n, *refs), grid=(3,), in_...  13.1 us
    all_to_all x1, starting transfers between devices, per_device(): lax.all_to_all(line, ALL, split_axis=0, concat_axis=0, tiled=True)  12.3 us
    all_to_all x1, waiting for transfers between devices, per_device(): lax.all_to_all(line, ALL, split_axis=0, concat_axis=0, tiled=True)  9.59 us
  transfers between devices with their start and end apart: 33, of which 18 were waited for; matrix products, arithmetic and copies ran while one was open for 1% of the time, Pallas kernels for 26%

profile of v2, /device:TPU:1, one launch (start us, length us, event | category | flops | bytes accessed | tf_op | source)
XLA Modules:
  0.0 251.8 jit_solution(6050039537091173664)
XLA Ops:
  0.6 1.5 collective-permute-start.1
  2.6 2.3 normalize.1.refs_0_
  4.9 1.7 collective-permute-start.4
  6.7 2.1 collective-permute-start.5
  8.8 1.2 collective-permute-start.6
  10.1 5.7 %feed_forward.3.refs_3_ = bf16[192,2176]{1,0:T(8,128)(2,1)} custom-call(bf16[192,2048]{1,0:T(8,128)(2,1)} %normalize.1.refs_0_, bf16[2048,512]{1,0:T(8,128)(2,1)} %refs_3_.3, bf16[2048,512]{1,0:T(8,128)(2,1)} %copy-done.6, bf16[512,2048]{1,0:T(8,128)(2,1)} %refs_5_.1, bf16[512,2048]{1,0:T(8,128)(2,1)} %collective-permute-done.2.refs_4_.refs_9_.refs_6_), custom_call_target="tpu_custom_call" | custom-call | flops 1610612736 | bytes 9961472 | tf_op jit(solution)/shard_map/feed_forward/pallas_call | solution.py:210
  15.8 11.0 %collective-permute-done.4.refs_1_.refs_0_ = bf16[192,2048]{1,0:T(8,128)(2,1)S(1)} collective-permute-done((bf16[192,2048]{1,0:T(8,128)(2,1)}, bf16[192,2048]{1,0:T(8,128)(2,1)S(1)}, u32[]{:S(2)}, u32[]{:S(2)}) %collective-permute-start.4) | collective-permute-done | bytes 786464 | tf_op jit(solution)/shard_map/ppermute | solution.py:23
  27.8 6.4 %project.2 = (bf16[4,2,6,16,768]{4,3,2,1,0:T(8,128)(2,1)}, bf16[4,2,16,512]{3,2,1,0:T(8,128)(2,1)}) custom-call(bf16[192,2048]{1,0:T(8,128)(2,1)} %normalize.1.refs_0_, bf16[192,2048]{1,0:T(8,128)(2,1)} %copy-done.26, bf16[192,2048]{1,0:T(8,128)(2,1)} %collective-permute-done.5.refs_2_.refs_1_, bf16[192,2048]{1,0:T(8,128)(2,1)} %collective-permute-done.6.refs_3_.refs_2_, ...), custom_call_target="tpu_custom_call" | custom-call | flops 2415919104 | bytes 6291456 | tf_op jit(solution)/shard_map/project/pallas_call | solution.py:107
  34.2 1.2 collective-permute-start.10
  35.4 6.7 %all-to-all-start = ((bf16[8,96,768]{2,1,0:T(8,128)(2,1)}), bf16[8,96,768]{2,1,0:T(8,128)(2,1)S(1)}, u32[]{:S(2)}, u32[]{:S(2)}) async-start(bf16[8,96,768]{2,1,0:T(8,128)(2,1)} %bitcast.17), calls=%async_computation | async-start | bytes 2359296 | tf_op jit(solution)/shard_map/all_to_all | solution.py:588
  42.5 2.6 %collective-permute-start.9 = (bf16[192,2048]{1,0:T(8,128)(2,1)}, bf16[192,2048]{1,0:T(8,128)(2,1)}, u32[]{:S(2)}, u32[]{:S(2)}) collective-permute-start(bf16[192,2048]{1,0:T(8,128)(2,1)} %collective-permute-done.6.refs_3_.refs_2_), channel_id=1, source_target_pairs={{0,6},{2,0},{4,2},{6,4},{1,7},{3,1},{5,3},{7,5},{8,14},{10,8},{12,... | collective-permute-start | bytes 2359304 | tf_op jit(solution)/shard_map/ppermute | solution.py:23
  45.1 17.2 %collective-permute-done.7.t0.refs_0_ = bf16[192,2048]{1,0:T(8,128)(2,1)S(1)} collective-permute-done((bf16[192,2048]{1,0:T(8,128)(2,1)}, bf16[192,2048]{1,0:T(8,128)(2,1)S(1)}, u32[]{:S(2)}, u32[]{:S(2)}) %collective-permute-start.7) | collective-permute-done | bytes 786464 | tf_op jit(solution)/shard_map/ppermute | solution.py:23
  62.3 10.7 %collective-permute-done.8.t1.refs_1_ = bf16[192,2048]{1,0:T(8,128)(2,1)} collective-permute-done((bf16[192,2048]{1,0:T(8,128)(2,1)}, bf16[192,2048]{1,0:T(8,128)(2,1)}, u32[]{:S(2)}, u32[]{:S(2)}) %collective-permute-start.8) | collective-permute-done | bytes 786464 | tf_op jit(solution)/shard_map/ppermute | solution.py:23
  73.0 2.1 thirds.1
  75.0 1.2 collective-permute-start.11
  76.2 2.7 %collective-permute-start.13 = (bf16[64,2048]{1,0:T(8,128)(2,1)}, bf16[64,2048]{1,0:T(8,128)(2,1)S(1)}, u32[]{:S(2)}, u32[]{:S(2)}) collective-permute-start(bf16[64,2048]{1,0:T(8,128)(2,1)} %get-tuple-element.74), channel_id=1, source_target_pairs={{0,6},{2,0},{4,2},{6,4},{1,7},{3,1},{5,3},{7,5},{8,14},{10,8},{12,... | collective-permute-start | bytes 786440 | tf_op jit(solution)/shard_map/ppermute | solution.py:23
  78.9 1.7 collective-permute-start
  82.3 4.1 %column_attention.2.refs_3_ = bf16[8,2,7,16,256]{4,3,2,1,0:T(8,128)(2,1)} custom-call(f32[1]{0:T(128)S(6)} %copy.32.refs_0_, f32[1]{0:T(128)} %collective-permute-done.refs_1_, bf16[48,16,768]{2,1,0:T(8,128)(2,1)} %bitcast.21), custom_call_target="tpu_custom_call" | custom-call | flops 452984832 | bytes 1572864 | tf_op jit(solution)/shard_map/column_attention/pallas_call | solution.py:345
  87.3 6.7 %project.3 = (bf16[4,2,6,16,768]{4,3,2,1,0:T(8,128)(2,1)}, bf16[4,2,16,512]{3,2,1,0:T(8,128)(2,1)}) custom-call(bf16[192,2048]{1,0:T(8,128)(2,1)} %copy-done.14, bf16[192,2048]{1,0:T(8,128)(2,1)} %collective-permute-done.8.t1.refs_1_, bf16[192,2048]{1,0:T(8,128)(2,1)} %collective-permute-done.9.t2.refs_2_, bf16[64,2048]{1,0:T(8,128)(2,1)} %copy-done.27, ...), custom_call_target="tpu_custom_call" | custom-call | flops 2415919104 | bytes 6291456 | tf_op jit(solution)/shard_map/project/pallas_call | solution.py:107
  94.2 6.8 %all-to-all-start.1 = ((bf16[8,96,768]{2,1,0:T(8,128)(2,1)}), bf16[8,96,768]{2,1,0:T(8,128)(2,1)S(1)}, u32[]{:S(2)}, u32[]{:S(2)}) async-start(bf16[8,96,768]{2,1,0:T(8,128)(2,1)} %bitcast.18), calls=%async_computation.1 | async-start | bytes 2359296 | tf_op jit(solution)/shard_map/all_to_all | solution.py:588
  101.9 11.6 %feed_forward.4 = (bf16[192,2176]{1,0:T(8,128)(2,1)}, bf16[192,2176]{1,0:T(8,128)(2,1)}, bf16[192,2176]{1,0:T(8,128)(2,1)}, bf16[192,2176]{1,0:T(8,128)(2,1)}) custom-call(bf16[192,2048]{1,0:T(8,128)(2,1)} %copy-done.14, bf16[192,2048]{1,0:T(8,128)(2,1)} %collective-permute-done.8.t1.refs_1_, bf16[192,2048]{1,0:T(8,128)(2,1)} %collective-permute-done.9.t2.refs_2_, ...), custom_call_target="tpu_custom_call" | custom-call | flops 6442450944 | bytes 14680064 | tf_op jit(solution)/shard_map/feed_forward/pallas_call | solution.py:210
  113.5 3.4 %all-to-all-done.1 = bf16[8,96,768]{2,1,0:T(8,128)(2,1)S(1)} async-done(((bf16[8,96,768]{2,1,0:T(8,128)(2,1)}), bf16[8,96,768]{2,1,0:T(8,128)(2,1)S(1)}, u32[]{:S(2)}, u32[]{:S(2)}) %all-to-all-start.1) | async-done | bytes 1179680 | tf_op jit(solution)/shard_map/all_to_all | solution.py:588
  116.9 1.1 copy-done.1
  118.0 4.1 %column_attention.3 = bf16[8,2,7,16,256]{4,3,2,1,0:T(8,128)(2,1)} custom-call(f32[1]{0:T(128)S(6)} %copy.32.refs_0_, f32[1]{0:T(128)} %collective-permute-done.refs_1_, bf16[48,16,768]{2,1,0:T(8,128)(2,1)} %bitcast.16, bf16[8,2,7,16,256]{4,3,2,1,0:T(8,128)(2,1)} %column_attention.2.refs_3_), custom_call_target="tpu_custom_call", output_to_operand_aliasing={{}: (3, {})} | custom-call | flops 452984832 | bytes 1572864 | tf_op jit(solution)/shard_map/column_attention/pallas_call | solution.py:345
  122.1 5.7 %all-to-all-start.2 = ((bf16[8,2,7,16,256]{4,3,2,1,0:T(8,128)(2,1)}), bf16[8,2,7,16,256]{4,3,2,1,0:T(8,128)(2,1)S(1)}, u32[]{:S(2)}, u32[]{:S(2)}) async-start(bf16[8,2,7,16,256]{4,3,2,1,0:T(8,128)(2,1)} %column_attention.3), calls=%async_computation.2 | async-start | bytes 1835008 | tf_op jit(solution)/shard_map/all_to_all | solution.py:612
  127.8 3.4 %collective-permute-start.15 = (bf16[4,2,16,512]{3,2,1,0:T(8,128)(2,1)S(1)}, bf16[4,2,16,512]{3,2,1,0:T(8,128)(2,1)S(1)}, u32[]{:S(2)}, u32[]{:S(2)}) collective-permute-start(bf16[4,2,16,512]{3,2,1,0:T(8,128)(2,1)S(1)} %copy-done.30), channel_id=1, source_target_pairs={{0,16},{16,32},{32,48},{48,64},{64,80},{80,96},{96,112},{1,17},{17... | collective-permute-start | bytes 393224 | tf_op jit(solution)/shard_map/ppermute | solution.py:44
  131.2 3.1 %collective-permute-start.16 = (bf16[4,2,16,512]{3,2,1,0:T(8,128)(2,1)}, bf16[4,2,16,512]{3,2,1,0:T(8,128)(2,1)S(1)}, u32[]{:S(2)}, u32[]{:S(2)}) collective-permute-start(bf16[4,2,16,512]{3,2,1,0:T(8,128)(2,1)} %get-tuple-element.95), channel_id=1, source_target_pairs={{0,16},{16,32},{32,48},{48,64},{64,80},{80,96},{96,112},{1,17},{17... | collective-permute-start | bytes 393224 | tf_op jit(solution)/shard_map/ppermute | solution.py:44
  134.3 5.7 %collective-permute-done.15.refs_9_ = bf16[4,2,16,512]{3,2,1,0:T(8,128)(2,1)S(1)} collective-permute-done((bf16[4,2,16,512]{3,2,1,0:T(8,128)(2,1)S(1)}, bf16[4,2,16,512]{3,2,1,0:T(8,128)(2,1)S(1)}, u32[]{:S(2)}, u32[]{:S(2)}) %collective-permute-start.15) | collective-permute-done | bytes 131104 | tf_op jit(solution)/shard_map/ppermute | solution.py:44
  140.0 2.4 collective-permute-start.17
  143.1 1.3 collective-permute-start.18
  146.7 9.4 %row_attention.1 = (bf16[4,2,6,16,256]{4,3,2,1,0:T(8,128)(2,1)}, bf16[4,2,6,16,256]{4,3,2,1,0:T(8,128)(2,1)}, f32[4,2,6,16,256]{4,3,2,1,0:T(8,128)}, f32[4,2,6,16,256]{4,3,2,1,0:T(8,128)}) custom-call(s32[1]{0:T(128)} %bitcast.6.refs_0_, s32[256,1]{1,0:T(8,128)} %add.135.refs_1_, s32[1,512]{1,0:T(1,128)} %bitcast.27, ...), custom_call_target="tpu_custom_call" | custom-call | flops 1610612736 | bytes 6291456 | tf_op jit(solution)/shard_map/row_attention/pallas_call | solution.py:283
  157.2 3.6 %terms.3 = (bf16[64,2176]{1,0:T(8,128)(2,1)}, bf16[64,2176]{1,0:T(8,128)(2,1)}, bf16[64,2176]{1,0:T(8,128)(2,1)}) custom-call(bf16[8,2,7,16,256]{4,3,2,1,0:T(8,128)(2,1)} %copy-done, bf16[4,2,6,16,256]{4,3,2,1,0:T(8,128)(2,1)} %get-tuple-element.102.refs_1_, f32[4,2,6,16,256]{4,3,2,1,0:T(8,128)} %get-tuple-element.103.refs_2_, ...), custom_call_target="tpu_custom_call" | custom-call | flops 213909504 | bytes 2088960 | tf_op jit(solution)/shard_map/terms/pallas_call | solution.py:400
  161.2 2.1 collective-permute-start.21
  163.3 5.0 %terms.4 = (bf16[192,2176]{1,0:T(8,128)(2,1)}, bf16[192,2176]{1,0:T(8,128)(2,1)}, bf16[192,2176]{1,0:T(8,128)(2,1)}) custom-call(bf16[8,2,7,16,256]{4,3,2,1,0:T(8,128)(2,1)} %copy-done, bf16[4,2,6,16,256]{4,3,2,1,0:T(8,128)(2,1)} %get-tuple-element.102.refs_1_, f32[4,2,6,16,256]{4,3,2,1,0:T(8,128)} %get-tuple-element.103.refs_2_, ...), custom_call_target="tpu_custom_call" | custom-call | flops 641728512 | bytes 6266880 | tf_op jit(solution)/shard_map/terms/pallas_call | solution.py:400
  169.3 3.0 %collective-permute-done.22.g2 = bf16[64,2176]{1,0:T(8,128)(2,1)S(1)} collective-permute-done((bf16[64,2176]{1,0:T(8,128)(2,1)}, bf16[64,2176]{1,0:T(8,128)(2,1)S(1)}, u32[]{:S(2)}, u32[]{:S(2)}) %collective-permute-start.22) | collective-permute-done | bytes 278560 | tf_op jit(solution)/shard_map/ppermute | solution.py:23
  173.0 2.3 add_far.1
  175.8 1.1 collective-permute-start.24
  176.9 1.1 collective-permute-start.25
  177.9 10.5 %feed_forward.5 = (bf16[192,2176]{1,0:T(8,128)(2,1)}, bf16[192,2176]{1,0:T(8,128)(2,1)}, bf16[192,2176]{1,0:T(8,128)(2,1)}) custom-call(bf16[192,2048]{1,0:T(8,128)(2,1)} %copy-done.26, bf16[192,2048]{1,0:T(8,128)(2,1)} %collective-permute-done.5.refs_2_.refs_1_, bf16[192,2048]{1,0:T(8,128)(2,1)} %collective-permute-done.6.refs_3_.refs_2_, ...), custom_call_target="tpu_custom_call" | custom-call | flops 4831838208 | bytes 13107200 | tf_op jit(solution)/shard_map/feed_forward/pallas_call | solution.py:210
  188.4 5.8 %terms.5 = (bf16[192,2176]{1,0:T(8,128)(2,1)}, bf16[192,2176]{1,0:T(8,128)(2,1)}, bf16[192,2176]{1,0:T(8,128)(2,1)}, bf16[192,2176]{1,0:T(8,128)(2,1)}) custom-call(bf16[8,2,7,16,256]{4,3,2,1,0:T(8,128)(2,1)} %copy-done, bf16[4,2,6,16,256]{4,3,2,1,0:T(8,128)(2,1)} %get-tuple-element.96.refs_1_, f32[4,2,6,16,256]{4,3,2,1,0:T(8,128)} %get-tuple-element.97.refs_2_, ...), custom_call_target="tpu_custom_call" | custom-call | flops 855638016 | bytes 8355840 | tf_op jit(solution)/shard_map/terms/pallas_call | solution.py:400
  194.7 2.0 collective-permute-done.25.r2
  197.7 4.1 %add_near.1 = (bf16[192,2176]{1,0:T(8,128)(2,1)}, bf16[192,2176]{1,0:T(8,128)(2,1)}) custom-call(bf16[192,2176]{1,0:T(8,128)(2,1)} %get-tuple-element.117.t0, bf16[192,2176]{1,0:T(8,128)(2,1)} %get-tuple-element.118.t1, bf16[192,2176]{1,0:T(8,128)(2,1)} %copy-done.11, bf16[192,2176]{1,0:T(8,128)(2,1)} %copy-done.12, bf16[192,2176]{1,0:T(8,128)(2,1)} %copy-done.13), custom_call_target="tpu_custom_call" | custom-call | flops 1253376 | bytes 5849088 | tf_op jit(solution)/shard_map/add_near/pallas_call | solution.py:460
  203.5 11.1 %collective-permute-done.27.m1 = bf16[192,2176]{1,0:T(8,128)(2,1)S(1)} collective-permute-done((bf16[192,2176]{1,0:T(8,128)(2,1)}, bf16[192,2176]{1,0:T(8,128)(2,1)S(1)}, u32[]{:S(2)}, u32[]{:S(2)}) %collective-permute-start.27) | collective-permute-done | bytes 835616 | tf_op jit(solution)/shard_map/ppermute | solution.py:23
  214.7 4.2 %collective-permute-done.26.m0 = bf16[192,2176]{1,0:T(8,128)(2,1)S(1)} collective-permute-done((bf16[192,2176]{1,0:T(8,128)(2,1)}, bf16[192,2176]{1,0:T(8,128)(2,1)S(1)}, u32[]{:S(2)}, u32[]{:S(2)}) %collective-permute-start.26) | collective-permute-done | bytes 835616 | tf_op jit(solution)/shard_map/ppermute | solution.py:23
  220.8 5.7 %head.1 = (bf16[192,2048]{1,0:T(8,128)(2,1)}, f32[128,1,256]{2,1,0:T(1,128)}) custom-call(bf16[192,2048]{1,0:T(8,128)(2,1)} %bitcast.20, bf16[192,2176]{1,0:T(8,128)(2,1)} %get-tuple-element.116.mine, bf16[192,2176]{1,0:T(8,128)(2,1)} %copy-done.9, bf16[192,2176]{1,0:T(8,128)(2,1)} %copy-done.8, bf16[192,2176]{1,0:T(8,128)(2,1)} %copy-done.10, ...), custom_call_target="tpu_custom_call" | custom-call | tf_op jit(solution)/shard_map/head/pallas_call | solution.py:499
  226.5 12.3 %all-to-all-start.3 = ((f32[128,1,256]{2,1,0:T(1,128)}), f32[128,1,256]{2,1,0:T(1,128)S(1)}, u32[]{:S(2)}, u32[]{:S(2)}) async-start(f32[128,1,256]{2,1,0:T(1,128)} %get-tuple-element.125), calls=%async_computation.3 | async-start | bytes 262144 | tf_op jit(solution)/shard_map/all_to_all | solution.py:667
  239.5 9.6 %all-to-all-done.3 = f32[128,1,256]{2,1,0:T(1,128)S(1)} async-done(((f32[128,1,256]{2,1,0:T(1,128)}), f32[128,1,256]{2,1,0:T(1,128)S(1)}, u32[]{:S(2)}, u32[]{:S(2)}) %all-to-all-start.3) | async-done | bytes 131104 | tf_op jit(solution)/shard_map/all_to_all | solution.py:667
  249.7 2.1 pick.1
  (108 shorter events, 18.0 us)
Async XLA Ops:
  0.6 8.2 %collective-permute-start.1 = (bf16[2048,512]{1,0:T(8,128)(2,1)}, bf16[2048,512]{1,0:T(8,128)(2,1)S(1)}, u32[]{:S(2)}, u32[]{:S(2)}) collective-permute-start(bf16[2048,512]{1,0:T(8,128)(2,1)} %refs_3_.3), channel_id=1, source_target_pairs={{0,1},{1,0},{2,3},{3,2},{4,5},{5,4},{6,7},{7,6},{8,9},{9,8},{10,11... | collective-permute-start | bytes 6291464 | tf_op jit(solution)/shard_map/ppermute | solution.py:23
  2.1 7.9 %collective-permute-start.2 = (bf16[512,2048]{1,0:T(8,128)(2,1)}, bf16[512,2048]{1,0:T(8,128)(2,1)}, u32[]{:S(2)}, u32[]{:S(2)}) collective-permute-start(bf16[512,2048]{1,0:T(8,128)(2,1)} %refs_5_.1), channel_id=1, source_target_pairs={{0,1},{1,0},{2,3},{3,2},{4,5},{5,4},{6,7},{7,6},{8,9},{9,8},{10,11... | collective-permute-start | bytes 6291464 | tf_op jit(solution)/shard_map/ppermute | solution.py:23
  2.2 25.7 %collective-permute-start.3 = (bf16[3,2048,128]{2,1,0:T(8,128)(2,1)}, bf16[3,2048,128]{2,1,0:T(8,128)(2,1)}, u32[]{:S(2)}, u32[]{:S(2)}) collective-permute-start(bf16[3,2048,128]{2,1,0:T(8,128)(2,1)} %refs_6_.3), channel_id=1, source_target_pairs={{0,1},{1,0},{2,3},{3,2},{4,5},{5,4},{6,7},{7,6},{8,9},{9,8},{10,11... | collective-permute-start | bytes 4718600 | tf_op jit(solution)/shard_map/ppermute | solution.py:23
  4.9 21.9 %collective-permute-start.4 = (bf16[192,2048]{1,0:T(8,128)(2,1)}, bf16[192,2048]{1,0:T(8,128)(2,1)S(1)}, u32[]{:S(2)}, u32[]{:S(2)}) collective-permute-start(bf16[192,2048]{1,0:T(8,128)(2,1)} %normalize.1.refs_0_), channel_id=1, source_target_pairs={{0,2},{2,4},{4,6},{6,0},{1,3},{3,5},{5,7},{7,1},{8,10},{10,12},{12... | collective-permute-start | bytes 2359304 | tf_op jit(solution)/shard_map/ppermute | solution.py:23
  6.7 20.2 %collective-permute-start.5 = (bf16[192,2048]{1,0:T(8,128)(2,1)}, bf16[192,2048]{1,0:T(8,128)(2,1)}, u32[]{:S(2)}, u32[]{:S(2)}) collective-permute-start(bf16[192,2048]{1,0:T(8,128)(2,1)} %normalize.1.refs_0_), channel_id=1, source_target_pairs={{0,6},{2,0},{4,2},{6,4},{1,7},{3,1},{5,3},{7,5},{8,14},{10,8},{12,... | collective-permute-start | bytes 2359304 | tf_op jit(solution)/shard_map/ppermute | solution.py:23
  8.8 19.0 %collective-permute-start.6 = (bf16[192,2048]{1,0:T(8,128)(2,1)}, bf16[192,2048]{1,0:T(8,128)(2,1)}, u32[]{:S(2)}, u32[]{:S(2)}) collective-permute-start(bf16[192,2048]{1,0:T(8,128)(2,1)} %normalize.1.refs_0_), channel_id=1, source_target_pairs={{0,8},{8,0},{1,9},{9,1},{2,10},{10,2},{3,11},{11,3},{4,12},{12,4},... | collective-permute-start | bytes 2359304 | tf_op jit(solution)/shard_map/ppermute | solution.py:23
  34.2 52.2 %collective-permute-start.10 = (bf16[4,2,6,16,768]{4,3,2,1,0:T(8,128)(2,1)}, bf16[4,2,6,16,768]{4,3,2,1,0:T(8,128)(2,1)S(1)}, u32[]{:S(2)}, u32[]{:S(2)}) collective-permute-start(bf16[4,2,6,16,768]{4,3,2,1,0:T(8,128)(2,1)} %get-tuple-element.67.refs_3_), channel_id=1, source_target_pairs={{0,1},{1,0},{2,3},{3,2},{4,5},{5,4},{6,7},{7,6},{8,9},{9,8},{10,11... | collective-permute-start | bytes 3538952 | tf_op jit(solution)/shard_map/ppermute | solution.py:23
  35.4 45.8 %all-to-all-start = ((bf16[8,96,768]{2,1,0:T(8,128)(2,1)}), bf16[8,96,768]{2,1,0:T(8,128)(2,1)S(1)}, u32[]{:S(2)}, u32[]{:S(2)}) async-start(bf16[8,96,768]{2,1,0:T(8,128)(2,1)} %bitcast.17), calls=%async_computation | async-start | bytes 2359296 | tf_op jit(solution)/shard_map/all_to_all | solution.py:588
  42.1 20.2 %collective-permute-start.7 = (bf16[192,2048]{1,0:T(8,128)(2,1)}, bf16[192,2048]{1,0:T(8,128)(2,1)S(1)}, u32[]{:S(2)}, u32[]{:S(2)}) collective-permute-start(bf16[192,2048]{1,0:T(8,128)(2,1)} %copy-done.26), channel_id=1, source_target_pairs={{0,2},{2,4},{4,6},{6,0},{1,3},{3,5},{5,7},{7,1},{8,10},{10,12},{12... | collective-permute-start | bytes 2359304 | tf_op jit(solution)/shard_map/ppermute | solution.py:23
  42.1 30.9 %collective-permute-start.8 = (bf16[192,2048]{1,0:T(8,128)(2,1)}, bf16[192,2048]{1,0:T(8,128)(2,1)}, u32[]{:S(2)}, u32[]{:S(2)}) collective-permute-start(bf16[192,2048]{1,0:T(8,128)(2,1)} %copy-done.26), channel_id=1, source_target_pairs={{0,8},{8,0},{1,9},{9,1},{2,10},{10,2},{3,11},{11,3},{4,12},{12,4},... | collective-permute-start | bytes 2359304 | tf_op jit(solution)/shard_map/ppermute | solution.py:23
  42.5 30.5 %collective-permute-start.9 = (bf16[192,2048]{1,0:T(8,128)(2,1)}, bf16[192,2048]{1,0:T(8,128)(2,1)}, u32[]{:S(2)}, u32[]{:S(2)}) collective-permute-start(bf16[192,2048]{1,0:T(8,128)(2,1)} %collective-permute-done.6.refs_3_.refs_2_), channel_id=1, source_target_pairs={{0,6},{2,0},{4,2},{6,4},{1,7},{3,1},{5,3},{7,5},{8,14},{10,8},{12,... | collective-permute-start | bytes 2359304 | tf_op jit(solution)/shard_map/ppermute | solution.py:23
  62.3 10.7 %copy-start.14 = (bf16[192,2048]{1,0:T(8,128)(2,1)}, bf16[192,2048]{1,0:T(8,128)(2,1)S(1)}, u32[]{:S(2)}) copy-start(bf16[192,2048]{1,0:T(8,128)(2,1)S(1)} %collective-permute-done.7.t0.refs_0_) | copy-start | bytes 2359300
  75.0 11.4 %collective-permute-start.11 = (bf16[64,2048]{1,0:T(8,128)(2,1)}, bf16[64,2048]{1,0:T(8,128)(2,1)S(1)}, u32[]{:S(2)}, u32[]{:S(2)}) collective-permute-start(bf16[64,2048]{1,0:T(8,128)(2,1)} %get-tuple-element.72), channel_id=1, source_target_pairs={{0,8},{8,0},{1,9},{9,1},{2,10},{10,2},{3,11},{11,3},{4,12},{12,4},... | collective-permute-start | bytes 786440 | tf_op jit(solution)/shard_map/ppermute | solution.py:23
  76.2 10.2 %collective-permute-start.12 = (bf16[64,2048]{1,0:T(8,128)(2,1)}, bf16[64,2048]{1,0:T(8,128)(2,1)S(1)}, u32[]{:S(2)}, u32[]{:S(2)}) collective-permute-start(bf16[64,2048]{1,0:T(8,128)(2,1)} %get-tuple-element.73), channel_id=1, source_target_pairs={{0,2},{2,4},{4,6},{6,0},{1,3},{3,5},{5,7},{7,1},{8,10},{10,12},{12... | collective-permute-start | bytes 786440 | tf_op jit(solution)/shard_map/ppermute | solution.py:23
  76.2 10.2 %collective-permute-start.13 = (bf16[64,2048]{1,0:T(8,128)(2,1)}, bf16[64,2048]{1,0:T(8,128)(2,1)S(1)}, u32[]{:S(2)}, u32[]{:S(2)}) collective-permute-start(bf16[64,2048]{1,0:T(8,128)(2,1)} %get-tuple-element.74), channel_id=1, source_target_pairs={{0,6},{2,0},{4,2},{6,4},{1,7},{3,1},{5,3},{7,5},{8,14},{10,8},{12,... | collective-permute-start | bytes 786440 | tf_op jit(solution)/shard_map/ppermute | solution.py:23
  78.9 2.8 %collective-permute-start = (f32[1]{0:T(128)}, f32[1]{0:T(128)}, u32[]{:S(2)}, u32[]{:S(2)}) collective-permute-start(f32[1]{0:T(128)} %param.21), channel_id=1, source_target_pairs={{0,1},{1,0},{2,3},{3,2},{4,5},{5,4},{6,7},{7,6},{8,9},{9,8},{10,11... | collective-permute-start | bytes 20 | tf_op jit(solution)/shard_map/ppermute | solution.py:23
  87.3 6.7 %copy-start.4 = (bf16[4,2,6,16,768]{4,3,2,1,0:T(8,128)(2,1)}, bf16[4,2,6,16,768]{4,3,2,1,0:T(8,128)(2,1)S(1)}, u32[]{:S(2)}) copy-start(bf16[4,2,6,16,768]{4,3,2,1,0:T(8,128)(2,1)S(1)} %collective-permute-done.10.refs_5_.refs_6_) | copy-start | bytes 3538948
  94.0 6.9 %copy-start.2 = (bf16[128,2048]{1,0:T(8,128)(2,1)S(1)}, bf16[128,2048]{1,0:T(8,128)(2,1)}, u32[]{:S(2)}) copy-start(bf16[128,2048]{1,0:T(8,128)(2,1)} %refs_7_.1) | copy-start | bytes 1572868
  94.0 7.8 %copy-start.24 = (s32[8]{0:T(128)S(1)}, s32[8]{0:T(128)}, u32[]{:S(2)}) copy-start(s32[8]{0:T(128)} %constant.117.clone) | copy-start | bytes 100
  94.0 7.8 %copy-start.25 = (s32[8]{0:T(128)S(1)}, s32[8]{0:T(128)}, u32[]{:S(2)}) copy-start(s32[8]{0:T(128)} %constant.118.clone) | copy-start | bytes 100
  94.1 22.8 %collective-permute-start.14 = (bf16[4,2,6,16,768]{4,3,2,1,0:T(8,128)(2,1)}, bf16[4,2,6,16,768]{4,3,2,1,0:T(8,128)(2,1)S(1)}, u32[]{:S(2)}, u32[]{:S(2)}) collective-permute-start(bf16[4,2,6,16,768]{4,3,2,1,0:T(8,128)(2,1)} %get-tuple-element.81.refs_4_), channel_id=1, source_target_pairs={{0,1},{1,0},{2,3},{3,2},{4,5},{5,4},{6,7},{7,6},{8,9},{9,8},{10,11... | collective-permute-start | bytes 3538952 | tf_op jit(solution)/shard_map/ppermute | solution.py:23
  94.2 22.8 %all-to-all-start.1 = ((bf16[8,96,768]{2,1,0:T(8,128)(2,1)}), bf16[8,96,768]{2,1,0:T(8,128)(2,1)S(1)}, u32[]{:S(2)}, u32[]{:S(2)}) async-start(bf16[8,96,768]{2,1,0:T(8,128)(2,1)} %bitcast.18), calls=%async_computation.1 | async-start | bytes 2359296 | tf_op jit(solution)/shard_map/all_to_all | solution.py:588
  100.9 55.2 %collective-permute-start.19 = (bf16[128,2048]{1,0:T(8,128)(2,1)S(1)}, bf16[128,2048]{1,0:T(8,128)(2,1)S(1)}, u32[]{:S(2)}, u32[]{:S(2)}) collective-permute-start(bf16[128,2048]{1,0:T(8,128)(2,1)S(1)} %copy-done.2), channel_id=1, source_target_pairs={{0,1},{1,0},{2,3},{3,2},{4,5},{5,4},{6,7},{7,6},{8,9},{9,8},{10,11... | collective-permute-start | bytes 1572872 | tf_op jit(solution)/shard_map/ppermute | solution.py:23
  116.9 5.2 %copy-start.5 = (bf16[4,2,6,16,768]{4,3,2,1,0:T(8,128)(2,1)}, bf16[4,2,6,16,768]{4,3,2,1,0:T(8,128)(2,1)S(1)}, u32[]{:S(2)}) copy-start(bf16[4,2,6,16,768]{4,3,2,1,0:T(8,128)(2,1)S(1)} %collective-permute-done.14.refs_7_.refs_8_) | copy-start | bytes 3538948
  122.1 5.7 %copy-start.30 = (bf16[4,2,16,512]{3,2,1,0:T(8,128)(2,1)S(1)}, bf16[4,2,16,512]{3,2,1,0:T(8,128)(2,1)}, u32[]{:S(2)}) copy-start(bf16[4,2,16,512]{3,2,1,0:T(8,128)(2,1)} %get-tuple-element.94) | copy-start | bytes 393220
  122.1 34.1 %all-to-all-start.2 = ((bf16[8,2,7,16,256]{4,3,2,1,0:T(8,128)(2,1)}), bf16[8,2,7,16,256]{4,3,2,1,0:T(8,128)(2,1)S(1)}, u32[]{:S(2)}, u32[]{:S(2)}) async-start(bf16[8,2,7,16,256]{4,3,2,1,0:T(8,128)(2,1)} %column_attention.3), calls=%async_computation.2 | async-start | bytes 1835008 | tf_op jit(solution)/shard_map/all_to_all | solution.py:612
  127.8 12.2 %collective-permute-start.15 = (bf16[4,2,16,512]{3,2,1,0:T(8,128)(2,1)S(1)}, bf16[4,2,16,512]{3,2,1,0:T(8,128)(2,1)S(1)}, u32[]{:S(2)}, u32[]{:S(2)}) collective-permute-start(bf16[4,2,16,512]{3,2,1,0:T(8,128)(2,1)S(1)} %copy-done.30), channel_id=1, source_target_pairs={{0,16},{16,32},{32,48},{48,64},{64,80},{80,96},{96,112},{1,17},{17... | collective-permute-start | bytes 393224 | tf_op jit(solution)/shard_map/ppermute | solution.py:44
  131.2 11.9 %collective-permute-start.16 = (bf16[4,2,16,512]{3,2,1,0:T(8,128)(2,1)}, bf16[4,2,16,512]{3,2,1,0:T(8,128)(2,1)S(1)}, u32[]{:S(2)}, u32[]{:S(2)}) collective-permute-start(bf16[4,2,16,512]{3,2,1,0:T(8,128)(2,1)} %get-tuple-element.95), channel_id=1, source_target_pairs={{0,16},{16,32},{32,48},{48,64},{64,80},{80,96},{96,112},{1,17},{17... | collective-permute-start | bytes 393224 | tf_op jit(solution)/shard_map/ppermute | solution.py:44
  140.0 6.0 %copy-start.18 = (bf16[4,2,16,512]{3,2,1,0:T(8,128)(2,1)}, bf16[4,2,16,512]{3,2,1,0:T(8,128)(2,1)S(1)}, u32[]{:S(2)}) copy-start(bf16[4,2,16,512]{3,2,1,0:T(8,128)(2,1)S(1)} %collective-permute-done.15.refs_9_) | copy-start | bytes 393220
  140.0 6.0 %collective-permute-start.17 = (bf16[4,2,16,512]{3,2,1,0:T(8,128)(2,1)S(1)}, bf16[4,2,16,512]{3,2,1,0:T(8,128)(2,1)S(1)}, u32[]{:S(2)}, u32[]{:S(2)}) collective-permute-start(bf16[4,2,16,512]{3,2,1,0:T(8,128)(2,1)S(1)} %collective-permute-done.15.refs_9_), channel_id=1, source_target_pairs={{0,1},{1,0},{2,3},{3,2},{4,5},{5,4},{6,7},{7,6},{8,9},{9,8},{10,11... | collective-permute-start | bytes 393224 | tf_op jit(solution)/shard_map/ppermute | solution.py:23
  143.1 3.0 %copy-start.19 = (bf16[4,2,16,512]{3,2,1,0:T(8,128)(2,1)}, bf16[4,2,16,512]{3,2,1,0:T(8,128)(2,1)S(1)}, u32[]{:S(2)}) copy-start(bf16[4,2,16,512]{3,2,1,0:T(8,128)(2,1)S(1)} %collective-permute-done.16.refs_10_) | copy-start | bytes 393220
  143.1 3.0 %collective-permute-start.18 = (bf16[4,2,16,512]{3,2,1,0:T(8,128)(2,1)S(1)}, bf16[4,2,16,512]{3,2,1,0:T(8,128)(2,1)S(1)}, u32[]{:S(2)}, u32[]{:S(2)}) collective-permute-start(bf16[4,2,16,512]{3,2,1,0:T(8,128)(2,1)S(1)} %collective-permute-done.16.refs_10_), channel_id=1, source_target_pairs={{0,1},{1,0},{2,3},{3,2},{4,5},{5,4},{6,7},{7,6},{8,9},{9,8},{10,11... | collective-permute-start | bytes 393224 | tf_op jit(solution)/shard_map/ppermute | solution.py:23
  160.8 8.4 %collective-permute-start.20 = (bf16[64,2176]{1,0:T(8,128)(2,1)}, bf16[64,2176]{1,0:T(8,128)(2,1)S(1)}, u32[]{:S(2)}, u32[]{:S(2)}) collective-permute-start(bf16[64,2176]{1,0:T(8,128)(2,1)} %get-tuple-element.100), channel_id=1, source_target_pairs={{0,8},{8,0},{1,9},{9,1},{2,10},{10,2},{3,11},{11,3},{4,12},{12,4},... | collective-permute-start | bytes 835592 | tf_op jit(solution)/shard_map/ppermute | solution.py:23
  161.2 8.1 %collective-permute-start.21 = (bf16[64,2176]{1,0:T(8,128)(2,1)}, bf16[64,2176]{1,0:T(8,128)(2,1)S(1)}, u32[]{:S(2)}, u32[]{:S(2)}) collective-permute-start(bf16[64,2176]{1,0:T(8,128)(2,1)} %get-tuple-element.107), channel_id=1, source_target_pairs={{0,6},{2,0},{4,2},{6,4},{1,7},{3,1},{5,3},{7,5},{8,14},{10,8},{12,... | collective-permute-start | bytes 835592 | tf_op jit(solution)/shard_map/ppermute | solution.py:23
  163.3 9.1 %collective-permute-start.22 = (bf16[64,2176]{1,0:T(8,128)(2,1)}, bf16[64,2176]{1,0:T(8,128)(2,1)S(1)}, u32[]{:S(2)}, u32[]{:S(2)}) collective-permute-start(bf16[64,2176]{1,0:T(8,128)(2,1)} %get-tuple-element.108), channel_id=1, source_target_pairs={{0,2},{2,4},{4,6},{6,0},{1,3},{3,5},{5,7},{7,1},{8,10},{10,12},{12... | collective-permute-start | bytes 835592 | tf_op jit(solution)/shard_map/ppermute | solution.py:23
  169.2 3.1 %copy-start.15 = (bf16[64,2176]{1,0:T(8,128)(2,1)}, bf16[64,2176]{1,0:T(8,128)(2,1)S(1)}, u32[]{:S(2)}) copy-start(bf16[64,2176]{1,0:T(8,128)(2,1)S(1)} %collective-permute-done.20.g0) | copy-start | bytes 835588
  169.3 3.0 %copy-start.16 = (bf16[64,2176]{1,0:T(8,128)(2,1)}, bf16[64,2176]{1,0:T(8,128)(2,1)S(1)}, u32[]{:S(2)}) copy-start(bf16[64,2176]{1,0:T(8,128)(2,1)S(1)} %collective-permute-done.21.g1) | copy-start | bytes 835588
  175.4 18.9 %collective-permute-start.23 = (bf16[192,2176]{1,0:T(8,128)(2,1)}, bf16[192,2176]{1,0:T(8,128)(2,1)S(1)}, u32[]{:S(2)}, u32[]{:S(2)}) collective-permute-start(bf16[192,2176]{1,0:T(8,128)(2,1)} %get-tuple-element.119), channel_id=1, source_target_pairs={{0,6},{2,0},{4,2},{6,4},{1,7},{3,1},{5,3},{7,5},{8,14},{10,8},{12,... | collective-permute-start | bytes 2506760 | tf_op jit(solution)/shard_map/ppermute | solution.py:23
  175.8 18.9 %collective-permute-start.24 = (bf16[192,2176]{1,0:T(8,128)(2,1)}, bf16[192,2176]{1,0:T(8,128)(2,1)S(1)}, u32[]{:S(2)}, u32[]{:S(2)}) collective-permute-start(bf16[192,2176]{1,0:T(8,128)(2,1)} %get-tuple-element.120), channel_id=1, source_target_pairs={{0,8},{8,0},{1,9},{9,1},{2,10},{10,2},{3,11},{11,3},{4,12},{12,4},... | collective-permute-start | bytes 2506760 | tf_op jit(solution)/shard_map/ppermute | solution.py:23
  176.9 19.9 %collective-permute-start.25 = (bf16[192,2176]{1,0:T(8,128)(2,1)}, bf16[192,2176]{1,0:T(8,128)(2,1)S(1)}, u32[]{:S(2)}, u32[]{:S(2)}) collective-permute-start(bf16[192,2176]{1,0:T(8,128)(2,1)} %get-tuple-element.109), channel_id=1, source_target_pairs={{0,2},{2,4},{4,6},{6,0},{1,3},{3,5},{5,7},{7,1},{8,10},{10,12},{12... | collective-permute-start | bytes 2506760 | tf_op jit(solution)/shard_map/ppermute | solution.py:23
  194.2 20.5 %collective-permute-start.27 = (bf16[192,2176]{1,0:T(8,128)(2,1)}, bf16[192,2176]{1,0:T(8,128)(2,1)S(1)}, u32[]{:S(2)}, u32[]{:S(2)}) collective-permute-start(bf16[192,2176]{1,0:T(8,128)(2,1)} %get-tuple-element.122), channel_id=1, source_target_pairs={{0,2},{2,4},{4,6},{6,0},{1,3},{3,5},{5,7},{7,1},{8,10},{10,12},{12... | collective-permute-start | bytes 2506760 | tf_op jit(solution)/shard_map/ppermute | solution.py:23
  194.3 2.4 copy-start.11
  197.7 5.1 %copy-start.22 = (s32[6,32]{1,0:T(8,128)S(1)}, s32[6,32]{1,0:T(8,128)}, u32[]{:S(2)}) copy-start(s32[6,32]{1,0:T(8,128)} %param.14) | copy-start | bytes 2308
  201.7 17.2 %collective-permute-start.26 = (bf16[192,2176]{1,0:T(8,128)(2,1)}, bf16[192,2176]{1,0:T(8,128)(2,1)S(1)}, u32[]{:S(2)}, u32[]{:S(2)}) collective-permute-start(bf16[192,2176]{1,0:T(8,128)(2,1)} %get-tuple-element.121), channel_id=1, source_target_pairs={{0,6},{2,0},{4,2},{6,4},{1,7},{3,1},{5,3},{7,5},{8,14},{10,8},{12,... | collective-permute-start | bytes 2506760 | tf_op jit(solution)/shard_map/ppermute | solution.py:23
  202.4 17.6 %collective-permute-start.28 = (bf16[192,2176]{1,0:T(8,128)(2,1)}, bf16[192,2176]{1,0:T(8,128)(2,1)S(1)}, u32[]{:S(2)}, u32[]{:S(2)}) collective-permute-start(bf16[192,2176]{1,0:T(8,128)(2,1)} %get-tuple-element.123), channel_id=1, source_target_pairs={{0,8},{8,0},{1,9},{9,1},{2,10},{10,2},{3,11},{11,3},{4,12},{12,4},... | collective-permute-start | bytes 2506760 | tf_op jit(solution)/shard_map/ppermute | solution.py:23
  214.7 5.2 %copy-start.8 = (bf16[192,2176]{1,0:T(8,128)(2,1)}, bf16[192,2176]{1,0:T(8,128)(2,1)S(1)}, u32[]{:S(2)}) copy-start(bf16[192,2176]{1,0:T(8,128)(2,1)S(1)} %collective-permute-done.27.m1) | copy-start | bytes 2506756
  220.8 18.0 %copy-start.23 = (s32[1024]{0:T(1024)S(1)}, s32[1024]{0:T(1024)}, u32[]{:S(2)}) copy-start(s32[1024]{0:T(1024)} %param.15) | copy-start | bytes 12292
  226.5 22.5 %all-to-all-start.3 = ((f32[128,1,256]{2,1,0:T(1,128)}), f32[128,1,256]{2,1,0:T(1,128)S(1)}, u32[]{:S(2)}, u32[]{:S(2)}) async-start(f32[128,1,256]{2,1,0:T(1,128)} %get-tuple-element.125), calls=%async_computation.3 | async-start | bytes 262144 | tf_op jit(solution)/shard_map/all_to_all | solution.py:667
  (16 other events, 15.5 us)

commit v3 on v2

--- a/solution.py
+++ b/solution.py
@@ -58,6 +58,7 @@
 
 VMEM = pl.BlockSpec(memory_space=pltpu.VMEM)
 SMEM = pl.BlockSpec(memory_space=pltpu.SMEM)
+ANY = pl.BlockSpec(memory_space=pl.ANY)
 HALF = 16
 
 
@@ -119,9 +120,6 @@
         cost_estimate=cost(2 * total * width * 6 * hs, 2 * total * width + 12 * width * hs),
         name="project",
     )(*shards, mine, theirs)
-
-
-ANY = pl.BlockSpec(memory_space=pl.ANY)
 
 
 def forward_body(n, slots, unrolled, *refs):
@@ -357,17 +355,15 @@
     )(*bias, x, *earlier)
 
 
-def term_body(hs, rows, group, base, splits, got, acc, den, *refs):
+def term_body(hs, rows, splits, got, acc, den, *refs):
     count = len({slot for slot, _, _ in splits})
     ffs, (w_mine, w_their), outs = refs[:count], refs[count : count + 2], refs[count + 2 :]
     spots = 2 * count * rows * HALF
     lines = 2 * count * HALF
-    pairs = slice(2 * base, 2 * (base + count))
-    slots = slice(base, base + count)
     unit = lax.broadcasted_iota(jnp.int32, (spots, lines), 0) // HALF
     line = lax.broadcasted_iota(jnp.int32, (spots, lines), 1)
     hit = jnp.logical_and(unit == (line // HALF) * rows + line % HALF, line % HALF < rows)
-    table = got[pairs, group, rows, :, 0:128].reshape(lines, 128)
+    table = got[:, 0, rows, :, 0:128].reshape(lines, 128)
     table = dot(jnp.where(hit, 1.0, 0.0).astype(BF16), table)
     lane = lax.broadcasted_iota(jnp.int32, (spots, 128), 1)
     spot = lax.broadcasted_iota(jnp.int32, (spots, 128), 0) % HALF
@@ -376,9 +372,9 @@
     for h in range(2):
         at = slice(h * hs, (h + 1) * hs)
         col_den = dot(jnp.where(lane == spot + HALF * h, table, 0.0).astype(BF16), ones)
-        total = acc[slots, :, :, :, at].reshape(spots, hs).astype(F32)
-        total = total + got[pairs, group, 0:rows, :, at].reshape(spots, hs).astype(F32)
-        parts.append((total / (den[slots, :, :, :, at].reshape(spots, hs) + col_den)).astype(BF16))
+        total = acc[:, :, :, :, at].reshape(spots, hs).astype(F32)
+        total = total + got[:, 0, 0:rows, :, at].reshape(spots, hs).astype(F32)
+        parts.append((total / (den[:, :, :, :, at].reshape(spots, hs) + col_den)).astype(BF16))
     halves = jnp.concatenate(parts, axis=1).reshape(count, 2, rows, HALF, 2 * hs)
     blocks = [halves[s, g, r] for s in range(count) for r in range(rows) for g in range(2)]
     attended = jnp.concatenate(blocks, axis=0)
@@ -397,12 +393,23 @@
 
 def terms(group, base, got, acc, den, ff, w_mine, w_their, hs, rows, splits):
     tokens, full = ff[0].shape
-    return pl.pallas_call(
-        lambda *refs: term_body(hs, rows, group, base, splits, *refs),
-        in_specs=[VMEM] * (5 + len(ff)),
-        out_specs=[VMEM] * len(splits),
+    count = len(ff)
+    whole = lambda a: pl.BlockSpec(a.shape, lambda i: (0,) * a.ndim)
+    local = pl.BlockSpec((count, 2, rows, HALF, 2 * hs), lambda i: (base // count, 0, 0, 0, 0))
+    return pl.pallas_call(
+        lambda *refs: term_body(hs, rows, splits, *refs),
+        grid=(1,),
+        in_specs=[
+            pl.BlockSpec(
+                (2 * count, 1, rows + 1, HALF, 2 * hs), lambda i: (base // count, group, 0, 0, 0)
+            ),
+            local,
+            local,
+        ]
+        + [whole(a) for a in (*ff, w_mine, w_their)],
+        out_specs=[pl.BlockSpec((b - a, full), lambda i: (0, 0)) for _, a, b in splits],
         out_shape=[jax.ShapeDtypeStruct((b - a, full), BF16) for _, a, b in splits],
-        cost_estimate=cost(4 * len(ff) * tokens * hs * full, 5 * len(ff) * tokens * full),
+        cost_estimate=cost(4 * count * tokens * hs * full, 5 * count * tokens * full),
         name="terms",
     )(got, acc, den, *ff, w_mine, w_their)
 
@@ -456,12 +463,10 @@
 
 def add_near(*arrays):
     rows, width = arrays[0].shape
-    block = pl.BlockSpec((rows // 3, width), lambda i: (i, 0))
     return pl.pallas_call(
         near_body,
-        grid=(3,),
-        in_specs=[block] * 5,
-        out_specs=[block] * 2,
+        in_specs=[VMEM] * 5,
+        out_specs=[VMEM] * 2,
         out_shape=[jax.ShapeDtypeStruct((rows, width), BF16)] * 2,
         cost_estimate=cost(3 * rows * width, 14 * rows * width),
         name="add_near",
@@ -601,13 +606,13 @@
     s_aa, s_pa, s_pb = after(qkv0, (s_aa, s_pa, s_pb))
     h_aa, h_pa, h_pb = thirds_of((s_aa, s_pa, s_pb))
     far = (swap_x(h_aa), up_z(h_pa), down_z(h_pb))
-    back = attend_columns(0, after((s_aa, s_pa, s_pb), got0))
-    away = after((back, their_qkv0), (s_aa, s_pa, s_pb, *far))
+    away = after(their_qkv0, (s_aa, s_pa, s_pb, *far))
     qkv1, edge1, got1 = columns(away)
+    back = attend_columns(0, after(qkv1, got0))
     their_qkv1 = swap_core(qkv1)
     edge1 = next_row(edge1)
     their_edge1 = swap_core(edge1)
-    ff1 = ffn(after(qkv1, away), 4)
+    ff1 = ffn(after((qkv1, back), away), 4)
     back = attend_columns(1, after((ff1, their_qkv1), got1), back)
     again = lax.all_to_all(back, ROW, split_axis=0, concat_axis=0, tiled=True)
 

time: 253 us -> 243 us (0.960)
  waiting for transfers between devices: 82.7 us -> 72 us
    ppermute x27, waiting for transfers between devices: 63.4 us -> 55.7 us  [permuted(): return lax.ppermute(array, axis, [(i, (i + by) % n) for i in range(n)])]
    all_to_all x2, waiting for transfers between devices: 3.4 us -> 0.01 us  [columns(): lax.all_to_all(qkv.reshape(row_peers, rows * HALF, 6 * hs), ROW, split_ax...]
  transfers between devices with their start and end apart: 33 -> 33, of which waited for: 18 -> 17; matrix products, arithmetic and copies ran while one was open for 1% -> 1% of each run, Pallas kernels for 26% -> 29%
where the time goes in v3:
time: 243 us; the launch traced here: 242 us
  Pallas kernels  89.5 us (37%)
  waiting for transfers between devices  72 us (30%)
  starting transfers between devices  66.9 us (28%)
  local copies, waits for them, and re-layouts  10.6 us (4%)
    ppermute x27, waiting for transfers between devices, permuted(): return lax.ppermute(array, axis, [(i, (i + by) % n) for i in range(n)])  55.7 us
    ppermute x27, starting transfers between devices, permuted(): return lax.ppermute(array, axis, [(i, (i + by) % n) for i in range(n)])  27.8 us
    pallas_call x3, Pallas kernels, feed_forward(): pl.pallas_call(lambda *refs: forward_body(n, slots, slots == 4, *refs), i...  27.7 us
    pallas_call x3, Pallas kernels, terms(): pl.pallas_call(lambda *refs: term_body(hs, rows, splits, *refs), grid=(1,...  13.4 us
    all_to_all x2, starting transfers between devices, columns(): lax.all_to_all(qkv.reshape(row_peers, rows * HALF, 6 * hs), ROW, split_ax...  13 us
    pallas_call x2, Pallas kernels, project(): pl.pallas_call(lambda *refs: project_body(rows, n, *refs), grid=(3,), in_...  13 us
    all_to_all x1, starting transfers between devices, per_device(): lax.all_to_all(line, ALL, split_axis=0, concat_axis=0, tiled=True)  12.7 us
    all_to_all x1, waiting for transfers between devices, per_device(): lax.all_to_all(line, ALL, split_axis=0, concat_axis=0, tiled=True)  9.59 us
  transfers between devices with their start and end apart: 33, of which 17 were waited for; matrix products, arithmetic and copies ran while one was open for 1% of the time, Pallas kernels for 29%

profile of v3, /device:TPU:1, one launch (start us, length us, event | category | flops | bytes accessed | tf_op | source)
XLA Modules:
  0.0 242.0 jit_solution(4021792077851041626)
XLA Ops:
  0.6 1.5 collective-permute-start.1
  2.6 2.3 normalize.1.refs_0_
  4.9 1.7 collective-permute-start.4
  6.7 2.1 collective-permute-start.5
  8.8 1.2 collective-permute-start.6
  10.1 5.7 %feed_forward.3.refs_3_ = bf16[192,2176]{1,0:T(8,128)(2,1)} custom-call(bf16[192,2048]{1,0:T(8,128)(2,1)} %normalize.1.refs_0_, bf16[2048,512]{1,0:T(8,128)(2,1)} %refs_3_.3, bf16[2048,512]{1,0:T(8,128)(2,1)} %copy-done.6, bf16[512,2048]{1,0:T(8,128)(2,1)} %refs_5_.1, bf16[512,2048]{1,0:T(8,128)(2,1)} %collective-permute-done.2.refs_4_.refs_9_.refs_6_), custom_call_target="tpu_custom_call" | custom-call | flops 1610612736 | bytes 9961472 | tf_op jit(solution)/shard_map/feed_forward/pallas_call | solution.py:208
  15.8 11.0 %collective-permute-done.4.refs_1_.refs_0_ = bf16[192,2048]{1,0:T(8,128)(2,1)S(1)} collective-permute-done((bf16[192,2048]{1,0:T(8,128)(2,1)}, bf16[192,2048]{1,0:T(8,128)(2,1)S(1)}, u32[]{:S(2)}, u32[]{:S(2)}) %collective-permute-start.4) | collective-permute-done | bytes 786464 | tf_op jit(solution)/shard_map/ppermute | solution.py:23
  26.8 1.0 collective-permute-done.6.refs_3_.refs_2_
  27.8 6.3 %project.2 = (bf16[4,2,6,16,768]{4,3,2,1,0:T(8,128)(2,1)}, bf16[4,2,16,512]{3,2,1,0:T(8,128)(2,1)}) custom-call(bf16[192,2048]{1,0:T(8,128)(2,1)} %normalize.1.refs_0_, bf16[192,2048]{1,0:T(8,128)(2,1)} %copy-done.26, bf16[192,2048]{1,0:T(8,128)(2,1)} %collective-permute-done.5.refs_2_.refs_1_, bf16[192,2048]{1,0:T(8,128)(2,1)} %collective-permute-done.6.refs_3_.refs_2_, ...), custom_call_target="tpu_custom_call" | custom-call | flops 2415919104 | bytes 6291456 | tf_op jit(solution)/shard_map/project/pallas_call | solution.py:108
  34.2 1.2 collective-permute-start.7
  35.4 1.2 collective-permute-start.9
  36.6 2.7 %collective-permute-start.10 = (bf16[192,2048]{1,0:T(8,128)(2,1)}, bf16[192,2048]{1,0:T(8,128)(2,1)}, u32[]{:S(2)}, u32[]{:S(2)}) collective-permute-start(bf16[192,2048]{1,0:T(8,128)(2,1)} %collective-permute-done.6.refs_3_.refs_2_), channel_id=1, source_target_pairs={{0,6},{2,0},{4,2},{6,4},{1,7},{3,1},{5,3},{7,5},{8,14},{10,8},{12,... | collective-permute-start | bytes 2359304 | tf_op jit(solution)/shard_map/ppermute | solution.py:23
  39.3 6.4 %all-to-all-start = ((bf16[8,96,768]{2,1,0:T(8,128)(2,1)}), bf16[8,96,768]{2,1,0:T(8,128)(2,1)S(1)}, u32[]{:S(2)}, u32[]{:S(2)}) async-start(bf16[8,96,768]{2,1,0:T(8,128)(2,1)} %bitcast.17), calls=%async_computation | async-start | bytes 2359296 | tf_op jit(solution)/shard_map/all_to_all | solution.py:593
  45.7 10.2 %collective-permute-done.8.t0.refs_0_ = bf16[192,2048]{1,0:T(8,128)(2,1)S(1)} collective-permute-done((bf16[192,2048]{1,0:T(8,128)(2,1)}, bf16[192,2048]{1,0:T(8,128)(2,1)S(1)}, u32[]{:S(2)}, u32[]{:S(2)}) %collective-permute-start.8) | collective-permute-done | bytes 786464 | tf_op jit(solution)/shard_map/ppermute | solution.py:23
  56.7 2.0 thirds.1
  58.8 1.2 collective-permute-start.11
  60.0 2.7 %collective-permute-start.13 = (bf16[64,2048]{1,0:T(8,128)(2,1)}, bf16[64,2048]{1,0:T(8,128)(2,1)S(1)}, u32[]{:S(2)}, u32[]{:S(2)}) collective-permute-start(bf16[64,2048]{1,0:T(8,128)(2,1)} %get-tuple-element.73), channel_id=1, source_target_pairs={{0,6},{2,0},{4,2},{6,4},{1,7},{3,1},{5,3},{7,5},{8,14},{10,8},{12,... | collective-permute-start | bytes 786440 | tf_op jit(solution)/shard_map/ppermute | solution.py:23
  62.7 10.2 %collective-permute-done.11.refs_3_ = bf16[64,2048]{1,0:T(8,128)(2,1)S(1)} collective-permute-done((bf16[64,2048]{1,0:T(8,128)(2,1)}, bf16[64,2048]{1,0:T(8,128)(2,1)S(1)}, u32[]{:S(2)}, u32[]{:S(2)}) %collective-permute-start.11) | collective-permute-done | bytes 262176 | tf_op jit(solution)/shard_map/ppermute | solution.py:23
  73.7 6.7 %project.3 = (bf16[4,2,6,16,768]{4,3,2,1,0:T(8,128)(2,1)}, bf16[4,2,16,512]{3,2,1,0:T(8,128)(2,1)}) custom-call(bf16[192,2048]{1,0:T(8,128)(2,1)} %copy-done.14, bf16[192,2048]{1,0:T(8,128)(2,1)} %collective-permute-done.9.t1.refs_1_, bf16[192,2048]{1,0:T(8,128)(2,1)} %collective-permute-done.10.t2.refs_2_, bf16[64,2048]{1,0:T(8,128)(2,1)} %copy-done.27, ...), custom_call_target="tpu_custom_call" | custom-call | flops 2415919104 | bytes 6291456 | tf_op jit(solution)/shard_map/project/pallas_call | solution.py:108
  80.4 1.1 collective-permute-start.14
  82.5 6.7 %all-to-all-start.1 = ((bf16[8,96,768]{2,1,0:T(8,128)(2,1)}), bf16[8,96,768]{2,1,0:T(8,128)(2,1)S(1)}, u32[]{:S(2)}, u32[]{:S(2)}) async-start(bf16[8,96,768]{2,1,0:T(8,128)(2,1)} %bitcast.18), calls=%async_computation.1 | async-start | bytes 2359296 | tf_op jit(solution)/shard_map/all_to_all | solution.py:593
  90.6 4.0 %column_attention.2.refs_3_ = bf16[8,2,7,16,256]{4,3,2,1,0:T(8,128)(2,1)} custom-call(f32[1]{0:T(128)S(6)} %copy.32.refs_0_, f32[1]{0:T(128)} %collective-permute-done.refs_1_, bf16[48,16,768]{2,1,0:T(8,128)(2,1)} %bitcast.21), custom_call_target="tpu_custom_call" | custom-call | flops 452984832 | bytes 1572864 | tf_op jit(solution)/shard_map/column_attention/pallas_call | solution.py:343
  94.6 11.6 %feed_forward.4 = (bf16[192,2176]{1,0:T(8,128)(2,1)}, bf16[192,2176]{1,0:T(8,128)(2,1)}, bf16[192,2176]{1,0:T(8,128)(2,1)}, bf16[192,2176]{1,0:T(8,128)(2,1)}) custom-call(bf16[192,2048]{1,0:T(8,128)(2,1)} %copy-done.14, bf16[192,2048]{1,0:T(8,128)(2,1)} %collective-permute-done.9.t1.refs_1_, bf16[192,2048]{1,0:T(8,128)(2,1)} %collective-permute-done.10.t2.refs_2_, ...), custom_call_target="tpu_custom_call" | custom-call | flops 6442450944 | bytes 14680064 | tf_op jit(solution)/shard_map/feed_forward/pallas_call | solution.py:208
  107.3 4.0 %column_attention.3 = bf16[8,2,7,16,256]{4,3,2,1,0:T(8,128)(2,1)} custom-call(f32[1]{0:T(128)S(6)} %copy.32.refs_0_, f32[1]{0:T(128)} %collective-permute-done.refs_1_, bf16[48,16,768]{2,1,0:T(8,128)(2,1)} %bitcast.16, bf16[8,2,7,16,256]{4,3,2,1,0:T(8,128)(2,1)} %column_attention.2.refs_3_), custom_call_target="tpu_custom_call", output_to_operand_aliasing={{}: (3, {})} | custom-call | flops 452984832 | bytes 1572864 | tf_op jit(solution)/shard_map/column_attention/pallas_call | solution.py:343
  111.3 7.0 %all-to-all-start.2 = ((bf16[8,2,7,16,256]{4,3,2,1,0:T(8,128)(2,1)}), bf16[8,2,7,16,256]{4,3,2,1,0:T(8,128)(2,1)S(1)}, u32[]{:S(2)}, u32[]{:S(2)}) async-start(bf16[8,2,7,16,256]{4,3,2,1,0:T(8,128)(2,1)} %column_attention.3), calls=%async_computation.2 | async-start | bytes 1835008 | tf_op jit(solution)/shard_map/all_to_all | solution.py:617
  118.4 3.4 %collective-permute-start.15 = (bf16[4,2,16,512]{3,2,1,0:T(8,128)(2,1)S(1)}, bf16[4,2,16,512]{3,2,1,0:T(8,128)(2,1)S(1)}, u32[]{:S(2)}, u32[]{:S(2)}) collective-permute-start(bf16[4,2,16,512]{3,2,1,0:T(8,128)(2,1)S(1)} %copy-done.30), channel_id=1, source_target_pairs={{0,16},{16,32},{32,48},{48,64},{64,80},{80,96},{96,112},{1,17},{17... | collective-permute-start | bytes 393224 | tf_op jit(solution)/shard_map/ppermute | solution.py:44
  121.7 3.1 %collective-permute-start.16 = (bf16[4,2,16,512]{3,2,1,0:T(8,128)(2,1)}, bf16[4,2,16,512]{3,2,1,0:T(8,128)(2,1)S(1)}, u32[]{:S(2)}, u32[]{:S(2)}) collective-permute-start(bf16[4,2,16,512]{3,2,1,0:T(8,128)(2,1)} %get-tuple-element.95), channel_id=1, source_target_pairs={{0,16},{16,32},{32,48},{48,64},{64,80},{80,96},{96,112},{1,17},{17... | collective-permute-start | bytes 393224 | tf_op jit(solution)/shard_map/ppermute | solution.py:44
  124.9 5.9 %collective-permute-done.15.refs_9_ = bf16[4,2,16,512]{3,2,1,0:T(8,128)(2,1)S(1)} collective-permute-done((bf16[4,2,16,512]{3,2,1,0:T(8,128)(2,1)S(1)}, bf16[4,2,16,512]{3,2,1,0:T(8,128)(2,1)S(1)}, u32[]{:S(2)}, u32[]{:S(2)}) %collective-permute-start.15) | collective-permute-done | bytes 131104 | tf_op jit(solution)/shard_map/ppermute | solution.py:44
  130.8 2.1 collective-permute-start.17
  133.8 1.2 collective-permute-start.18
  137.3 9.4 %row_attention.1 = (bf16[4,2,6,16,256]{4,3,2,1,0:T(8,128)(2,1)}, bf16[4,2,6,16,256]{4,3,2,1,0:T(8,128)(2,1)}, f32[4,2,6,16,256]{4,3,2,1,0:T(8,128)}, f32[4,2,6,16,256]{4,3,2,1,0:T(8,128)}) custom-call(s32[1]{0:T(128)} %bitcast.6.refs_0_, s32[256,1]{1,0:T(8,128)} %add.135.refs_1_, s32[1,512]{1,0:T(1,128)} %bitcast.27, ...), custom_call_target="tpu_custom_call" | custom-call | flops 1610612736 | bytes 6291456 | tf_op jit(solution)/shard_map/row_attention/pallas_call | solution.py:281
  147.9 3.1 %terms.3 = (bf16[64,2176]{1,0:T(8,128)(2,1)}, bf16[64,2176]{1,0:T(8,128)(2,1)}, bf16[64,2176]{1,0:T(8,128)(2,1)}) custom-call(bf16[8,2,7,16,256]{4,3,2,1,0:T(8,128)(2,1)} %copy-done, bf16[4,2,6,16,256]{4,3,2,1,0:T(8,128)(2,1)} %get-tuple-element.102.refs_1_, f32[4,2,6,16,256]{4,3,2,1,0:T(8,128)} %get-tuple-element.103.refs_2_, ...), custom_call_target="tpu_custom_call" | custom-call | flops 213909504 | bytes 2088960 | tf_op jit(solution)/shard_map/terms/pallas_call | solution.py:399
  151.3 2.7 %collective-permute-start.21 = (bf16[64,2176]{1,0:T(8,128)(2,1)}, bf16[64,2176]{1,0:T(8,128)(2,1)S(1)}, u32[]{:S(2)}, u32[]{:S(2)}) collective-permute-start(bf16[64,2176]{1,0:T(8,128)(2,1)} %get-tuple-element.107), channel_id=1, source_target_pairs={{0,6},{2,0},{4,2},{6,4},{1,7},{3,1},{5,3},{7,5},{8,14},{10,8},{12,... | collective-permute-start | bytes 835592 | tf_op jit(solution)/shard_map/ppermute | solution.py:23
  154.0 4.7 %terms.4 = (bf16[192,2176]{1,0:T(8,128)(2,1)}, bf16[192,2176]{1,0:T(8,128)(2,1)}, bf16[192,2176]{1,0:T(8,128)(2,1)}) custom-call(bf16[8,2,7,16,256]{4,3,2,1,0:T(8,128)(2,1)} %copy-done, bf16[4,2,6,16,256]{4,3,2,1,0:T(8,128)(2,1)} %get-tuple-element.102.refs_1_, f32[4,2,6,16,256]{4,3,2,1,0:T(8,128)} %get-tuple-element.103.refs_2_, ...), custom_call_target="tpu_custom_call" | custom-call | flops 641728512 | bytes 6266880 | tf_op jit(solution)/shard_map/terms/pallas_call | solution.py:399
  160.1 3.0 %collective-permute-done.22.g2 = bf16[64,2176]{1,0:T(8,128)(2,1)S(1)} collective-permute-done((bf16[64,2176]{1,0:T(8,128)(2,1)}, bf16[64,2176]{1,0:T(8,128)(2,1)S(1)}, u32[]{:S(2)}, u32[]{:S(2)}) %collective-permute-start.22) | collective-permute-done | bytes 278560 | tf_op jit(solution)/shard_map/ppermute | solution.py:23
  163.8 2.3 add_far.1
  166.5 1.1 collective-permute-start.24
  167.7 1.1 collective-permute-start.25
  168.7 10.4 %feed_forward.5 = (bf16[192,2176]{1,0:T(8,128)(2,1)}, bf16[192,2176]{1,0:T(8,128)(2,1)}, bf16[192,2176]{1,0:T(8,128)(2,1)}) custom-call(bf16[192,2048]{1,0:T(8,128)(2,1)} %copy-done.26, bf16[192,2048]{1,0:T(8,128)(2,1)} %collective-permute-done.5.refs_2_.refs_1_, bf16[192,2048]{1,0:T(8,128)(2,1)} %collective-permute-done.6.refs_3_.refs_2_, ...), custom_call_target="tpu_custom_call" | custom-call | flops 4831838208 | bytes 13107200 | tf_op jit(solution)/shard_map/feed_forward/pallas_call | solution.py:208
  179.2 5.6 %terms.5 = (bf16[192,2176]{1,0:T(8,128)(2,1)}, bf16[192,2176]{1,0:T(8,128)(2,1)}, bf16[192,2176]{1,0:T(8,128)(2,1)}, bf16[192,2176]{1,0:T(8,128)(2,1)}) custom-call(bf16[8,2,7,16,256]{4,3,2,1,0:T(8,128)(2,1)} %copy-done, bf16[4,2,6,16,256]{4,3,2,1,0:T(8,128)(2,1)} %get-tuple-element.96.refs_1_, f32[4,2,6,16,256]{4,3,2,1,0:T(8,128)} %get-tuple-element.97.refs_2_, ...), custom_call_target="tpu_custom_call" | custom-call | flops 855638016 | bytes 8355840 | tf_op jit(solution)/shard_map/terms/pallas_call | solution.py:399
  185.5 2.1 collective-permute-done.25.r2
  188.5 3.5 %add_near.1 = (bf16[192,2176]{1,0:T(8,128)(2,1)}, bf16[192,2176]{1,0:T(8,128)(2,1)}) custom-call(bf16[192,2176]{1,0:T(8,128)(2,1)} %get-tuple-element.117.t0, bf16[192,2176]{1,0:T(8,128)(2,1)} %get-tuple-element.118.t1, bf16[192,2176]{1,0:T(8,128)(2,1)} %copy-done.11, bf16[192,2176]{1,0:T(8,128)(2,1)} %copy-done.12, bf16[192,2176]{1,0:T(8,128)(2,1)} %copy-done.13), custom_call_target="tpu_custom_call" | custom-call | flops 1253376 | bytes 5849088 | tf_op jit(solution)/shard_map/add_near/pallas_call | solution.py:466
  193.8 11.9 %collective-permute-done.27.m1 = bf16[192,2176]{1,0:T(8,128)(2,1)S(1)} collective-permute-done((bf16[192,2176]{1,0:T(8,128)(2,1)}, bf16[192,2176]{1,0:T(8,128)(2,1)S(1)}, u32[]{:S(2)}, u32[]{:S(2)}) %collective-permute-start.27) | collective-permute-done | bytes 835616 | tf_op jit(solution)/shard_map/ppermute | solution.py:23
  205.7 3.2 %collective-permute-done.26.m0 = bf16[192,2176]{1,0:T(8,128)(2,1)S(1)} collective-permute-done((bf16[192,2176]{1,0:T(8,128)(2,1)}, bf16[192,2176]{1,0:T(8,128)(2,1)S(1)}, u32[]{:S(2)}, u32[]{:S(2)}) %collective-permute-start.26) | collective-permute-done | bytes 835616 | tf_op jit(solution)/shard_map/ppermute | solution.py:23
  210.7 5.7 %head.1 = (bf16[192,2048]{1,0:T(8,128)(2,1)}, f32[128,1,256]{2,1,0:T(1,128)}) custom-call(bf16[192,2048]{1,0:T(8,128)(2,1)} %bitcast.20, bf16[192,2176]{1,0:T(8,128)(2,1)} %get-tuple-element.116.mine, bf16[192,2176]{1,0:T(8,128)(2,1)} %copy-done.9, bf16[192,2176]{1,0:T(8,128)(2,1)} %copy-done.8, bf16[192,2176]{1,0:T(8,128)(2,1)} %copy-done.10, ...), custom_call_target="tpu_custom_call" | custom-call | tf_op jit(solution)/shard_map/head/pallas_call | solution.py:504
  216.4 12.7 %all-to-all-start.3 = ((f32[128,1,256]{2,1,0:T(1,128)}), f32[128,1,256]{2,1,0:T(1,128)S(1)}, u32[]{:S(2)}, u32[]{:S(2)}) async-start(f32[128,1,256]{2,1,0:T(1,128)} %get-tuple-element.125), calls=%async_computation.3 | async-start | bytes 262144 | tf_op jit(solution)/shard_map/all_to_all | solution.py:672
  229.7 9.6 %all-to-all-done.3 = f32[128,1,256]{2,1,0:T(1,128)S(1)} async-done(((f32[128,1,256]{2,1,0:T(1,128)}), f32[128,1,256]{2,1,0:T(1,128)S(1)}, u32[]{:S(2)}, u32[]{:S(2)}) %all-to-all-start.3) | async-done | bytes 131104 | tf_op jit(solution)/shard_map/all_to_all | solution.py:672
  239.9 2.1 pick.1
  (108 shorter events, 18.9 us)
Async XLA Ops:
  0.6 8.2 %collective-permute-start.1 = (bf16[2048,512]{1,0:T(8,128)(2,1)}, bf16[2048,512]{1,0:T(8,128)(2,1)S(1)}, u32[]{:S(2)}, u32[]{:S(2)}) collective-permute-start(bf16[2048,512]{1,0:T(8,128)(2,1)} %refs_3_.3), channel_id=1, source_target_pairs={{0,1},{1,0},{2,3},{3,2},{4,5},{5,4},{6,7},{7,6},{8,9},{9,8},{10,11... | collective-permute-start | bytes 6291464 | tf_op jit(solution)/shard_map/ppermute | solution.py:23
  2.1 7.9 %collective-permute-start.2 = (bf16[512,2048]{1,0:T(8,128)(2,1)}, bf16[512,2048]{1,0:T(8,128)(2,1)}, u32[]{:S(2)}, u32[]{:S(2)}) collective-permute-start(bf16[512,2048]{1,0:T(8,128)(2,1)} %refs_5_.1), channel_id=1, source_target_pairs={{0,1},{1,0},{2,3},{3,2},{4,5},{5,4},{6,7},{7,6},{8,9},{9,8},{10,11... | collective-permute-start | bytes 6291464 | tf_op jit(solution)/shard_map/ppermute | solution.py:23
  2.2 25.7 %collective-permute-start.3 = (bf16[3,2048,128]{2,1,0:T(8,128)(2,1)}, bf16[3,2048,128]{2,1,0:T(8,128)(2,1)}, u32[]{:S(2)}, u32[]{:S(2)}) collective-permute-start(bf16[3,2048,128]{2,1,0:T(8,128)(2,1)} %refs_6_.3), channel_id=1, source_target_pairs={{0,1},{1,0},{2,3},{3,2},{4,5},{5,4},{6,7},{7,6},{8,9},{9,8},{10,11... | collective-permute-start | bytes 4718600 | tf_op jit(solution)/shard_map/ppermute | solution.py:23
  4.9 21.9 %collective-permute-start.4 = (bf16[192,2048]{1,0:T(8,128)(2,1)}, bf16[192,2048]{1,0:T(8,128)(2,1)S(1)}, u32[]{:S(2)}, u32[]{:S(2)}) collective-permute-start(bf16[192,2048]{1,0:T(8,128)(2,1)} %normalize.1.refs_0_), channel_id=1, source_target_pairs={{0,2},{2,4},{4,6},{6,0},{1,3},{3,5},{5,7},{7,1},{8,10},{10,12},{12... | collective-permute-start | bytes 2359304 | tf_op jit(solution)/shard_map/ppermute | solution.py:23
  6.7 20.2 %collective-permute-start.5 = (bf16[192,2048]{1,0:T(8,128)(2,1)}, bf16[192,2048]{1,0:T(8,128)(2,1)}, u32[]{:S(2)}, u32[]{:S(2)}) collective-permute-start(bf16[192,2048]{1,0:T(8,128)(2,1)} %normalize.1.refs_0_), channel_id=1, source_target_pairs={{0,6},{2,0},{4,2},{6,4},{1,7},{3,1},{5,3},{7,5},{8,14},{10,8},{12,... | collective-permute-start | bytes 2359304 | tf_op jit(solution)/shard_map/ppermute | solution.py:23
  8.8 19.0 %collective-permute-start.6 = (bf16[192,2048]{1,0:T(8,128)(2,1)}, bf16[192,2048]{1,0:T(8,128)(2,1)}, u32[]{:S(2)}, u32[]{:S(2)}) collective-permute-start(bf16[192,2048]{1,0:T(8,128)(2,1)} %normalize.1.refs_0_), channel_id=1, source_target_pairs={{0,8},{8,0},{1,9},{9,1},{2,10},{10,2},{3,11},{11,3},{4,12},{12,4},... | collective-permute-start | bytes 2359304 | tf_op jit(solution)/shard_map/ppermute | solution.py:23
  34.2 38.7 %collective-permute-start.7 = (bf16[4,2,6,16,768]{4,3,2,1,0:T(8,128)(2,1)}, bf16[4,2,6,16,768]{4,3,2,1,0:T(8,128)(2,1)S(1)}, u32[]{:S(2)}, u32[]{:S(2)}) collective-permute-start(bf16[4,2,6,16,768]{4,3,2,1,0:T(8,128)(2,1)} %get-tuple-element.67.refs_3_), channel_id=1, source_target_pairs={{0,1},{1,0},{2,3},{3,2},{4,5},{5,4},{6,7},{7,6},{8,9},{9,8},{10,11... | collective-permute-start | bytes 3538952 | tf_op jit(solution)/shard_map/ppermute | solution.py:23
  35.4 20.4 %collective-permute-start.8 = (bf16[192,2048]{1,0:T(8,128)(2,1)}, bf16[192,2048]{1,0:T(8,128)(2,1)S(1)}, u32[]{:S(2)}, u32[]{:S(2)}) collective-permute-start(bf16[192,2048]{1,0:T(8,128)(2,1)} %copy-done.26), channel_id=1, source_target_pairs={{0,2},{2,4},{4,6},{6,0},{1,3},{3,5},{5,7},{7,1},{8,10},{10,12},{12... | collective-permute-start | bytes 2359304 | tf_op jit(solution)/shard_map/ppermute | solution.py:23
  35.4 20.4 %collective-permute-start.9 = (bf16[192,2048]{1,0:T(8,128)(2,1)}, bf16[192,2048]{1,0:T(8,128)(2,1)}, u32[]{:S(2)}, u32[]{:S(2)}) collective-permute-start(bf16[192,2048]{1,0:T(8,128)(2,1)} %copy-done.26), channel_id=1, source_target_pairs={{0,8},{8,0},{1,9},{9,1},{2,10},{10,2},{3,11},{11,3},{4,12},{12,4},... | collective-permute-start | bytes 2359304 | tf_op jit(solution)/shard_map/ppermute | solution.py:23
  36.6 19.3 %collective-permute-start.10 = (bf16[192,2048]{1,0:T(8,128)(2,1)}, bf16[192,2048]{1,0:T(8,128)(2,1)}, u32[]{:S(2)}, u32[]{:S(2)}) collective-permute-start(bf16[192,2048]{1,0:T(8,128)(2,1)} %collective-permute-done.6.refs_3_.refs_2_), channel_id=1, source_target_pairs={{0,6},{2,0},{4,2},{6,4},{1,7},{3,1},{5,3},{7,5},{8,14},{10,8},{12,... | collective-permute-start | bytes 2359304 | tf_op jit(solution)/shard_map/ppermute | solution.py:23
  39.3 42.2 %all-to-all-start = ((bf16[8,96,768]{2,1,0:T(8,128)(2,1)}), bf16[8,96,768]{2,1,0:T(8,128)(2,1)S(1)}, u32[]{:S(2)}, u32[]{:S(2)}) async-start(bf16[8,96,768]{2,1,0:T(8,128)(2,1)} %bitcast.17), calls=%async_computation | async-start | bytes 2359296 | tf_op jit(solution)/shard_map/all_to_all | solution.py:593
  58.8 14.1 %collective-permute-start.11 = (bf16[64,2048]{1,0:T(8,128)(2,1)}, bf16[64,2048]{1,0:T(8,128)(2,1)S(1)}, u32[]{:S(2)}, u32[]{:S(2)}) collective-permute-start(bf16[64,2048]{1,0:T(8,128)(2,1)} %get-tuple-element.71), channel_id=1, source_target_pairs={{0,8},{8,0},{1,9},{9,1},{2,10},{10,2},{3,11},{11,3},{4,12},{12,4},... | collective-permute-start | bytes 786440 | tf_op jit(solution)/shard_map/ppermute | solution.py:23
  60.0 12.8 %collective-permute-start.12 = (bf16[64,2048]{1,0:T(8,128)(2,1)}, bf16[64,2048]{1,0:T(8,128)(2,1)S(1)}, u32[]{:S(2)}, u32[]{:S(2)}) collective-permute-start(bf16[64,2048]{1,0:T(8,128)(2,1)} %get-tuple-element.72), channel_id=1, source_target_pairs={{0,2},{2,4},{4,6},{6,0},{1,3},{3,5},{5,7},{7,1},{8,10},{10,12},{12... | collective-permute-start | bytes 786440 | tf_op jit(solution)/shard_map/ppermute | solution.py:23
  60.0 12.8 %collective-permute-start.13 = (bf16[64,2048]{1,0:T(8,128)(2,1)}, bf16[64,2048]{1,0:T(8,128)(2,1)S(1)}, u32[]{:S(2)}, u32[]{:S(2)}) collective-permute-start(bf16[64,2048]{1,0:T(8,128)(2,1)} %get-tuple-element.73), channel_id=1, source_target_pairs={{0,6},{2,0},{4,2},{6,4},{1,7},{3,1},{5,3},{7,5},{8,14},{10,8},{12,... | collective-permute-start | bytes 786440 | tf_op jit(solution)/shard_map/ppermute | solution.py:23
  73.7 6.7 %copy-start.4 = (bf16[4,2,6,16,768]{4,3,2,1,0:T(8,128)(2,1)}, bf16[4,2,6,16,768]{4,3,2,1,0:T(8,128)(2,1)S(1)}, u32[]{:S(2)}) copy-start(bf16[4,2,6,16,768]{4,3,2,1,0:T(8,128)(2,1)S(1)} %collective-permute-done.7.refs_5_.refs_6_) | copy-start | bytes 3538948
  80.4 9.1 %copy-start.2 = (bf16[128,2048]{1,0:T(8,128)(2,1)S(1)}, bf16[128,2048]{1,0:T(8,128)(2,1)}, u32[]{:S(2)}) copy-start(bf16[128,2048]{1,0:T(8,128)(2,1)} %refs_7_.1) | copy-start | bytes 1572868
  80.4 10.0 %copy-start.24 = (s32[8]{0:T(128)S(1)}, s32[8]{0:T(128)}, u32[]{:S(2)}) copy-start(s32[8]{0:T(128)} %constant.117.clone) | copy-start | bytes 100
  80.4 10.0 %copy-start.25 = (s32[8]{0:T(128)S(1)}, s32[8]{0:T(128)}, u32[]{:S(2)}) copy-start(s32[8]{0:T(128)} %constant.118.clone) | copy-start | bytes 100
  80.4 25.9 %collective-permute-start.14 = (bf16[4,2,6,16,768]{4,3,2,1,0:T(8,128)(2,1)}, bf16[4,2,6,16,768]{4,3,2,1,0:T(8,128)(2,1)S(1)}, u32[]{:S(2)}, u32[]{:S(2)}) collective-permute-start(bf16[4,2,6,16,768]{4,3,2,1,0:T(8,128)(2,1)} %get-tuple-element.80.refs_4_), channel_id=1, source_target_pairs={{0,1},{1,0},{2,3},{3,2},{4,5},{5,4},{6,7},{7,6},{8,9},{9,8},{10,11... | collective-permute-start | bytes 3538952 | tf_op jit(solution)/shard_map/ppermute | solution.py:23
  82.5 23.7 %all-to-all-start.1 = ((bf16[8,96,768]{2,1,0:T(8,128)(2,1)}), bf16[8,96,768]{2,1,0:T(8,128)(2,1)S(1)}, u32[]{:S(2)}, u32[]{:S(2)}) async-start(bf16[8,96,768]{2,1,0:T(8,128)(2,1)} %bitcast.18), calls=%async_computation.1 | async-start | bytes 2359296 | tf_op jit(solution)/shard_map/all_to_all | solution.py:593
  89.2 1.4 collective-permute-start
  89.5 57.3 %collective-permute-start.19 = (bf16[128,2048]{1,0:T(8,128)(2,1)S(1)}, bf16[128,2048]{1,0:T(8,128)(2,1)S(1)}, u32[]{:S(2)}, u32[]{:S(2)}) collective-permute-start(bf16[128,2048]{1,0:T(8,128)(2,1)S(1)} %copy-done.2), channel_id=1, source_target_pairs={{0,1},{1,0},{2,3},{3,2},{4,5},{5,4},{6,7},{7,6},{8,9},{9,8},{10,11... | collective-permute-start | bytes 1572872 | tf_op jit(solution)/shard_map/ppermute | solution.py:23
  106.3 5.0 %copy-start.5 = (bf16[4,2,6,16,768]{4,3,2,1,0:T(8,128)(2,1)}, bf16[4,2,6,16,768]{4,3,2,1,0:T(8,128)(2,1)S(1)}, u32[]{:S(2)}) copy-start(bf16[4,2,6,16,768]{4,3,2,1,0:T(8,128)(2,1)S(1)} %collective-permute-done.14.refs_7_.refs_8_) | copy-start | bytes 3538948
  111.3 7.0 %copy-start.30 = (bf16[4,2,16,512]{3,2,1,0:T(8,128)(2,1)S(1)}, bf16[4,2,16,512]{3,2,1,0:T(8,128)(2,1)}, u32[]{:S(2)}) copy-start(bf16[4,2,16,512]{3,2,1,0:T(8,128)(2,1)} %get-tuple-element.94) | copy-start | bytes 393220
  111.3 35.4 %all-to-all-start.2 = ((bf16[8,2,7,16,256]{4,3,2,1,0:T(8,128)(2,1)}), bf16[8,2,7,16,256]{4,3,2,1,0:T(8,128)(2,1)S(1)}, u32[]{:S(2)}, u32[]{:S(2)}) async-start(bf16[8,2,7,16,256]{4,3,2,1,0:T(8,128)(2,1)} %column_attention.3), calls=%async_computation.2 | async-start | bytes 1835008 | tf_op jit(solution)/shard_map/all_to_all | solution.py:617
  118.4 12.4 %collective-permute-start.15 = (bf16[4,2,16,512]{3,2,1,0:T(8,128)(2,1)S(1)}, bf16[4,2,16,512]{3,2,1,0:T(8,128)(2,1)S(1)}, u32[]{:S(2)}, u32[]{:S(2)}) collective-permute-start(bf16[4,2,16,512]{3,2,1,0:T(8,128)(2,1)S(1)} %copy-done.30), channel_id=1, source_target_pairs={{0,16},{16,32},{32,48},{48,64},{64,80},{80,96},{96,112},{1,17},{17... | collective-permute-start | bytes 393224 | tf_op jit(solution)/shard_map/ppermute | solution.py:44
  121.7 12.1 %collective-permute-start.16 = (bf16[4,2,16,512]{3,2,1,0:T(8,128)(2,1)}, bf16[4,2,16,512]{3,2,1,0:T(8,128)(2,1)S(1)}, u32[]{:S(2)}, u32[]{:S(2)}) collective-permute-start(bf16[4,2,16,512]{3,2,1,0:T(8,128)(2,1)} %get-tuple-element.95), channel_id=1, source_target_pairs={{0,16},{16,32},{32,48},{48,64},{64,80},{80,96},{96,112},{1,17},{17... | collective-permute-start | bytes 393224 | tf_op jit(solution)/shard_map/ppermute | solution.py:44
  130.8 5.9 %copy-start.18 = (bf16[4,2,16,512]{3,2,1,0:T(8,128)(2,1)}, bf16[4,2,16,512]{3,2,1,0:T(8,128)(2,1)S(1)}, u32[]{:S(2)}) copy-start(bf16[4,2,16,512]{3,2,1,0:T(8,128)(2,1)S(1)} %collective-permute-done.15.refs_9_) | copy-start | bytes 393220
  130.8 5.9 %collective-permute-start.17 = (bf16[4,2,16,512]{3,2,1,0:T(8,128)(2,1)S(1)}, bf16[4,2,16,512]{3,2,1,0:T(8,128)(2,1)S(1)}, u32[]{:S(2)}, u32[]{:S(2)}) collective-permute-start(bf16[4,2,16,512]{3,2,1,0:T(8,128)(2,1)S(1)} %collective-permute-done.15.refs_9_), channel_id=1, source_target_pairs={{0,1},{1,0},{2,3},{3,2},{4,5},{5,4},{6,7},{7,6},{8,9},{9,8},{10,11... | collective-permute-start | bytes 393224 | tf_op jit(solution)/shard_map/ppermute | solution.py:23
  133.8 2.8 %copy-start.19 = (bf16[4,2,16,512]{3,2,1,0:T(8,128)(2,1)}, bf16[4,2,16,512]{3,2,1,0:T(8,128)(2,1)S(1)}, u32[]{:S(2)}) copy-start(bf16[4,2,16,512]{3,2,1,0:T(8,128)(2,1)S(1)} %collective-permute-done.16.refs_10_) | copy-start | bytes 393220
  133.8 2.8 %collective-permute-start.18 = (bf16[4,2,16,512]{3,2,1,0:T(8,128)(2,1)S(1)}, bf16[4,2,16,512]{3,2,1,0:T(8,128)(2,1)S(1)}, u32[]{:S(2)}, u32[]{:S(2)}) collective-permute-start(bf16[4,2,16,512]{3,2,1,0:T(8,128)(2,1)S(1)} %collective-permute-done.16.refs_10_), channel_id=1, source_target_pairs={{0,1},{1,0},{2,3},{3,2},{4,5},{5,4},{6,7},{7,6},{8,9},{9,8},{10,11... | collective-permute-start | bytes 393224 | tf_op jit(solution)/shard_map/ppermute | solution.py:23
  151.0 8.4 %collective-permute-start.20 = (bf16[64,2176]{1,0:T(8,128)(2,1)}, bf16[64,2176]{1,0:T(8,128)(2,1)S(1)}, u32[]{:S(2)}, u32[]{:S(2)}) collective-permute-start(bf16[64,2176]{1,0:T(8,128)(2,1)} %get-tuple-element.100), channel_id=1, source_target_pairs={{0,8},{8,0},{1,9},{9,1},{2,10},{10,2},{3,11},{11,3},{4,12},{12,4},... | collective-permute-start | bytes 835592 | tf_op jit(solution)/shard_map/ppermute | solution.py:23
  151.3 8.7 %collective-permute-start.21 = (bf16[64,2176]{1,0:T(8,128)(2,1)}, bf16[64,2176]{1,0:T(8,128)(2,1)S(1)}, u32[]{:S(2)}, u32[]{:S(2)}) collective-permute-start(bf16[64,2176]{1,0:T(8,128)(2,1)} %get-tuple-element.107), channel_id=1, source_target_pairs={{0,6},{2,0},{4,2},{6,4},{1,7},{3,1},{5,3},{7,5},{8,14},{10,8},{12,... | collective-permute-start | bytes 835592 | tf_op jit(solution)/shard_map/ppermute | solution.py:23
  154.0 9.1 %collective-permute-start.22 = (bf16[64,2176]{1,0:T(8,128)(2,1)}, bf16[64,2176]{1,0:T(8,128)(2,1)S(1)}, u32[]{:S(2)}, u32[]{:S(2)}) collective-permute-start(bf16[64,2176]{1,0:T(8,128)(2,1)} %get-tuple-element.108), channel_id=1, source_target_pairs={{0,2},{2,4},{4,6},{6,0},{1,3},{3,5},{5,7},{7,1},{8,10},{10,12},{12... | collective-permute-start | bytes 835592 | tf_op jit(solution)/shard_map/ppermute | solution.py:23
  159.4 3.6 %copy-start.15 = (bf16[64,2176]{1,0:T(8,128)(2,1)}, bf16[64,2176]{1,0:T(8,128)(2,1)S(1)}, u32[]{:S(2)}) copy-start(bf16[64,2176]{1,0:T(8,128)(2,1)S(1)} %collective-permute-done.20.g0) | copy-start | bytes 835588
  160.1 3.0 %copy-start.16 = (bf16[64,2176]{1,0:T(8,128)(2,1)}, bf16[64,2176]{1,0:T(8,128)(2,1)S(1)}, u32[]{:S(2)}) copy-start(bf16[64,2176]{1,0:T(8,128)(2,1)S(1)} %collective-permute-done.21.g1) | copy-start | bytes 835588
  166.1 18.9 %collective-permute-start.23 = (bf16[192,2176]{1,0:T(8,128)(2,1)}, bf16[192,2176]{1,0:T(8,128)(2,1)S(1)}, u32[]{:S(2)}, u32[]{:S(2)}) collective-permute-start(bf16[192,2176]{1,0:T(8,128)(2,1)} %get-tuple-element.119), channel_id=1, source_target_pairs={{0,6},{2,0},{4,2},{6,4},{1,7},{3,1},{5,3},{7,5},{8,14},{10,8},{12,... | collective-permute-start | bytes 2506760 | tf_op jit(solution)/shard_map/ppermute | solution.py:23
  166.5 18.9 %collective-permute-start.24 = (bf16[192,2176]{1,0:T(8,128)(2,1)}, bf16[192,2176]{1,0:T(8,128)(2,1)S(1)}, u32[]{:S(2)}, u32[]{:S(2)}) collective-permute-start(bf16[192,2176]{1,0:T(8,128)(2,1)} %get-tuple-element.120), channel_id=1, source_target_pairs={{0,8},{8,0},{1,9},{9,1},{2,10},{10,2},{3,11},{11,3},{4,12},{12,4},... | collective-permute-start | bytes 2506760 | tf_op jit(solution)/shard_map/ppermute | solution.py:23
  167.7 19.9 %collective-permute-start.25 = (bf16[192,2176]{1,0:T(8,128)(2,1)}, bf16[192,2176]{1,0:T(8,128)(2,1)S(1)}, u32[]{:S(2)}, u32[]{:S(2)}) collective-permute-start(bf16[192,2176]{1,0:T(8,128)(2,1)} %get-tuple-element.109), channel_id=1, source_target_pairs={{0,2},{2,4},{4,6},{6,0},{1,3},{3,5},{5,7},{7,1},{8,10},{10,12},{12... | collective-permute-start | bytes 2506760 | tf_op jit(solution)/shard_map/ppermute | solution.py:23
  184.7 21.0 %collective-permute-start.27 = (bf16[192,2176]{1,0:T(8,128)(2,1)}, bf16[192,2176]{1,0:T(8,128)(2,1)S(1)}, u32[]{:S(2)}, u32[]{:S(2)}) collective-permute-start(bf16[192,2176]{1,0:T(8,128)(2,1)} %get-tuple-element.122), channel_id=1, source_target_pairs={{0,2},{2,4},{4,6},{6,0},{1,3},{3,5},{5,7},{7,1},{8,10},{10,12},{12... | collective-permute-start | bytes 2506760 | tf_op jit(solution)/shard_map/ppermute | solution.py:23
  185.1 2.5 %copy-start.11 = (bf16[192,2176]{1,0:T(8,128)(2,1)}, bf16[192,2176]{1,0:T(8,128)(2,1)S(1)}, u32[]{:S(2)}) copy-start(bf16[192,2176]{1,0:T(8,128)(2,1)S(1)} %collective-permute-done.23.r0) | copy-start | bytes 2506756
  185.5 2.1 copy-start.12
  188.5 4.6 %copy-start.22 = (s32[6,32]{1,0:T(8,128)S(1)}, s32[6,32]{1,0:T(8,128)}, u32[]{:S(2)}) copy-start(s32[6,32]{1,0:T(8,128)} %param.14) | copy-start | bytes 2308
  191.9 17.0 %collective-permute-start.26 = (bf16[192,2176]{1,0:T(8,128)(2,1)}, bf16[192,2176]{1,0:T(8,128)(2,1)S(1)}, u32[]{:S(2)}, u32[]{:S(2)}) collective-permute-start(bf16[192,2176]{1,0:T(8,128)(2,1)} %get-tuple-element.121), channel_id=1, source_target_pairs={{0,6},{2,0},{4,2},{6,4},{1,7},{3,1},{5,3},{7,5},{8,14},{10,8},{12,... | collective-permute-start | bytes 2506760 | tf_op jit(solution)/shard_map/ppermute | solution.py:23
  192.4 17.4 %collective-permute-start.28 = (bf16[192,2176]{1,0:T(8,128)(2,1)}, bf16[192,2176]{1,0:T(8,128)(2,1)S(1)}, u32[]{:S(2)}, u32[]{:S(2)}) collective-permute-start(bf16[192,2176]{1,0:T(8,128)(2,1)} %get-tuple-element.123), channel_id=1, source_target_pairs={{0,8},{8,0},{1,9},{9,1},{2,10},{10,2},{3,11},{11,3},{4,12},{12,4},... | collective-permute-start | bytes 2506760 | tf_op jit(solution)/shard_map/ppermute | solution.py:23
  205.7 4.0 %copy-start.8 = (bf16[192,2176]{1,0:T(8,128)(2,1)}, bf16[192,2176]{1,0:T(8,128)(2,1)S(1)}, u32[]{:S(2)}) copy-start(bf16[192,2176]{1,0:T(8,128)(2,1)S(1)} %collective-permute-done.27.m1) | copy-start | bytes 2506756
  210.7 18.4 %copy-start.23 = (s32[1024]{0:T(1024)S(1)}, s32[1024]{0:T(1024)}, u32[]{:S(2)}) copy-start(s32[1024]{0:T(1024)} %param.15) | copy-start | bytes 12292
  216.4 22.9 %all-to-all-start.3 = ((f32[128,1,256]{2,1,0:T(1,128)}), f32[128,1,256]{2,1,0:T(1,128)S(1)}, u32[]{:S(2)}, u32[]{:S(2)}) async-start(f32[128,1,256]{2,1,0:T(1,128)} %get-tuple-element.125), calls=%async_computation.3 | async-start | bytes 262144 | tf_op jit(solution)/shard_map/all_to_all | solution.py:672
  (16 other events, 14.5 us)

commit v4 on v3

--- a/solution.py
+++ b/solution.py
@@ -414,25 +414,23 @@
     )(got, acc, den, *ff, w_mine, w_their)
 
 
-def thirds_body(t0, t1, t2, o0, o1, o2):
+def halves_body(t0, t1, o0, o1):
     o0[...] = t0[...]
     o1[...] = t1[...]
-    o2[...] = t2[...]
-
-
-def thirds_of(arrays):
-    rows, width = arrays[0].shape
-    third = rows // 3
-    block = lambda at: pl.BlockSpec((third, width), lambda i: (at, 0))
-    return pl.pallas_call(
-        thirds_body,
+
+
+def halves_of(first, second):
+    rows, width = first.shape
+    block = lambda at: pl.BlockSpec((rows // 2, width), lambda i: (at, 0))
+    return pl.pallas_call(
+        halves_body,
         grid=(1,),
-        in_specs=[block(0), block(1), block(2)],
-        out_specs=[block(0)] * 3,
-        out_shape=[jax.ShapeDtypeStruct((third, width), BF16)] * 3,
+        in_specs=[block(0), block(1)],
+        out_specs=[block(0)] * 2,
+        out_shape=[jax.ShapeDtypeStruct((rows // 2, width), BF16)] * 2,
         cost_estimate=cost(0, 4 * rows * width),
-        name="thirds",
-    )(*arrays)
+        name="halves",
+    )(first, second)
 
 
 def far_body(t0, t1, t2, g0, g1, g2, o0, o1, o2):
@@ -604,8 +602,8 @@
     their_edge0 = swap_core(edge0)
     their_qkv0 = swap_core(qkv0)
     s_aa, s_pa, s_pb = after(qkv0, (s_aa, s_pa, s_pb))
-    h_aa, h_pa, h_pb = thirds_of((s_aa, s_pa, s_pb))
-    far = (swap_x(h_aa), up_z(h_pa), down_z(h_pb))
+    h_pa, h_pb = halves_of(s_pa, s_pb)
+    far = (up_z(h_pa), down_z(h_pb))
     away = after(their_qkv0, (s_aa, s_pa, s_pb, *far))
     qkv1, edge1, got1 = columns(away)
     back = attend_columns(0, after(qkv1, got0))

time: 243 us -> 232 us (0.955)
  waiting for transfers between devices: 72 us -> 59.5 us
    ppermute x27 -> x26, waiting for transfers between devices: 55.7 us -> 43 us  [permuted(): return lax.ppermute(array, axis, [(i, (i + by) % n) for i in range(n)])]
    ppermute x27 -> x26, starting transfers between devices: 27.8 us -> 29.6 us  [permuted(): return lax.ppermute(array, axis, [(i, (i + by) % n) for i in range(n)])]
    unnamed x63 -> x61, local copies, waits for them, and re-layouts: 8.93 us -> 8.94 us
  transfers between devices with their start and end apart: 33 -> 32, of which waited for: 17 -> 17; matrix products, arithmetic and copies ran while one was open for 1% -> 1% of each run, Pallas kernels for 29% -> 33%
where the time goes in v4:
time: 232 us; the launch traced here: 231 us
  Pallas kernels  89.8 us (39%)
  starting transfers between devices  68.5 us (30%)
  waiting for transfers between devices  59.5 us (26%)
  local copies, waits for them, and re-layouts  10.6 us (5%)
    ppermute x26, waiting for transfers between devices, permuted(): return lax.ppermute(array, axis, [(i, (i + by) % n) for i in range(n)])  43 us
    ppermute x26, starting transfers between devices, permuted(): return lax.ppermute(array, axis, [(i, (i + by) % n) for i in range(n)])  29.6 us
    pallas_call x3, Pallas kernels, feed_forward(): pl.pallas_call(lambda *refs: forward_body(n, slots, slots == 4, *refs), i...  27.7 us
    pallas_call x3, Pallas kernels, terms(): pl.pallas_call(lambda *refs: term_body(hs, rows, splits, *refs), grid=(1,...  13.4 us
    pallas_call x2, Pallas kernels, project(): pl.pallas_call(lambda *refs: project_body(rows, n, *refs), grid=(3,), in_...  13.1 us
    all_to_all x2, starting transfers between devices, columns(): lax.all_to_all(qkv.reshape(row_peers, rows * HALF, 6 * hs), ROW, split_ax...  13 us
    all_to_all x1, starting transfers between devices, per_device(): lax.all_to_all(line, ALL, split_axis=0, concat_axis=0, tiled=True)  12.5 us
    all_to_all x1, waiting for transfers between devices, per_device(): lax.all_to_all(line, ALL, split_axis=0, concat_axis=0, tiled=True)  9.59 us
  transfers between devices with their start and end apart: 32, of which 17 were waited for; matrix products, arithmetic and copies ran while one was open for 1% of the time, Pallas kernels for 33%

profile of v4, /device:TPU:1, one launch (start us, length us, event | category | flops | bytes accessed | tf_op | source)
XLA Modules:
  0.0 231.3 jit_solution(5150606063322440089)
XLA Ops:
  0.6 1.5 collective-permute-start.1
  2.6 2.3 %normalize.1.refs_0_ = bf16[192,2048]{1,0:T(8,128)(2,1)} custom-call(bf16[192,2048]{1,0:T(8,128)(2,1)} %bitcast.19, f32[1,2048]{1,0:T(1,128)} %bitcast.25), custom_call_target="tpu_custom_call" | custom-call | flops 1966080 | bytes 1572864 | tf_op jit(solution)/shard_map/normalize/pallas_call | solution.py:78
  4.9 1.7 collective-permute-start.4
  6.7 2.1 collective-permute-start.5
  8.8 1.2 collective-permute-start.6
  10.1 5.7 %feed_forward.3.refs_3_ = bf16[192,2176]{1,0:T(8,128)(2,1)} custom-call(bf16[192,2048]{1,0:T(8,128)(2,1)} %normalize.1.refs_0_, bf16[2048,512]{1,0:T(8,128)(2,1)} %refs_3_.3, bf16[2048,512]{1,0:T(8,128)(2,1)} %copy-done.6, bf16[512,2048]{1,0:T(8,128)(2,1)} %refs_5_.5, bf16[512,2048]{1,0:T(8,128)(2,1)} %collective-permute-done.2.refs_4_.refs_8_.refs_6_), custom_call_target="tpu_custom_call" | custom-call | flops 1610612736 | bytes 9961472 | tf_op jit(solution)/shard_map/feed_forward/pallas_call | solution.py:208
  15.8 11.1 %collective-permute-done.4.refs_1_.refs_0_ = bf16[192,2048]{1,0:T(8,128)(2,1)} collective-permute-done((bf16[192,2048]{1,0:T(8,128)(2,1)}, bf16[192,2048]{1,0:T(8,128)(2,1)}, u32[]{:S(2)}, u32[]{:S(2)}) %collective-permute-start.4) | collective-permute-done | bytes 786464 | tf_op jit(solution)/shard_map/ppermute | solution.py:23
  27.8 1.2 collective-permute-start.9
  29.1 2.7 %collective-permute-start.10 = (bf16[192,2048]{1,0:T(8,128)(2,1)}, bf16[192,2048]{1,0:T(8,128)(2,1)}, u32[]{:S(2)}, u32[]{:S(2)}) collective-permute-start(bf16[192,2048]{1,0:T(8,128)(2,1)} %collective-permute-done.6.refs_3_.refs_2_), channel_id=1, source_target_pairs={{0,6},{2,0},{4,2},{6,4},{1,7},{3,1},{5,3},{7,5},{8,14},{10,8},{12,... | collective-permute-start | bytes 2359304 | tf_op jit(solution)/shard_map/ppermute | solution.py:23
  31.7 6.4 %project.2 = (bf16[4,2,6,16,768]{4,3,2,1,0:T(8,128)(2,1)}, bf16[4,2,16,512]{3,2,1,0:T(8,128)(2,1)}) custom-call(bf16[192,2048]{1,0:T(8,128)(2,1)} %normalize.1.refs_0_, bf16[192,2048]{1,0:T(8,128)(2,1)} %collective-permute-done.4.refs_1_.refs_0_, bf16[192,2048]{1,0:T(8,128)(2,1)} %copy-done.26, bf16[192,2048]{1,0:T(8,128)(2,1)} %collective-permute-done.6.refs_3_.refs_2_, ...), custom_call_target="tpu_custom_call" | custom-call | flops 2415919104 | bytes 6291456 | tf_op jit(solution)/shard_map/project/pallas_call | solution.py:108
  38.1 2.1 collective-permute-start.7
  40.2 6.4 %all-to-all-start = ((bf16[8,96,768]{2,1,0:T(8,128)(2,1)}), bf16[8,96,768]{2,1,0:T(8,128)(2,1)S(1)}, u32[]{:S(2)}, u32[]{:S(2)}) async-start(bf16[8,96,768]{2,1,0:T(8,128)(2,1)} %bitcast.17), calls=%async_computation | async-start | bytes 2359296 | tf_op jit(solution)/shard_map/all_to_all | solution.py:591
  48.1 2.0 halves.1
  50.2 2.7 %collective-permute-start.12 = (bf16[96,2048]{1,0:T(8,128)(2,1)}, bf16[96,2048]{1,0:T(8,128)(2,1)S(1)}, u32[]{:S(2)}, u32[]{:S(2)}) collective-permute-start(bf16[96,2048]{1,0:T(8,128)(2,1)} %get-tuple-element.69), channel_id=1, source_target_pairs={{0,6},{2,0},{4,2},{6,4},{1,7},{3,1},{5,3},{7,5},{8,14},{10,8},{12,... | collective-permute-start | bytes 1179656 | tf_op jit(solution)/shard_map/ppermute | solution.py:23
  52.8 7.0 %collective-permute-done.11.refs_3_ = bf16[96,2048]{1,0:T(8,128)(2,1)S(1)} collective-permute-done((bf16[96,2048]{1,0:T(8,128)(2,1)}, bf16[96,2048]{1,0:T(8,128)(2,1)S(1)}, u32[]{:S(2)}, u32[]{:S(2)}) %collective-permute-start.11) | collective-permute-done | bytes 393248 | tf_op jit(solution)/shard_map/ppermute | solution.py:23
  60.7 6.7 %project.3 = (bf16[4,2,6,16,768]{4,3,2,1,0:T(8,128)(2,1)}, bf16[4,2,16,512]{3,2,1,0:T(8,128)(2,1)}) custom-call(bf16[192,2048]{1,0:T(8,128)(2,1)} %collective-permute-done.8.refs_0_, bf16[192,2048]{1,0:T(8,128)(2,1)} %copy-done.14, bf16[192,2048]{1,0:T(8,128)(2,1)} %collective-permute-done.10.t1.refs_2_, bf16[96,2048]{1,0:T(8,128)(2,1)} %copy-done.27, ...), custom_call_target="tpu_custom_call" | custom-call | flops 2415919104 | bytes 6291456 | tf_op jit(solution)/shard_map/project/pallas_call | solution.py:108
  67.4 3.4 %collective-permute-start.13 = (bf16[4,2,6,16,768]{4,3,2,1,0:T(8,128)(2,1)}, bf16[4,2,6,16,768]{4,3,2,1,0:T(8,128)(2,1)S(1)}, u32[]{:S(2)}, u32[]{:S(2)}) collective-permute-start(bf16[4,2,6,16,768]{4,3,2,1,0:T(8,128)(2,1)} %get-tuple-element.75.refs_4_), channel_id=1, source_target_pairs={{0,1},{1,0},{2,3},{3,2},{4,5},{5,4},{6,7},{7,6},{8,9},{9,8},{10,11... | collective-permute-start | bytes 3538952 | tf_op jit(solution)/shard_map/ppermute | solution.py:23
  70.8 1.0 copy-done.7
  71.9 6.7 %all-to-all-start.1 = ((bf16[8,96,768]{2,1,0:T(8,128)(2,1)}), bf16[8,96,768]{2,1,0:T(8,128)(2,1)S(1)}, u32[]{:S(2)}, u32[]{:S(2)}) async-start(bf16[8,96,768]{2,1,0:T(8,128)(2,1)} %bitcast.18), calls=%async_computation.1 | async-start | bytes 2359296 | tf_op jit(solution)/shard_map/all_to_all | solution.py:591
  79.9 4.1 %column_attention.2.refs_3_ = bf16[8,2,7,16,256]{4,3,2,1,0:T(8,128)(2,1)} custom-call(f32[1]{0:T(128)S(6)} %copy.32.refs_0_, f32[1]{0:T(128)} %collective-permute-done.refs_1_, bf16[48,16,768]{2,1,0:T(8,128)(2,1)} %bitcast.21), custom_call_target="tpu_custom_call" | custom-call | flops 452984832 | bytes 1572864 | tf_op jit(solution)/shard_map/column_attention/pallas_call | solution.py:343
  84.0 11.6 %feed_forward.4 = (bf16[192,2176]{1,0:T(8,128)(2,1)}, bf16[192,2176]{1,0:T(8,128)(2,1)}, bf16[192,2176]{1,0:T(8,128)(2,1)}, bf16[192,2176]{1,0:T(8,128)(2,1)}) custom-call(bf16[192,2048]{1,0:T(8,128)(2,1)} %collective-permute-done.8.refs_0_, bf16[192,2048]{1,0:T(8,128)(2,1)} %copy-done.14, bf16[192,2048]{1,0:T(8,128)(2,1)} %collective-permute-done.10.t1.refs_2_, ...), custom_call_target="tpu_custom_call" | custom-call | flops 6442450944 | bytes 14680064 | tf_op jit(solution)/shard_map/feed_forward/pallas_call | solution.py:208
  95.7 1.0 copy-done.1
  96.7 4.1 %column_attention.3 = bf16[8,2,7,16,256]{4,3,2,1,0:T(8,128)(2,1)} custom-call(f32[1]{0:T(128)S(6)} %copy.32.refs_0_, f32[1]{0:T(128)} %collective-permute-done.refs_1_, bf16[48,16,768]{2,1,0:T(8,128)(2,1)} %bitcast.16, bf16[8,2,7,16,256]{4,3,2,1,0:T(8,128)(2,1)} %column_attention.2.refs_3_), custom_call_target="tpu_custom_call", output_to_operand_aliasing={{}: (3, {})} | custom-call | flops 452984832 | bytes 1572864 | tf_op jit(solution)/shard_map/column_attention/pallas_call | solution.py:343
  100.8 7.0 %all-to-all-start.2 = ((bf16[8,2,7,16,256]{4,3,2,1,0:T(8,128)(2,1)}), bf16[8,2,7,16,256]{4,3,2,1,0:T(8,128)(2,1)S(1)}, u32[]{:S(2)}, u32[]{:S(2)}) async-start(bf16[8,2,7,16,256]{4,3,2,1,0:T(8,128)(2,1)} %column_attention.3), calls=%async_computation.2 | async-start | bytes 1835008 | tf_op jit(solution)/shard_map/all_to_all | solution.py:615
  107.8 3.4 %collective-permute-start.14 = (bf16[4,2,16,512]{3,2,1,0:T(8,128)(2,1)S(1)}, bf16[4,2,16,512]{3,2,1,0:T(8,128)(2,1)S(1)}, u32[]{:S(2)}, u32[]{:S(2)}) collective-permute-start(bf16[4,2,16,512]{3,2,1,0:T(8,128)(2,1)S(1)} %copy-done.29), channel_id=1, source_target_pairs={{0,16},{16,32},{32,48},{48,64},{64,80},{80,96},{96,112},{1,17},{17... | collective-permute-start | bytes 393224 | tf_op jit(solution)/shard_map/ppermute | solution.py:44
  111.2 3.1 %collective-permute-start.15 = (bf16[4,2,16,512]{3,2,1,0:T(8,128)(2,1)}, bf16[4,2,16,512]{3,2,1,0:T(8,128)(2,1)S(1)}, u32[]{:S(2)}, u32[]{:S(2)}) collective-permute-start(bf16[4,2,16,512]{3,2,1,0:T(8,128)(2,1)} %get-tuple-element.89), channel_id=1, source_target_pairs={{0,16},{16,32},{32,48},{48,64},{64,80},{80,96},{96,112},{1,17},{17... | collective-permute-start | bytes 393224 | tf_op jit(solution)/shard_map/ppermute | solution.py:44
  114.4 5.9 %collective-permute-done.14.refs_9_ = bf16[4,2,16,512]{3,2,1,0:T(8,128)(2,1)S(1)} collective-permute-done((bf16[4,2,16,512]{3,2,1,0:T(8,128)(2,1)S(1)}, bf16[4,2,16,512]{3,2,1,0:T(8,128)(2,1)S(1)}, u32[]{:S(2)}, u32[]{:S(2)}) %collective-permute-start.14) | collective-permute-done | bytes 131104 | tf_op jit(solution)/shard_map/ppermute | solution.py:44
  120.2 2.1 collective-permute-start.16
  123.3 1.2 collective-permute-start.17
  126.8 9.4 %row_attention.1 = (bf16[4,2,6,16,256]{4,3,2,1,0:T(8,128)(2,1)}, bf16[4,2,6,16,256]{4,3,2,1,0:T(8,128)(2,1)}, f32[4,2,6,16,256]{4,3,2,1,0:T(8,128)}, f32[4,2,6,16,256]{4,3,2,1,0:T(8,128)}) custom-call(s32[1]{0:T(128)} %bitcast.6.refs_0_, s32[256,1]{1,0:T(8,128)} %add.135.refs_1_, s32[1,512]{1,0:T(1,128)} %bitcast.27, ...), custom_call_target="tpu_custom_call" | custom-call | flops 1610612736 | bytes 6291456 | tf_op jit(solution)/shard_map/row_attention/pallas_call | solution.py:281
  137.4 3.1 %terms.3 = (bf16[64,2176]{1,0:T(8,128)(2,1)}, bf16[64,2176]{1,0:T(8,128)(2,1)}, bf16[64,2176]{1,0:T(8,128)(2,1)}) custom-call(bf16[8,2,7,16,256]{4,3,2,1,0:T(8,128)(2,1)} %copy-done, bf16[4,2,6,16,256]{4,3,2,1,0:T(8,128)(2,1)} %get-tuple-element.96.refs_1_, f32[4,2,6,16,256]{4,3,2,1,0:T(8,128)} %get-tuple-element.97.refs_2_, ...), custom_call_target="tpu_custom_call" | custom-call | flops 213909504 | bytes 2088960 | tf_op jit(solution)/shard_map/terms/pallas_call | solution.py:399
  140.8 2.6 %collective-permute-start.20 = (bf16[64,2176]{1,0:T(8,128)(2,1)}, bf16[64,2176]{1,0:T(8,128)(2,1)S(1)}, u32[]{:S(2)}, u32[]{:S(2)}) collective-permute-start(bf16[64,2176]{1,0:T(8,128)(2,1)} %get-tuple-element.101), channel_id=1, source_target_pairs={{0,6},{2,0},{4,2},{6,4},{1,7},{3,1},{5,3},{7,5},{8,14},{10,8},{12,... | collective-permute-start | bytes 835592 | tf_op jit(solution)/shard_map/ppermute | solution.py:23
  143.4 4.7 %terms.4 = (bf16[192,2176]{1,0:T(8,128)(2,1)}, bf16[192,2176]{1,0:T(8,128)(2,1)}, bf16[192,2176]{1,0:T(8,128)(2,1)}) custom-call(bf16[8,2,7,16,256]{4,3,2,1,0:T(8,128)(2,1)} %copy-done, bf16[4,2,6,16,256]{4,3,2,1,0:T(8,128)(2,1)} %get-tuple-element.96.refs_1_, f32[4,2,6,16,256]{4,3,2,1,0:T(8,128)} %get-tuple-element.97.refs_2_, ...), custom_call_target="tpu_custom_call" | custom-call | flops 641728512 | bytes 6266880 | tf_op jit(solution)/shard_map/terms/pallas_call | solution.py:399
  149.4 3.0 %collective-permute-done.21.g2 = bf16[64,2176]{1,0:T(8,128)(2,1)S(1)} collective-permute-done((bf16[64,2176]{1,0:T(8,128)(2,1)}, bf16[64,2176]{1,0:T(8,128)(2,1)S(1)}, u32[]{:S(2)}, u32[]{:S(2)}) %collective-permute-start.21) | collective-permute-done | bytes 278560 | tf_op jit(solution)/shard_map/ppermute | solution.py:23
  153.2 2.3 %add_far.1 = (bf16[192,2176]{1,0:T(8,128)(2,1)}, bf16[192,2176]{1,0:T(8,128)(2,1)}, bf16[192,2176]{1,0:T(8,128)(2,1)}) custom-call(bf16[192,2176]{1,0:T(8,128)(2,1)} %get-tuple-element.98.t0, bf16[192,2176]{1,0:T(8,128)(2,1)} %get-tuple-element.99.t1, ...), custom_call_target="tpu_custom_call", output_to_operand_aliasing={{0}: (0, {}), {1}: (1, {}), {2}: (2, {})} | custom-call | flops 835584 | bytes 2506752 | tf_op jit(solution)/shard_map/add_far/pallas_call | solution.py:445
  155.9 1.2 collective-permute-start.23
  157.0 1.1 collective-permute-start.24
  158.1 10.4 %feed_forward.5 = (bf16[192,2176]{1,0:T(8,128)(2,1)}, bf16[192,2176]{1,0:T(8,128)(2,1)}, bf16[192,2176]{1,0:T(8,128)(2,1)}) custom-call(bf16[192,2048]{1,0:T(8,128)(2,1)} %collective-permute-done.4.refs_1_.refs_0_, bf16[192,2048]{1,0:T(8,128)(2,1)} %copy-done.26, bf16[192,2048]{1,0:T(8,128)(2,1)} %collective-permute-done.6.refs_3_.refs_2_, ...), custom_call_target="tpu_custom_call" | custom-call | flops 4831838208 | bytes 13107200 | tf_op jit(solution)/shard_map/feed_forward/pallas_call | solution.py:208
  168.6 5.6 %terms.5 = (bf16[192,2176]{1,0:T(8,128)(2,1)}, bf16[192,2176]{1,0:T(8,128)(2,1)}, bf16[192,2176]{1,0:T(8,128)(2,1)}, bf16[192,2176]{1,0:T(8,128)(2,1)}) custom-call(bf16[8,2,7,16,256]{4,3,2,1,0:T(8,128)(2,1)} %copy-done, bf16[4,2,6,16,256]{4,3,2,1,0:T(8,128)(2,1)} %get-tuple-element.90.refs_1_, f32[4,2,6,16,256]{4,3,2,1,0:T(8,128)} %get-tuple-element.91.refs_2_, ...), custom_call_target="tpu_custom_call" | custom-call | flops 855638016 | bytes 8355840 | tf_op jit(solution)/shard_map/terms/pallas_call | solution.py:399
  174.8 2.1 collective-permute-done.24.r2
  177.8 3.5 %add_near.1 = (bf16[192,2176]{1,0:T(8,128)(2,1)}, bf16[192,2176]{1,0:T(8,128)(2,1)}) custom-call(bf16[192,2176]{1,0:T(8,128)(2,1)} %get-tuple-element.111.t0, bf16[192,2176]{1,0:T(8,128)(2,1)} %get-tuple-element.112.t1, bf16[192,2176]{1,0:T(8,128)(2,1)} %copy-done.11, bf16[192,2176]{1,0:T(8,128)(2,1)} %copy-done.12, bf16[192,2176]{1,0:T(8,128)(2,1)} %copy-done.13), custom_call_target="tpu_custom_call" | custom-call | flops 1253376 | bytes 5849088 | tf_op jit(solution)/shard_map/add_near/pallas_call | solution.py:464
  183.2 11.9 %collective-permute-done.26.m1 = bf16[192,2176]{1,0:T(8,128)(2,1)S(1)} collective-permute-done((bf16[192,2176]{1,0:T(8,128)(2,1)}, bf16[192,2176]{1,0:T(8,128)(2,1)S(1)}, u32[]{:S(2)}, u32[]{:S(2)}) %collective-permute-start.26) | collective-permute-done | bytes 835616 | tf_op jit(solution)/shard_map/ppermute | solution.py:23
  195.0 3.3 %collective-permute-done.25.m0 = bf16[192,2176]{1,0:T(8,128)(2,1)S(1)} collective-permute-done((bf16[192,2176]{1,0:T(8,128)(2,1)}, bf16[192,2176]{1,0:T(8,128)(2,1)S(1)}, u32[]{:S(2)}, u32[]{:S(2)}) %collective-permute-start.25) | collective-permute-done | bytes 835616 | tf_op jit(solution)/shard_map/ppermute | solution.py:23
  198.3 1.0 collective-permute-done.27.m2
  200.2 5.7 %head.1 = (bf16[192,2048]{1,0:T(8,128)(2,1)}, f32[128,1,256]{2,1,0:T(1,128)}) custom-call(bf16[192,2048]{1,0:T(8,128)(2,1)} %bitcast.20, bf16[192,2176]{1,0:T(8,128)(2,1)} %get-tuple-element.110.mine, bf16[192,2176]{1,0:T(8,128)(2,1)} %copy-done.9, bf16[192,2176]{1,0:T(8,128)(2,1)} %copy-done.8, bf16[192,2176]{1,0:T(8,128)(2,1)} %copy-done.10, ...), custom_call_target="tpu_custom_call" | custom-call | tf_op jit(solution)/shard_map/head/pallas_call | solution.py:502
  205.9 12.5 %all-to-all-start.3 = ((f32[128,1,256]{2,1,0:T(1,128)}), f32[128,1,256]{2,1,0:T(1,128)S(1)}, u32[]{:S(2)}, u32[]{:S(2)}) async-start(f32[128,1,256]{2,1,0:T(1,128)} %get-tuple-element.119), calls=%async_computation.3 | async-start | bytes 262144 | tf_op jit(solution)/shard_map/all_to_all | solution.py:670
  219.0 9.6 %all-to-all-done.3 = f32[128,1,256]{2,1,0:T(1,128)S(1)} async-done(((f32[128,1,256]{2,1,0:T(1,128)}), f32[128,1,256]{2,1,0:T(1,128)S(1)}, u32[]{:S(2)}, u32[]{:S(2)}) %all-to-all-start.3) | async-done | bytes 131104 | tf_op jit(solution)/shard_map/all_to_all | solution.py:670
  229.2 2.1 pick.1
  (104 shorter events, 17.6 us)
Async XLA Ops:
  0.6 8.2 %collective-permute-start.1 = (bf16[2048,512]{1,0:T(8,128)(2,1)}, bf16[2048,512]{1,0:T(8,128)(2,1)S(1)}, u32[]{:S(2)}, u32[]{:S(2)}) collective-permute-start(bf16[2048,512]{1,0:T(8,128)(2,1)} %refs_3_.3), channel_id=1, source_target_pairs={{0,1},{1,0},{2,3},{3,2},{4,5},{5,4},{6,7},{7,6},{8,9},{9,8},{10,11... | collective-permute-start | bytes 6291464 | tf_op jit(solution)/shard_map/ppermute | solution.py:23
  2.1 7.9 %collective-permute-start.2 = (bf16[512,2048]{1,0:T(8,128)(2,1)}, bf16[512,2048]{1,0:T(8,128)(2,1)}, u32[]{:S(2)}, u32[]{:S(2)}) collective-permute-start(bf16[512,2048]{1,0:T(8,128)(2,1)} %refs_5_.5), channel_id=1, source_target_pairs={{0,1},{1,0},{2,3},{3,2},{4,5},{5,4},{6,7},{7,6},{8,9},{9,8},{10,11... | collective-permute-start | bytes 6291464 | tf_op jit(solution)/shard_map/ppermute | solution.py:23
  2.2 25.7 %collective-permute-start.3 = (bf16[3,2048,128]{2,1,0:T(8,128)(2,1)}, bf16[3,2048,128]{2,1,0:T(8,128)(2,1)}, u32[]{:S(2)}, u32[]{:S(2)}) collective-permute-start(bf16[3,2048,128]{2,1,0:T(8,128)(2,1)} %refs_5_.3), channel_id=1, source_target_pairs={{0,1},{1,0},{2,3},{3,2},{4,5},{5,4},{6,7},{7,6},{8,9},{9,8},{10,11... | collective-permute-start | bytes 4718600 | tf_op jit(solution)/shard_map/ppermute | solution.py:23
  4.9 22.0 %collective-permute-start.4 = (bf16[192,2048]{1,0:T(8,128)(2,1)}, bf16[192,2048]{1,0:T(8,128)(2,1)}, u32[]{:S(2)}, u32[]{:S(2)}) collective-permute-start(bf16[192,2048]{1,0:T(8,128)(2,1)} %normalize.1.refs_0_), channel_id=1, source_target_pairs={{0,2},{2,4},{4,6},{6,0},{1,3},{3,5},{5,7},{7,1},{8,10},{10,12},{12... | collective-permute-start | bytes 2359304 | tf_op jit(solution)/shard_map/ppermute | solution.py:23
  6.7 20.3 %collective-permute-start.5 = (bf16[192,2048]{1,0:T(8,128)(2,1)}, bf16[192,2048]{1,0:T(8,128)(2,1)S(1)}, u32[]{:S(2)}, u32[]{:S(2)}) collective-permute-start(bf16[192,2048]{1,0:T(8,128)(2,1)} %normalize.1.refs_0_), channel_id=1, source_target_pairs={{0,6},{2,0},{4,2},{6,4},{1,7},{3,1},{5,3},{7,5},{8,14},{10,8},{12,... | collective-permute-start | bytes 2359304 | tf_op jit(solution)/shard_map/ppermute | solution.py:23
  8.8 19.0 %collective-permute-start.6 = (bf16[192,2048]{1,0:T(8,128)(2,1)}, bf16[192,2048]{1,0:T(8,128)(2,1)}, u32[]{:S(2)}, u32[]{:S(2)}) collective-permute-start(bf16[192,2048]{1,0:T(8,128)(2,1)} %normalize.1.refs_0_), channel_id=1, source_target_pairs={{0,8},{8,0},{1,9},{9,1},{2,10},{10,2},{3,11},{11,3},{4,12},{12,4},... | collective-permute-start | bytes 2359304 | tf_op jit(solution)/shard_map/ppermute | solution.py:23
  26.9 4.8 %copy-start.26 = (bf16[192,2048]{1,0:T(8,128)(2,1)}, bf16[192,2048]{1,0:T(8,128)(2,1)S(1)}, u32[]{:S(2)}) copy-start(bf16[192,2048]{1,0:T(8,128)(2,1)S(1)} %collective-permute-done.5.refs_2_.refs_1_) | copy-start | bytes 2359300
  27.8 19.4 %collective-permute-start.8 = (bf16[192,2048]{1,0:T(8,128)(2,1)}, bf16[192,2048]{1,0:T(8,128)(2,1)}, u32[]{:S(2)}, u32[]{:S(2)}) collective-permute-start(bf16[192,2048]{1,0:T(8,128)(2,1)} %collective-permute-done.4.refs_1_.refs_0_), channel_id=1, source_target_pairs={{0,2},{2,4},{4,6},{6,0},{1,3},{3,5},{5,7},{7,1},{8,10},{10,12},{12... | collective-permute-start | bytes 2359304 | tf_op jit(solution)/shard_map/ppermute | solution.py:23
  27.8 19.4 %collective-permute-start.9 = (bf16[192,2048]{1,0:T(8,128)(2,1)}, bf16[192,2048]{1,0:T(8,128)(2,1)S(1)}, u32[]{:S(2)}, u32[]{:S(2)}) collective-permute-start(bf16[192,2048]{1,0:T(8,128)(2,1)} %collective-permute-done.4.refs_1_.refs_0_), channel_id=1, source_target_pairs={{0,8},{8,0},{1,9},{9,1},{2,10},{10,2},{3,11},{11,3},{4,12},{12,4},... | collective-permute-start | bytes 2359304 | tf_op jit(solution)/shard_map/ppermute | solution.py:23
  29.1 18.2 %collective-permute-start.10 = (bf16[192,2048]{1,0:T(8,128)(2,1)}, bf16[192,2048]{1,0:T(8,128)(2,1)}, u32[]{:S(2)}, u32[]{:S(2)}) collective-permute-start(bf16[192,2048]{1,0:T(8,128)(2,1)} %collective-permute-done.6.refs_3_.refs_2_), channel_id=1, source_target_pairs={{0,6},{2,0},{4,2},{6,4},{1,7},{3,1},{5,3},{7,5},{8,14},{10,8},{12,... | collective-permute-start | bytes 2359304 | tf_op jit(solution)/shard_map/ppermute | solution.py:23
  38.1 21.7 %collective-permute-start.7 = (bf16[4,2,6,16,768]{4,3,2,1,0:T(8,128)(2,1)}, bf16[4,2,6,16,768]{4,3,2,1,0:T(8,128)(2,1)S(1)}, u32[]{:S(2)}, u32[]{:S(2)}) collective-permute-start(bf16[4,2,6,16,768]{4,3,2,1,0:T(8,128)(2,1)} %get-tuple-element.64.refs_3_), channel_id=1, source_target_pairs={{0,1},{1,0},{2,3},{3,2},{4,5},{5,4},{6,7},{7,6},{8,9},{9,8},{10,11... | collective-permute-start | bytes 3538952 | tf_op jit(solution)/shard_map/ppermute | solution.py:23
  40.2 30.6 %all-to-all-start = ((bf16[8,96,768]{2,1,0:T(8,128)(2,1)}), bf16[8,96,768]{2,1,0:T(8,128)(2,1)S(1)}, u32[]{:S(2)}, u32[]{:S(2)}) async-start(bf16[8,96,768]{2,1,0:T(8,128)(2,1)} %bitcast.17), calls=%async_computation | async-start | bytes 2359296 | tf_op jit(solution)/shard_map/all_to_all | solution.py:591
  50.2 9.6 %collective-permute-start.11 = (bf16[96,2048]{1,0:T(8,128)(2,1)}, bf16[96,2048]{1,0:T(8,128)(2,1)S(1)}, u32[]{:S(2)}, u32[]{:S(2)}) collective-permute-start(bf16[96,2048]{1,0:T(8,128)(2,1)} %get-tuple-element.68), channel_id=1, source_target_pairs={{0,2},{2,4},{4,6},{6,0},{1,3},{3,5},{5,7},{7,1},{8,10},{10,12},{12... | collective-permute-start | bytes 1179656 | tf_op jit(solution)/shard_map/ppermute | solution.py:23
  50.2 9.6 %collective-permute-start.12 = (bf16[96,2048]{1,0:T(8,128)(2,1)}, bf16[96,2048]{1,0:T(8,128)(2,1)S(1)}, u32[]{:S(2)}, u32[]{:S(2)}) collective-permute-start(bf16[96,2048]{1,0:T(8,128)(2,1)} %get-tuple-element.69), channel_id=1, source_target_pairs={{0,6},{2,0},{4,2},{6,4},{1,7},{3,1},{5,3},{7,5},{8,14},{10,8},{12,... | collective-permute-start | bytes 1179656 | tf_op jit(solution)/shard_map/ppermute | solution.py:23
  60.7 6.7 %copy-start.4 = (bf16[4,2,6,16,768]{4,3,2,1,0:T(8,128)(2,1)}, bf16[4,2,6,16,768]{4,3,2,1,0:T(8,128)(2,1)S(1)}, u32[]{:S(2)}) copy-start(bf16[4,2,6,16,768]{4,3,2,1,0:T(8,128)(2,1)S(1)} %collective-permute-done.7.refs_5_.refs_6_) | copy-start | bytes 3538948
  67.4 11.4 %copy-start.2 = (bf16[128,2048]{1,0:T(8,128)(2,1)S(1)}, bf16[128,2048]{1,0:T(8,128)(2,1)}, u32[]{:S(2)}) copy-start(bf16[128,2048]{1,0:T(8,128)(2,1)} %refs_7_.3) | copy-start | bytes 1572868
  67.4 12.4 %copy-start.24 = (s32[8]{0:T(128)S(1)}, s32[8]{0:T(128)}, u32[]{:S(2)}) copy-start(s32[8]{0:T(128)} %constant.117.clone) | copy-start | bytes 100
  67.4 12.4 %copy-start.25 = (s32[8]{0:T(128)S(1)}, s32[8]{0:T(128)}, u32[]{:S(2)}) copy-start(s32[8]{0:T(128)} %constant.118.clone) | copy-start | bytes 100
  67.4 28.3 %collective-permute-start.13 = (bf16[4,2,6,16,768]{4,3,2,1,0:T(8,128)(2,1)}, bf16[4,2,6,16,768]{4,3,2,1,0:T(8,128)(2,1)S(1)}, u32[]{:S(2)}, u32[]{:S(2)}) collective-permute-start(bf16[4,2,6,16,768]{4,3,2,1,0:T(8,128)(2,1)} %get-tuple-element.75.refs_4_), channel_id=1, source_target_pairs={{0,1},{1,0},{2,3},{3,2},{4,5},{5,4},{6,7},{7,6},{8,9},{9,8},{10,11... | collective-permute-start | bytes 3538952 | tf_op jit(solution)/shard_map/ppermute | solution.py:23
  71.9 23.8 %all-to-all-start.1 = ((bf16[8,96,768]{2,1,0:T(8,128)(2,1)}), bf16[8,96,768]{2,1,0:T(8,128)(2,1)S(1)}, u32[]{:S(2)}, u32[]{:S(2)}) async-start(bf16[8,96,768]{2,1,0:T(8,128)(2,1)} %bitcast.18), calls=%async_computation.1 | async-start | bytes 2359296 | tf_op jit(solution)/shard_map/all_to_all | solution.py:591
  78.5 1.4 collective-permute-start
  78.8 57.4 %collective-permute-start.18 = (bf16[128,2048]{1,0:T(8,128)(2,1)S(1)}, bf16[128,2048]{1,0:T(8,128)(2,1)S(1)}, u32[]{:S(2)}, u32[]{:S(2)}) collective-permute-start(bf16[128,2048]{1,0:T(8,128)(2,1)S(1)} %copy-done.2), channel_id=1, source_target_pairs={{0,1},{1,0},{2,3},{3,2},{4,5},{5,4},{6,7},{7,6},{8,9},{9,8},{10,11... | collective-permute-start | bytes 1572872 | tf_op jit(solution)/shard_map/ppermute | solution.py:23
  95.7 5.1 %copy-start.5 = (bf16[4,2,6,16,768]{4,3,2,1,0:T(8,128)(2,1)}, bf16[4,2,6,16,768]{4,3,2,1,0:T(8,128)(2,1)S(1)}, u32[]{:S(2)}) copy-start(bf16[4,2,6,16,768]{4,3,2,1,0:T(8,128)(2,1)S(1)} %collective-permute-done.13.refs_7_.refs_8_) | copy-start | bytes 3538948
  100.8 7.0 %copy-start.29 = (bf16[4,2,16,512]{3,2,1,0:T(8,128)(2,1)S(1)}, bf16[4,2,16,512]{3,2,1,0:T(8,128)(2,1)}, u32[]{:S(2)}) copy-start(bf16[4,2,16,512]{3,2,1,0:T(8,128)(2,1)} %get-tuple-element.88) | copy-start | bytes 393220
  100.8 35.4 %all-to-all-start.2 = ((bf16[8,2,7,16,256]{4,3,2,1,0:T(8,128)(2,1)}), bf16[8,2,7,16,256]{4,3,2,1,0:T(8,128)(2,1)S(1)}, u32[]{:S(2)}, u32[]{:S(2)}) async-start(bf16[8,2,7,16,256]{4,3,2,1,0:T(8,128)(2,1)} %column_attention.3), calls=%async_computation.2 | async-start | bytes 1835008 | tf_op jit(solution)/shard_map/all_to_all | solution.py:615
  107.8 12.4 %collective-permute-start.14 = (bf16[4,2,16,512]{3,2,1,0:T(8,128)(2,1)S(1)}, bf16[4,2,16,512]{3,2,1,0:T(8,128)(2,1)S(1)}, u32[]{:S(2)}, u32[]{:S(2)}) collective-permute-start(bf16[4,2,16,512]{3,2,1,0:T(8,128)(2,1)S(1)} %copy-done.29), channel_id=1, source_target_pairs={{0,16},{16,32},{32,48},{48,64},{64,80},{80,96},{96,112},{1,17},{17... | collective-permute-start | bytes 393224 | tf_op jit(solution)/shard_map/ppermute | solution.py:44
  111.2 12.1 %collective-permute-start.15 = (bf16[4,2,16,512]{3,2,1,0:T(8,128)(2,1)}, bf16[4,2,16,512]{3,2,1,0:T(8,128)(2,1)S(1)}, u32[]{:S(2)}, u32[]{:S(2)}) collective-permute-start(bf16[4,2,16,512]{3,2,1,0:T(8,128)(2,1)} %get-tuple-element.89), channel_id=1, source_target_pairs={{0,16},{16,32},{32,48},{48,64},{64,80},{80,96},{96,112},{1,17},{17... | collective-permute-start | bytes 393224 | tf_op jit(solution)/shard_map/ppermute | solution.py:44
  120.2 5.9 %copy-start.18 = (bf16[4,2,16,512]{3,2,1,0:T(8,128)(2,1)}, bf16[4,2,16,512]{3,2,1,0:T(8,128)(2,1)S(1)}, u32[]{:S(2)}) copy-start(bf16[4,2,16,512]{3,2,1,0:T(8,128)(2,1)S(1)} %collective-permute-done.14.refs_9_) | copy-start | bytes 393220
  120.2 5.8 %collective-permute-start.16 = (bf16[4,2,16,512]{3,2,1,0:T(8,128)(2,1)S(1)}, bf16[4,2,16,512]{3,2,1,0:T(8,128)(2,1)S(1)}, u32[]{:S(2)}, u32[]{:S(2)}) collective-permute-start(bf16[4,2,16,512]{3,2,1,0:T(8,128)(2,1)S(1)} %collective-permute-done.14.refs_9_), channel_id=1, source_target_pairs={{0,1},{1,0},{2,3},{3,2},{4,5},{5,4},{6,7},{7,6},{8,9},{9,8},{10,11... | collective-permute-start | bytes 393224 | tf_op jit(solution)/shard_map/ppermute | solution.py:23
  123.3 2.8 %copy-start.19 = (bf16[4,2,16,512]{3,2,1,0:T(8,128)(2,1)}, bf16[4,2,16,512]{3,2,1,0:T(8,128)(2,1)S(1)}, u32[]{:S(2)}) copy-start(bf16[4,2,16,512]{3,2,1,0:T(8,128)(2,1)S(1)} %collective-permute-done.15.refs_10_) | copy-start | bytes 393220
  123.3 2.8 %collective-permute-start.17 = (bf16[4,2,16,512]{3,2,1,0:T(8,128)(2,1)S(1)}, bf16[4,2,16,512]{3,2,1,0:T(8,128)(2,1)S(1)}, u32[]{:S(2)}, u32[]{:S(2)}) collective-permute-start(bf16[4,2,16,512]{3,2,1,0:T(8,128)(2,1)S(1)} %collective-permute-done.15.refs_10_), channel_id=1, source_target_pairs={{0,1},{1,0},{2,3},{3,2},{4,5},{5,4},{6,7},{7,6},{8,9},{9,8},{10,11... | collective-permute-start | bytes 393224 | tf_op jit(solution)/shard_map/ppermute | solution.py:23
  140.5 8.4 %collective-permute-start.19 = (bf16[64,2176]{1,0:T(8,128)(2,1)}, bf16[64,2176]{1,0:T(8,128)(2,1)S(1)}, u32[]{:S(2)}, u32[]{:S(2)}) collective-permute-start(bf16[64,2176]{1,0:T(8,128)(2,1)} %get-tuple-element.94), channel_id=1, source_target_pairs={{0,8},{8,0},{1,9},{9,1},{2,10},{10,2},{3,11},{11,3},{4,12},{12,4},... | collective-permute-start | bytes 835592 | tf_op jit(solution)/shard_map/ppermute | solution.py:23
  140.8 8.6 %collective-permute-start.20 = (bf16[64,2176]{1,0:T(8,128)(2,1)}, bf16[64,2176]{1,0:T(8,128)(2,1)S(1)}, u32[]{:S(2)}, u32[]{:S(2)}) collective-permute-start(bf16[64,2176]{1,0:T(8,128)(2,1)} %get-tuple-element.101), channel_id=1, source_target_pairs={{0,6},{2,0},{4,2},{6,4},{1,7},{3,1},{5,3},{7,5},{8,14},{10,8},{12,... | collective-permute-start | bytes 835592 | tf_op jit(solution)/shard_map/ppermute | solution.py:23
  143.4 9.1 %collective-permute-start.21 = (bf16[64,2176]{1,0:T(8,128)(2,1)}, bf16[64,2176]{1,0:T(8,128)(2,1)S(1)}, u32[]{:S(2)}, u32[]{:S(2)}) collective-permute-start(bf16[64,2176]{1,0:T(8,128)(2,1)} %get-tuple-element.102), channel_id=1, source_target_pairs={{0,2},{2,4},{4,6},{6,0},{1,3},{3,5},{5,7},{7,1},{8,10},{10,12},{12... | collective-permute-start | bytes 835592 | tf_op jit(solution)/shard_map/ppermute | solution.py:23
  148.9 3.5 %copy-start.15 = (bf16[64,2176]{1,0:T(8,128)(2,1)}, bf16[64,2176]{1,0:T(8,128)(2,1)S(1)}, u32[]{:S(2)}) copy-start(bf16[64,2176]{1,0:T(8,128)(2,1)S(1)} %collective-permute-done.19.g0) | copy-start | bytes 835588
  149.4 3.0 %copy-start.16 = (bf16[64,2176]{1,0:T(8,128)(2,1)}, bf16[64,2176]{1,0:T(8,128)(2,1)S(1)}, u32[]{:S(2)}) copy-start(bf16[64,2176]{1,0:T(8,128)(2,1)S(1)} %collective-permute-done.20.g1) | copy-start | bytes 835588
  155.5 18.9 %collective-permute-start.22 = (bf16[192,2176]{1,0:T(8,128)(2,1)}, bf16[192,2176]{1,0:T(8,128)(2,1)S(1)}, u32[]{:S(2)}, u32[]{:S(2)}) collective-permute-start(bf16[192,2176]{1,0:T(8,128)(2,1)} %get-tuple-element.113), channel_id=1, source_target_pairs={{0,6},{2,0},{4,2},{6,4},{1,7},{3,1},{5,3},{7,5},{8,14},{10,8},{12,... | collective-permute-start | bytes 2506760 | tf_op jit(solution)/shard_map/ppermute | solution.py:23
  155.9 18.9 %collective-permute-start.23 = (bf16[192,2176]{1,0:T(8,128)(2,1)}, bf16[192,2176]{1,0:T(8,128)(2,1)S(1)}, u32[]{:S(2)}, u32[]{:S(2)}) collective-permute-start(bf16[192,2176]{1,0:T(8,128)(2,1)} %get-tuple-element.114), channel_id=1, source_target_pairs={{0,8},{8,0},{1,9},{9,1},{2,10},{10,2},{3,11},{11,3},{4,12},{12,4},... | collective-permute-start | bytes 2506760 | tf_op jit(solution)/shard_map/ppermute | solution.py:23
  157.0 19.9 %collective-permute-start.24 = (bf16[192,2176]{1,0:T(8,128)(2,1)}, bf16[192,2176]{1,0:T(8,128)(2,1)S(1)}, u32[]{:S(2)}, u32[]{:S(2)}) collective-permute-start(bf16[192,2176]{1,0:T(8,128)(2,1)} %get-tuple-element.103), channel_id=1, source_target_pairs={{0,2},{2,4},{4,6},{6,0},{1,3},{3,5},{5,7},{7,1},{8,10},{10,12},{12... | collective-permute-start | bytes 2506760 | tf_op jit(solution)/shard_map/ppermute | solution.py:23
  174.2 20.9 %collective-permute-start.26 = (bf16[192,2176]{1,0:T(8,128)(2,1)}, bf16[192,2176]{1,0:T(8,128)(2,1)S(1)}, u32[]{:S(2)}, u32[]{:S(2)}) collective-permute-start(bf16[192,2176]{1,0:T(8,128)(2,1)} %get-tuple-element.116), channel_id=1, source_target_pairs={{0,2},{2,4},{4,6},{6,0},{1,3},{3,5},{5,7},{7,1},{8,10},{10,12},{12... | collective-permute-start | bytes 2506760 | tf_op jit(solution)/shard_map/ppermute | solution.py:23
  174.5 2.5 %copy-start.11 = (bf16[192,2176]{1,0:T(8,128)(2,1)}, bf16[192,2176]{1,0:T(8,128)(2,1)S(1)}, u32[]{:S(2)}) copy-start(bf16[192,2176]{1,0:T(8,128)(2,1)S(1)} %collective-permute-done.22.r0) | copy-start | bytes 2506756
  174.8 2.1 copy-start.12
  177.8 4.6 %copy-start.22 = (s32[6,32]{1,0:T(8,128)S(1)}, s32[6,32]{1,0:T(8,128)}, u32[]{:S(2)}) copy-start(s32[6,32]{1,0:T(8,128)} %param.14) | copy-start | bytes 2308
  181.3 17.0 %collective-permute-start.25 = (bf16[192,2176]{1,0:T(8,128)(2,1)}, bf16[192,2176]{1,0:T(8,128)(2,1)S(1)}, u32[]{:S(2)}, u32[]{:S(2)}) collective-permute-start(bf16[192,2176]{1,0:T(8,128)(2,1)} %get-tuple-element.115), channel_id=1, source_target_pairs={{0,6},{2,0},{4,2},{6,4},{1,7},{3,1},{5,3},{7,5},{8,14},{10,8},{12,... | collective-permute-start | bytes 2506760 | tf_op jit(solution)/shard_map/ppermute | solution.py:23
  181.8 17.5 %collective-permute-start.27 = (bf16[192,2176]{1,0:T(8,128)(2,1)}, bf16[192,2176]{1,0:T(8,128)(2,1)S(1)}, u32[]{:S(2)}, u32[]{:S(2)}) collective-permute-start(bf16[192,2176]{1,0:T(8,128)(2,1)} %get-tuple-element.117), channel_id=1, source_target_pairs={{0,8},{8,0},{1,9},{9,1},{2,10},{10,2},{3,11},{11,3},{4,12},{12,4},... | collective-permute-start | bytes 2506760 | tf_op jit(solution)/shard_map/ppermute | solution.py:23
  195.0 4.3 %copy-start.8 = (bf16[192,2176]{1,0:T(8,128)(2,1)}, bf16[192,2176]{1,0:T(8,128)(2,1)S(1)}, u32[]{:S(2)}) copy-start(bf16[192,2176]{1,0:T(8,128)(2,1)S(1)} %collective-permute-done.26.m1) | copy-start | bytes 2506756
  200.2 18.2 %copy-start.23 = (s32[1024]{0:T(1024)S(1)}, s32[1024]{0:T(1024)}, u32[]{:S(2)}) copy-start(s32[1024]{0:T(1024)} %param.15) | copy-start | bytes 12292
  205.9 22.7 %all-to-all-start.3 = ((f32[128,1,256]{2,1,0:T(1,128)}), f32[128,1,256]{2,1,0:T(1,128)S(1)}, u32[]{:S(2)}, u32[]{:S(2)}) async-start(f32[128,1,256]{2,1,0:T(1,128)} %get-tuple-element.119), calls=%async_computation.3 | async-start | bytes 262144 | tf_op jit(solution)/shard_map/all_to_all | solution.py:670
  (14 other events, 12.7 us)

commit v5 on v4

--- a/solution.py
+++ b/solution.py
@@ -581,9 +581,20 @@
     def ffn(shards, slots):
         return feed_forward(shards, slots, up_weight, their_up, down_weight, their_down)
 
+    xl, z, core = lax.axis_index(XL), lax.axis_index(Z), lax.axis_index(CORE)
+    n_z = lax.axis_size(Z)
+    shift_x = jnp.array([0, 0, 0, 1, 0, 1, 1, 1], jnp.int32)
+    shift_z = jnp.array([0, 3, 1, 0, 2, 3, 1, 2], jnp.int32)
+    chip = ((xl + shift_x) % 2) * n_z + (z + shift_z) % n_z
+    starts = chip * 2 * cols
+    offs = jnp.arange(cols, dtype=jnp.int32)
+    mine = (starts[:, None] + core * cols + offs[None, :]).reshape(-1)
+    theirs = (starts[:, None] + (1 - core) * cols + offs[None, :]).reshape(-1)
+    columns_of = (mine[:, None], jnp.concatenate([mine, theirs])[None, :])
+
     near = (up_z(own), down_z(own), swap_x(own))
     (ff_own,) = ffn((own,), 1)
-    s_a, s_b, s_p = after((ff_own, their_project), near)
+    s_a, s_b, s_p = after((ff_own, their_project, columns_of), near)
     s_aa, s_pb, s_pa = up_z(s_a), down_z(s_p), swap_x(s_a)
 
     def columns(shards):
@@ -614,20 +625,10 @@
     back = attend_columns(1, after((ff1, their_qkv1), got1), back)
     again = lax.all_to_all(back, ROW, split_axis=0, concat_axis=0, tiled=True)
 
-    xl, z, core = lax.axis_index(XL), lax.axis_index(Z), lax.axis_index(CORE)
-    n_z = lax.axis_size(Z)
-    shift_x = jnp.array([0, 0, 0, 1, 0, 1, 1, 1], jnp.int32)
-    shift_z = jnp.array([0, 3, 1, 0, 2, 3, 1, 2], jnp.int32)
-    chip = ((xl + shift_x) % 2) * n_z + (z + shift_z) % n_z
-    starts = chip * 2 * cols
-    offs = jnp.arange(cols, dtype=jnp.int32)
-    mine = (starts[:, None] + core * cols + offs[None, :]).reshape(-1)
-    theirs = (starts[:, None] + (1 - core) * cols + offs[None, :]).reshape(-1)
     top = (lax.axis_index(ROW) == 0).astype(jnp.int32)[None]
     acc, den = row_attention(
         after(back, top),
-        mine[:, None],
-        jnp.concatenate([mine, theirs])[None, :],
+        *columns_of,
         (qkv0, qkv1),
         (their_qkv0, their_qkv1),
         (edge0, edge1),

time: 232 us -> 232 us (level)
    unnamed x61 -> x63, local copies, waits for them, and re-layouts: 8.94 us -> 9.2 us
  transfers between devices with their start and end apart: 32 -> 32, of which waited for: 17 -> 18; matrix products, arithmetic and copies ran while one was open for 1% -> 1% of each run, Pallas kernels for 33% -> 31%
where the time goes in v5:
time: 232 us; the launch traced here: 231 us
  Pallas kernels  89.6 us (39%)
  starting transfers between devices  69.2 us (30%)
  waiting for transfers between devices  58.4 us (25%)
  local copies, waits for them, and re-layouts  11 us (5%)
    ppermute x26, waiting for transfers between devices, permuted(): return lax.ppermute(array, axis, [(i, (i + by) % n) for i in range(n)])  42.9 us
    ppermute x26, starting transfers between devices, permuted(): return lax.ppermute(array, axis, [(i, (i + by) % n) for i in range(n)])  29.9 us
    pallas_call x3, Pallas kernels, feed_forward(): pl.pallas_call(lambda *refs: forward_body(n, slots, slots == 4, *refs), i...  27.7 us
    pallas_call x3, Pallas kernels, terms(): pl.pallas_call(lambda *refs: term_body(hs, rows, splits, *refs), grid=(1,...  13.4 us
    pallas_call x2, Pallas kernels, project(): pl.pallas_call(lambda *refs: project_body(rows, n, *refs), grid=(3,), in_...  13 us
    all_to_all x2, starting transfers between devices, columns(): lax.all_to_all(qkv.reshape(row_peers, rows * HALF, 6 * hs), ROW, split_ax...  13 us
    all_to_all x1, starting transfers between devices, per_device(): lax.all_to_all(line, ALL, split_axis=0, concat_axis=0, tiled=True)  12.6 us
    all_to_all x1, waiting for transfers between devices, per_device(): lax.all_to_all(line, ALL, split_axis=0, concat_axis=0, tiled=True)  9.59 us
  transfers between devices with their start and end apart: 32, of which 18 were waited for; matrix products, arithmetic and copies ran while one was open for 1% of the time, Pallas kernels for 31%

profile of v5, /device:TPU:1, one launch (start us, length us, event | category | flops | bytes accessed | tf_op | source)
XLA Modules:
  0.0 231.1 jit_solution(5088788234631900996)
XLA Ops:
  0.7 1.5 collective-permute-start.1
  2.6 2.3 %normalize.1.refs_0_ = bf16[192,2048]{1,0:T(8,128)(2,1)} custom-call(bf16[192,2048]{1,0:T(8,128)(2,1)} %bitcast.19, f32[1,2048]{1,0:T(1,128)} %bitcast.24), custom_call_target="tpu_custom_call" | custom-call | flops 1966080 | bytes 1572864 | tf_op jit(solution)/shard_map/normalize/pallas_call | solution.py:78
  4.9 1.7 collective-permute-start.4
  6.7 2.1 collective-permute-start.5
  8.9 1.3 collective-permute-start.6
  11.1 5.7 %feed_forward.3.refs_3_ = bf16[192,2176]{1,0:T(8,128)(2,1)} custom-call(bf16[192,2048]{1,0:T(8,128)(2,1)} %normalize.1.refs_0_, bf16[2048,512]{1,0:T(8,128)(2,1)} %refs_3_.3, bf16[2048,512]{1,0:T(8,128)(2,1)} %copy-done.6, bf16[512,2048]{1,0:T(8,128)(2,1)} %refs_5_.5, bf16[512,2048]{1,0:T(8,128)(2,1)} %collective-permute-done.2.refs_4_.refs_8_.refs_6_), custom_call_target="tpu_custom_call" | custom-call | flops 1610612736 | bytes 9961472 | tf_op jit(solution)/shard_map/feed_forward/pallas_call | solution.py:208
  16.8 10.1 %collective-permute-done.4.refs_1_.refs_0_ = bf16[192,2048]{1,0:T(8,128)(2,1)} collective-permute-done((bf16[192,2048]{1,0:T(8,128)(2,1)}, bf16[192,2048]{1,0:T(8,128)(2,1)}, u32[]{:S(2)}, u32[]{:S(2)}) %collective-permute-start.4) | collective-permute-done | bytes 786464 | tf_op jit(solution)/shard_map/ppermute | solution.py:23
  27.0 1.0 collective-permute-done.6.refs_3_.refs_2_
  28.0 1.3 collective-permute-start.9
  29.3 2.6 %collective-permute-start.10 = (bf16[192,2048]{1,0:T(8,128)(2,1)}, bf16[192,2048]{1,0:T(8,128)(2,1)S(1)}, u32[]{:S(2)}, u32[]{:S(2)}) collective-permute-start(bf16[192,2048]{1,0:T(8,128)(2,1)} %collective-permute-done.6.refs_3_.refs_2_), channel_id=1, source_target_pairs={{0,6},{2,0},{4,2},{6,4},{1,7},{3,1},{5,3},{7,5},{8,14},{10,8},{12,... | collective-permute-start | bytes 2359304 | tf_op jit(solution)/shard_map/ppermute | solution.py:23
  31.9 6.3 %project.2 = (bf16[4,2,6,16,768]{4,3,2,1,0:T(8,128)(2,1)}, bf16[4,2,16,512]{3,2,1,0:T(8,128)(2,1)}) custom-call(bf16[192,2048]{1,0:T(8,128)(2,1)} %normalize.1.refs_0_, bf16[192,2048]{1,0:T(8,128)(2,1)} %collective-permute-done.4.refs_1_.refs_0_, bf16[192,2048]{1,0:T(8,128)(2,1)} %copy-done.26, bf16[192,2048]{1,0:T(8,128)(2,1)} %collective-permute-done.6.refs_3_.refs_2_, ...), custom_call_target="tpu_custom_call" | custom-call | flops 2415919104 | bytes 6291456 | tf_op jit(solution)/shard_map/project/pallas_call | solution.py:108
  38.2 2.1 collective-permute-start.7
  40.3 6.4 %all-to-all-start = ((bf16[8,96,768]{2,1,0:T(8,128)(2,1)}), bf16[8,96,768]{2,1,0:T(8,128)(2,1)}, u32[]{:S(2)}, u32[]{:S(2)}) async-start(bf16[8,96,768]{2,1,0:T(8,128)(2,1)} %bitcast.17), calls=%async_computation | async-start | bytes 2359296 | tf_op jit(solution)/shard_map/all_to_all | solution.py:602
  49.2 2.0 halves.1
  51.2 2.7 %collective-permute-start.12 = (bf16[96,2048]{1,0:T(8,128)(2,1)}, bf16[96,2048]{1,0:T(8,128)(2,1)S(1)}, u32[]{:S(2)}, u32[]{:S(2)}) collective-permute-start(bf16[96,2048]{1,0:T(8,128)(2,1)} %get-tuple-element.69), channel_id=1, source_target_pairs={{0,6},{2,0},{4,2},{6,4},{1,7},{3,1},{5,3},{7,5},{8,14},{10,8},{12,... | collective-permute-start | bytes 1179656 | tf_op jit(solution)/shard_map/ppermute | solution.py:23
  53.9 7.1 %collective-permute-done.11.refs_3_ = bf16[96,2048]{1,0:T(8,128)(2,1)S(1)} collective-permute-done((bf16[96,2048]{1,0:T(8,128)(2,1)}, bf16[96,2048]{1,0:T(8,128)(2,1)S(1)}, u32[]{:S(2)}, u32[]{:S(2)}) %collective-permute-start.11) | collective-permute-done | bytes 393248 | tf_op jit(solution)/shard_map/ppermute | solution.py:23
  61.8 6.7 %project.3 = (bf16[4,2,6,16,768]{4,3,2,1,0:T(8,128)(2,1)}, bf16[4,2,16,512]{3,2,1,0:T(8,128)(2,1)}) custom-call(bf16[192,2048]{1,0:T(8,128)(2,1)} %collective-permute-done.8.refs_0_, bf16[192,2048]{1,0:T(8,128)(2,1)} %copy-done.13, bf16[192,2048]{1,0:T(8,128)(2,1)} %copy-done.14, bf16[96,2048]{1,0:T(8,128)(2,1)} %copy-done.27, bf16[96,2048]{1,0:T(8,128)(2,1)} %copy-done.28, ...), custom_call_target="tpu_custom_call" | custom-call | flops 2415919104 | bytes 6291456 | tf_op jit(solution)/shard_map/project/pallas_call | solution.py:108
  68.6 3.3 %collective-permute-start.13 = (bf16[4,2,6,16,768]{4,3,2,1,0:T(8,128)(2,1)}, bf16[4,2,6,16,768]{4,3,2,1,0:T(8,128)(2,1)S(1)}, u32[]{:S(2)}, u32[]{:S(2)}) collective-permute-start(bf16[4,2,6,16,768]{4,3,2,1,0:T(8,128)(2,1)} %get-tuple-element.75.refs_4_), channel_id=1, source_target_pairs={{0,1},{1,0},{2,3},{3,2},{4,5},{5,4},{6,7},{7,6},{8,9},{9,8},{10,11... | collective-permute-start | bytes 3538952 | tf_op jit(solution)/shard_map/ppermute | solution.py:23
  71.9 6.7 %all-to-all-start.1 = ((bf16[8,96,768]{2,1,0:T(8,128)(2,1)}), bf16[8,96,768]{2,1,0:T(8,128)(2,1)S(1)}, u32[]{:S(2)}, u32[]{:S(2)}) async-start(bf16[8,96,768]{2,1,0:T(8,128)(2,1)} %bitcast.18), calls=%async_computation.1 | async-start | bytes 2359296 | tf_op jit(solution)/shard_map/all_to_all | solution.py:602
  79.9 4.1 %column_attention.2.refs_3_ = bf16[8,2,7,16,256]{4,3,2,1,0:T(8,128)(2,1)} custom-call(f32[1]{0:T(128)S(6)} %copy.32.refs_0_, f32[1]{0:T(128)} %collective-permute-done.refs_1_, bf16[48,16,768]{2,1,0:T(8,128)(2,1)} %bitcast.4.refs_2_), custom_call_target="tpu_custom_call" | custom-call | flops 452984832 | bytes 1572864 | tf_op jit(solution)/shard_map/column_attention/pallas_call | solution.py:343
  84.0 11.6 %feed_forward.4 = (bf16[192,2176]{1,0:T(8,128)(2,1)}, bf16[192,2176]{1,0:T(8,128)(2,1)}, bf16[192,2176]{1,0:T(8,128)(2,1)}, bf16[192,2176]{1,0:T(8,128)(2,1)}) custom-call(bf16[192,2048]{1,0:T(8,128)(2,1)} %collective-permute-done.8.refs_0_, bf16[192,2048]{1,0:T(8,128)(2,1)} %copy-done.13, bf16[192,2048]{1,0:T(8,128)(2,1)} %copy-done.14, ...), custom_call_target="tpu_custom_call" | custom-call | flops 6442450944 | bytes 14680064 | tf_op jit(solution)/shard_map/feed_forward/pallas_call | solution.py:208
  95.7 1.0 copy-done.1
  96.7 4.0 %column_attention.3 = bf16[8,2,7,16,256]{4,3,2,1,0:T(8,128)(2,1)} custom-call(f32[1]{0:T(128)S(6)} %copy.32.refs_0_, f32[1]{0:T(128)} %collective-permute-done.refs_1_, bf16[48,16,768]{2,1,0:T(8,128)(2,1)} %bitcast.16, bf16[8,2,7,16,256]{4,3,2,1,0:T(8,128)(2,1)} %column_attention.2.refs_3_), custom_call_target="tpu_custom_call", output_to_operand_aliasing={{}: (3, {})} | custom-call | flops 452984832 | bytes 1572864 | tf_op jit(solution)/shard_map/column_attention/pallas_call | solution.py:343
  100.7 7.1 %all-to-all-start.2 = ((bf16[8,2,7,16,256]{4,3,2,1,0:T(8,128)(2,1)}), bf16[8,2,7,16,256]{4,3,2,1,0:T(8,128)(2,1)S(1)}, u32[]{:S(2)}, u32[]{:S(2)}) async-start(bf16[8,2,7,16,256]{4,3,2,1,0:T(8,128)(2,1)} %column_attention.3), calls=%async_computation.2 | async-start | bytes 1835008 | tf_op jit(solution)/shard_map/all_to_all | solution.py:626
  108.5 3.6 %collective-permute-start.14 = (bf16[4,2,16,512]{3,2,1,0:T(8,128)(2,1)S(1)}, bf16[4,2,16,512]{3,2,1,0:T(8,128)(2,1)S(1)}, u32[]{:S(2)}, u32[]{:S(2)}) collective-permute-start(bf16[4,2,16,512]{3,2,1,0:T(8,128)(2,1)S(1)} %copy-done.29), channel_id=1, source_target_pairs={{0,16},{16,32},{32,48},{48,64},{64,80},{80,96},{96,112},{1,17},{17... | collective-permute-start | bytes 393224 | tf_op jit(solution)/shard_map/ppermute | solution.py:44
  112.1 3.1 %collective-permute-start.15 = (bf16[4,2,16,512]{3,2,1,0:T(8,128)(2,1)S(1)}, bf16[4,2,16,512]{3,2,1,0:T(8,128)(2,1)S(1)}, u32[]{:S(2)}, u32[]{:S(2)}) collective-permute-start(bf16[4,2,16,512]{3,2,1,0:T(8,128)(2,1)S(1)} %copy-done.30), channel_id=1, source_target_pairs={{0,16},{16,32},{32,48},{48,64},{64,80},{80,96},{96,112},{1,17},{17... | collective-permute-start | bytes 393224 | tf_op jit(solution)/shard_map/ppermute | solution.py:44
  115.2 5.1 %collective-permute-done.14.refs_9_ = bf16[4,2,16,512]{3,2,1,0:T(8,128)(2,1)S(1)} collective-permute-done((bf16[4,2,16,512]{3,2,1,0:T(8,128)(2,1)S(1)}, bf16[4,2,16,512]{3,2,1,0:T(8,128)(2,1)S(1)}, u32[]{:S(2)}, u32[]{:S(2)}) %collective-permute-start.14) | collective-permute-done | bytes 131104 | tf_op jit(solution)/shard_map/ppermute | solution.py:44
  120.2 2.1 collective-permute-start.16
  123.2 1.2 collective-permute-start.17
  126.5 9.4 %row_attention.1 = (bf16[4,2,6,16,256]{4,3,2,1,0:T(8,128)(2,1)}, bf16[4,2,6,16,256]{4,3,2,1,0:T(8,128)(2,1)}, f32[4,2,6,16,256]{4,3,2,1,0:T(8,128)}, f32[4,2,6,16,256]{4,3,2,1,0:T(8,128)}) custom-call(s32[1]{0:T(128)} %bitcast.7.refs_0_, s32[256,1]{1,0:T(8,128)} %copy.23.refs_1_, s32[1,512]{1,0:T(1,128)} %bitcast.26, ...), custom_call_target="tpu_custom_call" | custom-call | flops 1610612736 | bytes 6291456 | tf_op jit(solution)/shard_map/row_attention/pallas_call | solution.py:281
  137.1 3.1 %terms.3 = (bf16[64,2176]{1,0:T(8,128)(2,1)}, bf16[64,2176]{1,0:T(8,128)(2,1)}, bf16[64,2176]{1,0:T(8,128)(2,1)}) custom-call(bf16[8,2,7,16,256]{4,3,2,1,0:T(8,128)(2,1)} %copy-done, bf16[4,2,6,16,256]{4,3,2,1,0:T(8,128)(2,1)} %get-tuple-element.96.refs_1_, f32[4,2,6,16,256]{4,3,2,1,0:T(8,128)} %get-tuple-element.97.refs_2_, ...), custom_call_target="tpu_custom_call" | custom-call | flops 213909504 | bytes 2088960 | tf_op jit(solution)/shard_map/terms/pallas_call | solution.py:399
  140.5 2.6 %collective-permute-start.20 = (bf16[64,2176]{1,0:T(8,128)(2,1)}, bf16[64,2176]{1,0:T(8,128)(2,1)S(1)}, u32[]{:S(2)}, u32[]{:S(2)}) collective-permute-start(bf16[64,2176]{1,0:T(8,128)(2,1)} %get-tuple-element.101), channel_id=1, source_target_pairs={{0,6},{2,0},{4,2},{6,4},{1,7},{3,1},{5,3},{7,5},{8,14},{10,8},{12,... | collective-permute-start | bytes 835592 | tf_op jit(solution)/shard_map/ppermute | solution.py:23
  143.1 4.7 %terms.4 = (bf16[192,2176]{1,0:T(8,128)(2,1)}, bf16[192,2176]{1,0:T(8,128)(2,1)}, bf16[192,2176]{1,0:T(8,128)(2,1)}) custom-call(bf16[8,2,7,16,256]{4,3,2,1,0:T(8,128)(2,1)} %copy-done, bf16[4,2,6,16,256]{4,3,2,1,0:T(8,128)(2,1)} %get-tuple-element.96.refs_1_, f32[4,2,6,16,256]{4,3,2,1,0:T(8,128)} %get-tuple-element.97.refs_2_, ...), custom_call_target="tpu_custom_call" | custom-call | flops 641728512 | bytes 6266880 | tf_op jit(solution)/shard_map/terms/pallas_call | solution.py:399
  149.1 3.0 %collective-permute-done.21.g2 = bf16[64,2176]{1,0:T(8,128)(2,1)S(1)} collective-permute-done((bf16[64,2176]{1,0:T(8,128)(2,1)}, bf16[64,2176]{1,0:T(8,128)(2,1)S(1)}, u32[]{:S(2)}, u32[]{:S(2)}) %collective-permute-start.21) | collective-permute-done | bytes 278560 | tf_op jit(solution)/shard_map/ppermute | solution.py:23
  152.9 2.3 %add_far.1 = (bf16[192,2176]{1,0:T(8,128)(2,1)}, bf16[192,2176]{1,0:T(8,128)(2,1)}, bf16[192,2176]{1,0:T(8,128)(2,1)}) custom-call(bf16[192,2176]{1,0:T(8,128)(2,1)} %get-tuple-element.98.t0, bf16[192,2176]{1,0:T(8,128)(2,1)} %get-tuple-element.99.t1, ...), custom_call_target="tpu_custom_call", output_to_operand_aliasing={{0}: (0, {}), {1}: (1, {}), {2}: (2, {})} | custom-call | flops 835584 | bytes 2506752 | tf_op jit(solution)/shard_map/add_far/pallas_call | solution.py:445
  155.6 1.1 collective-permute-start.23
  156.7 1.1 collective-permute-start.24
  157.8 10.4 %feed_forward.5 = (bf16[192,2176]{1,0:T(8,128)(2,1)}, bf16[192,2176]{1,0:T(8,128)(2,1)}, bf16[192,2176]{1,0:T(8,128)(2,1)}) custom-call(bf16[192,2048]{1,0:T(8,128)(2,1)} %collective-permute-done.4.refs_1_.refs_0_, bf16[192,2048]{1,0:T(8,128)(2,1)} %copy-done.26, bf16[192,2048]{1,0:T(8,128)(2,1)} %collective-permute-done.6.refs_3_.refs_2_, ...), custom_call_target="tpu_custom_call" | custom-call | flops 4831838208 | bytes 13107200 | tf_op jit(solution)/shard_map/feed_forward/pallas_call | solution.py:208
  168.2 5.6 %terms.5 = (bf16[192,2176]{1,0:T(8,128)(2,1)}, bf16[192,2176]{1,0:T(8,128)(2,1)}, bf16[192,2176]{1,0:T(8,128)(2,1)}, bf16[192,2176]{1,0:T(8,128)(2,1)}) custom-call(bf16[8,2,7,16,256]{4,3,2,1,0:T(8,128)(2,1)} %copy-done, bf16[4,2,6,16,256]{4,3,2,1,0:T(8,128)(2,1)} %get-tuple-element.90.refs_1_, f32[4,2,6,16,256]{4,3,2,1,0:T(8,128)} %get-tuple-element.91.refs_2_, ...), custom_call_target="tpu_custom_call" | custom-call | flops 855638016 | bytes 8355840 | tf_op jit(solution)/shard_map/terms/pallas_call | solution.py:399
  174.5 2.0 collective-permute-done.24.r2
  177.5 3.5 %add_near.1 = (bf16[192,2176]{1,0:T(8,128)(2,1)}, bf16[192,2176]{1,0:T(8,128)(2,1)}) custom-call(bf16[192,2176]{1,0:T(8,128)(2,1)} %get-tuple-element.111.t0, bf16[192,2176]{1,0:T(8,128)(2,1)} %get-tuple-element.112.t1, bf16[192,2176]{1,0:T(8,128)(2,1)} %copy-done.10, bf16[192,2176]{1,0:T(8,128)(2,1)} %copy-done.11, bf16[192,2176]{1,0:T(8,128)(2,1)} %copy-done.12), custom_call_target="tpu_custom_call" | custom-call | flops 1253376 | bytes 5849088 | tf_op jit(solution)/shard_map/add_near/pallas_call | solution.py:464
  182.8 11.9 %collective-permute-done.26.m1 = bf16[192,2176]{1,0:T(8,128)(2,1)S(1)} collective-permute-done((bf16[192,2176]{1,0:T(8,128)(2,1)}, bf16[192,2176]{1,0:T(8,128)(2,1)S(1)}, u32[]{:S(2)}, u32[]{:S(2)}) %collective-permute-start.26) | collective-permute-done | bytes 835616 | tf_op jit(solution)/shard_map/ppermute | solution.py:23
  194.7 3.3 %collective-permute-done.25.m0 = bf16[192,2176]{1,0:T(8,128)(2,1)S(1)} collective-permute-done((bf16[192,2176]{1,0:T(8,128)(2,1)}, bf16[192,2176]{1,0:T(8,128)(2,1)S(1)}, u32[]{:S(2)}, u32[]{:S(2)}) %collective-permute-start.25) | collective-permute-done | bytes 835616 | tf_op jit(solution)/shard_map/ppermute | solution.py:23
  198.0 1.0 collective-permute-done.27.m2
  199.9 5.7 %head.1 = (bf16[192,2048]{1,0:T(8,128)(2,1)}, f32[128,1,256]{2,1,0:T(1,128)}) custom-call(bf16[192,2048]{1,0:T(8,128)(2,1)} %bitcast.20, bf16[192,2176]{1,0:T(8,128)(2,1)} %get-tuple-element.110.mine, bf16[192,2176]{1,0:T(8,128)(2,1)} %copy-done.8, bf16[192,2176]{1,0:T(8,128)(2,1)} %copy-done.7, bf16[192,2176]{1,0:T(8,128)(2,1)} %copy-done.9, ...), custom_call_target="tpu_custom_call" | custom-call | tf_op jit(solution)/shard_map/head/pallas_call | solution.py:502
  205.6 12.6 %all-to-all-start.3 = ((f32[128,1,256]{2,1,0:T(1,128)}), f32[128,1,256]{2,1,0:T(1,128)S(1)}, u32[]{:S(2)}, u32[]{:S(2)}) async-start(f32[128,1,256]{2,1,0:T(1,128)} %get-tuple-element.119), calls=%async_computation.3 | async-start | bytes 262144 | tf_op jit(solution)/shard_map/all_to_all | solution.py:671
  218.8 9.6 %all-to-all-done.3 = f32[128,1,256]{2,1,0:T(1,128)S(1)} async-done(((f32[128,1,256]{2,1,0:T(1,128)}), f32[128,1,256]{2,1,0:T(1,128)S(1)}, u32[]{:S(2)}, u32[]{:S(2)}) %all-to-all-start.3) | async-done | bytes 131104 | tf_op jit(solution)/shard_map/all_to_all | solution.py:671
  229.1 2.1 pick.1
  (107 shorter events, 19.0 us)
Async XLA Ops:
  0.6 8.2 %copy-start.24 = (s32[8]{0:T(128)S(1)}, s32[8]{0:T(128)}, u32[]{:S(2)}) copy-start(s32[8]{0:T(128)} %constant.117.clone) | copy-start | bytes 100
  0.6 8.2 %copy-start.25 = (s32[8]{0:T(128)S(1)}, s32[8]{0:T(128)}, u32[]{:S(2)}) copy-start(s32[8]{0:T(128)} %constant.118.clone) | copy-start | bytes 100
  0.7 8.2 %collective-permute-start.1 = (bf16[2048,512]{1,0:T(8,128)(2,1)}, bf16[2048,512]{1,0:T(8,128)(2,1)S(1)}, u32[]{:S(2)}, u32[]{:S(2)}) collective-permute-start(bf16[2048,512]{1,0:T(8,128)(2,1)} %refs_3_.3), channel_id=1, source_target_pairs={{0,1},{1,0},{2,3},{3,2},{4,5},{5,4},{6,7},{7,6},{8,9},{9,8},{10,11... | collective-permute-start | bytes 6291464 | tf_op jit(solution)/shard_map/ppermute | solution.py:23
  2.1 9.0 %collective-permute-start.2 = (bf16[512,2048]{1,0:T(8,128)(2,1)}, bf16[512,2048]{1,0:T(8,128)(2,1)}, u32[]{:S(2)}, u32[]{:S(2)}) collective-permute-start(bf16[512,2048]{1,0:T(8,128)(2,1)} %refs_5_.5), channel_id=1, source_target_pairs={{0,1},{1,0},{2,3},{3,2},{4,5},{5,4},{6,7},{7,6},{8,9},{9,8},{10,11... | collective-permute-start | bytes 6291464 | tf_op jit(solution)/shard_map/ppermute | solution.py:23
  2.2 25.8 %collective-permute-start.3 = (bf16[3,2048,128]{2,1,0:T(8,128)(2,1)}, bf16[3,2048,128]{2,1,0:T(8,128)(2,1)}, u32[]{:S(2)}, u32[]{:S(2)}) collective-permute-start(bf16[3,2048,128]{2,1,0:T(8,128)(2,1)} %refs_5_.3), channel_id=1, source_target_pairs={{0,1},{1,0},{2,3},{3,2},{4,5},{5,4},{6,7},{7,6},{8,9},{9,8},{10,11... | collective-permute-start | bytes 4718600 | tf_op jit(solution)/shard_map/ppermute | solution.py:23
  4.9 22.0 %collective-permute-start.4 = (bf16[192,2048]{1,0:T(8,128)(2,1)}, bf16[192,2048]{1,0:T(8,128)(2,1)}, u32[]{:S(2)}, u32[]{:S(2)}) collective-permute-start(bf16[192,2048]{1,0:T(8,128)(2,1)} %normalize.1.refs_0_), channel_id=1, source_target_pairs={{0,2},{2,4},{4,6},{6,0},{1,3},{3,5},{5,7},{7,1},{8,10},{10,12},{12... | collective-permute-start | bytes 2359304 | tf_op jit(solution)/shard_map/ppermute | solution.py:23
  6.7 20.3 %collective-permute-start.5 = (bf16[192,2048]{1,0:T(8,128)(2,1)}, bf16[192,2048]{1,0:T(8,128)(2,1)S(1)}, u32[]{:S(2)}, u32[]{:S(2)}) collective-permute-start(bf16[192,2048]{1,0:T(8,128)(2,1)} %normalize.1.refs_0_), channel_id=1, source_target_pairs={{0,6},{2,0},{4,2},{6,4},{1,7},{3,1},{5,3},{7,5},{8,14},{10,8},{12,... | collective-permute-start | bytes 2359304 | tf_op jit(solution)/shard_map/ppermute | solution.py:23
  8.9 2.3 copy-start.6
  8.9 19.1 %collective-permute-start.6 = (bf16[192,2048]{1,0:T(8,128)(2,1)}, bf16[192,2048]{1,0:T(8,128)(2,1)}, u32[]{:S(2)}, u32[]{:S(2)}) collective-permute-start(bf16[192,2048]{1,0:T(8,128)(2,1)} %normalize.1.refs_0_), channel_id=1, source_target_pairs={{0,8},{8,0},{1,9},{9,1},{2,10},{10,2},{3,11},{11,3},{4,12},{12,4},... | collective-permute-start | bytes 2359304 | tf_op jit(solution)/shard_map/ppermute | solution.py:23
  28.0 19.4 %collective-permute-start.8 = (bf16[192,2048]{1,0:T(8,128)(2,1)}, bf16[192,2048]{1,0:T(8,128)(2,1)}, u32[]{:S(2)}, u32[]{:S(2)}) collective-permute-start(bf16[192,2048]{1,0:T(8,128)(2,1)} %collective-permute-done.4.refs_1_.refs_0_), channel_id=1, source_target_pairs={{0,2},{2,4},{4,6},{6,0},{1,3},{3,5},{5,7},{7,1},{8,10},{10,12},{12... | collective-permute-start | bytes 2359304 | tf_op jit(solution)/shard_map/ppermute | solution.py:23
  28.0 19.4 %collective-permute-start.9 = (bf16[192,2048]{1,0:T(8,128)(2,1)}, bf16[192,2048]{1,0:T(8,128)(2,1)S(1)}, u32[]{:S(2)}, u32[]{:S(2)}) collective-permute-start(bf16[192,2048]{1,0:T(8,128)(2,1)} %collective-permute-done.4.refs_1_.refs_0_), channel_id=1, source_target_pairs={{0,8},{8,0},{1,9},{9,1},{2,10},{10,2},{3,11},{11,3},{4,12},{12,4},... | collective-permute-start | bytes 2359304 | tf_op jit(solution)/shard_map/ppermute | solution.py:23
  29.3 18.1 %collective-permute-start.10 = (bf16[192,2048]{1,0:T(8,128)(2,1)}, bf16[192,2048]{1,0:T(8,128)(2,1)S(1)}, u32[]{:S(2)}, u32[]{:S(2)}) collective-permute-start(bf16[192,2048]{1,0:T(8,128)(2,1)} %collective-permute-done.6.refs_3_.refs_2_), channel_id=1, source_target_pairs={{0,6},{2,0},{4,2},{6,4},{1,7},{3,1},{5,3},{7,5},{8,14},{10,8},{12,... | collective-permute-start | bytes 2359304 | tf_op jit(solution)/shard_map/ppermute | solution.py:23
  38.2 22.8 %collective-permute-start.7 = (bf16[4,2,6,16,768]{4,3,2,1,0:T(8,128)(2,1)}, bf16[4,2,6,16,768]{4,3,2,1,0:T(8,128)(2,1)S(1)}, u32[]{:S(2)}, u32[]{:S(2)}) collective-permute-start(bf16[4,2,6,16,768]{4,3,2,1,0:T(8,128)(2,1)} %get-tuple-element.64.refs_3_), channel_id=1, source_target_pairs={{0,1},{1,0},{2,3},{3,2},{4,5},{5,4},{6,7},{7,6},{8,9},{9,8},{10,11... | collective-permute-start | bytes 3538952 | tf_op jit(solution)/shard_map/ppermute | solution.py:23
  40.3 31.6 %all-to-all-start = ((bf16[8,96,768]{2,1,0:T(8,128)(2,1)}), bf16[8,96,768]{2,1,0:T(8,128)(2,1)}, u32[]{:S(2)}, u32[]{:S(2)}) async-start(bf16[8,96,768]{2,1,0:T(8,128)(2,1)} %bitcast.17), calls=%async_computation | async-start | bytes 2359296 | tf_op jit(solution)/shard_map/all_to_all | solution.py:602
  51.2 9.7 %collective-permute-start.11 = (bf16[96,2048]{1,0:T(8,128)(2,1)}, bf16[96,2048]{1,0:T(8,128)(2,1)S(1)}, u32[]{:S(2)}, u32[]{:S(2)}) collective-permute-start(bf16[96,2048]{1,0:T(8,128)(2,1)} %get-tuple-element.68), channel_id=1, source_target_pairs={{0,2},{2,4},{4,6},{6,0},{1,3},{3,5},{5,7},{7,1},{8,10},{10,12},{12... | collective-permute-start | bytes 1179656 | tf_op jit(solution)/shard_map/ppermute | solution.py:23
  51.2 9.7 %collective-permute-start.12 = (bf16[96,2048]{1,0:T(8,128)(2,1)}, bf16[96,2048]{1,0:T(8,128)(2,1)S(1)}, u32[]{:S(2)}, u32[]{:S(2)}) collective-permute-start(bf16[96,2048]{1,0:T(8,128)(2,1)} %get-tuple-element.69), channel_id=1, source_target_pairs={{0,6},{2,0},{4,2},{6,4},{1,7},{3,1},{5,3},{7,5},{8,14},{10,8},{12,... | collective-permute-start | bytes 1179656 | tf_op jit(solution)/shard_map/ppermute | solution.py:23
  61.8 6.7 %copy-start.4 = (bf16[4,2,6,16,768]{4,3,2,1,0:T(8,128)(2,1)}, bf16[4,2,6,16,768]{4,3,2,1,0:T(8,128)(2,1)S(1)}, u32[]{:S(2)}) copy-start(bf16[4,2,6,16,768]{4,3,2,1,0:T(8,128)(2,1)S(1)} %collective-permute-done.7.refs_5_.refs_6_) | copy-start | bytes 3538948
  68.6 27.1 %collective-permute-start.13 = (bf16[4,2,6,16,768]{4,3,2,1,0:T(8,128)(2,1)}, bf16[4,2,6,16,768]{4,3,2,1,0:T(8,128)(2,1)S(1)}, u32[]{:S(2)}, u32[]{:S(2)}) collective-permute-start(bf16[4,2,6,16,768]{4,3,2,1,0:T(8,128)(2,1)} %get-tuple-element.75.refs_4_), channel_id=1, source_target_pairs={{0,1},{1,0},{2,3},{3,2},{4,5},{5,4},{6,7},{7,6},{8,9},{9,8},{10,11... | collective-permute-start | bytes 3538952 | tf_op jit(solution)/shard_map/ppermute | solution.py:23
  71.9 23.8 %all-to-all-start.1 = ((bf16[8,96,768]{2,1,0:T(8,128)(2,1)}), bf16[8,96,768]{2,1,0:T(8,128)(2,1)S(1)}, u32[]{:S(2)}, u32[]{:S(2)}) async-start(bf16[8,96,768]{2,1,0:T(8,128)(2,1)} %bitcast.18), calls=%async_computation.1 | async-start | bytes 2359296 | tf_op jit(solution)/shard_map/all_to_all | solution.py:602
  78.5 1.4 collective-permute-start
  95.7 5.1 %copy-start.5 = (bf16[4,2,6,16,768]{4,3,2,1,0:T(8,128)(2,1)}, bf16[4,2,6,16,768]{4,3,2,1,0:T(8,128)(2,1)S(1)}, u32[]{:S(2)}) copy-start(bf16[4,2,6,16,768]{4,3,2,1,0:T(8,128)(2,1)S(1)} %collective-permute-done.13.refs_7_.refs_8_) | copy-start | bytes 3538948
  100.7 7.1 %copy-start.2 = (bf16[128,2048]{1,0:T(8,128)(2,1)S(1)}, bf16[128,2048]{1,0:T(8,128)(2,1)}, u32[]{:S(2)}) copy-start(bf16[128,2048]{1,0:T(8,128)(2,1)} %refs_7_.3) | copy-start | bytes 1572868
  100.7 7.8 %copy-start.29 = (bf16[4,2,16,512]{3,2,1,0:T(8,128)(2,1)S(1)}, bf16[4,2,16,512]{3,2,1,0:T(8,128)(2,1)}, u32[]{:S(2)}) copy-start(bf16[4,2,16,512]{3,2,1,0:T(8,128)(2,1)} %get-tuple-element.88) | copy-start | bytes 393220
  100.7 11.3 %copy-start.30 = (bf16[4,2,16,512]{3,2,1,0:T(8,128)(2,1)S(1)}, bf16[4,2,16,512]{3,2,1,0:T(8,128)(2,1)}, u32[]{:S(2)}) copy-start(bf16[4,2,16,512]{3,2,1,0:T(8,128)(2,1)} %get-tuple-element.89) | copy-start | bytes 393220
  100.7 35.2 %all-to-all-start.2 = ((bf16[8,2,7,16,256]{4,3,2,1,0:T(8,128)(2,1)}), bf16[8,2,7,16,256]{4,3,2,1,0:T(8,128)(2,1)S(1)}, u32[]{:S(2)}, u32[]{:S(2)}) async-start(bf16[8,2,7,16,256]{4,3,2,1,0:T(8,128)(2,1)} %column_attention.3), calls=%async_computation.2 | async-start | bytes 1835008 | tf_op jit(solution)/shard_map/all_to_all | solution.py:626
  107.8 28.1 %collective-permute-start.18 = (bf16[128,2048]{1,0:T(8,128)(2,1)S(1)}, bf16[128,2048]{1,0:T(8,128)(2,1)S(1)}, u32[]{:S(2)}, u32[]{:S(2)}) collective-permute-start(bf16[128,2048]{1,0:T(8,128)(2,1)S(1)} %copy-done.2), channel_id=1, source_target_pairs={{0,1},{1,0},{2,3},{3,2},{4,5},{5,4},{6,7},{7,6},{8,9},{9,8},{10,11... | collective-permute-start | bytes 1572872 | tf_op jit(solution)/shard_map/ppermute | solution.py:23
  108.5 11.7 %collective-permute-start.14 = (bf16[4,2,16,512]{3,2,1,0:T(8,128)(2,1)S(1)}, bf16[4,2,16,512]{3,2,1,0:T(8,128)(2,1)S(1)}, u32[]{:S(2)}, u32[]{:S(2)}) collective-permute-start(bf16[4,2,16,512]{3,2,1,0:T(8,128)(2,1)S(1)} %copy-done.29), channel_id=1, source_target_pairs={{0,16},{16,32},{32,48},{48,64},{64,80},{80,96},{96,112},{1,17},{17... | collective-permute-start | bytes 393224 | tf_op jit(solution)/shard_map/ppermute | solution.py:44
  112.1 11.1 %collective-permute-start.15 = (bf16[4,2,16,512]{3,2,1,0:T(8,128)(2,1)S(1)}, bf16[4,2,16,512]{3,2,1,0:T(8,128)(2,1)S(1)}, u32[]{:S(2)}, u32[]{:S(2)}) collective-permute-start(bf16[4,2,16,512]{3,2,1,0:T(8,128)(2,1)S(1)} %copy-done.30), channel_id=1, source_target_pairs={{0,16},{16,32},{32,48},{48,64},{64,80},{80,96},{96,112},{1,17},{17... | collective-permute-start | bytes 393224 | tf_op jit(solution)/shard_map/ppermute | solution.py:44
  120.2 5.1 %copy-start.18 = (bf16[4,2,16,512]{3,2,1,0:T(8,128)(2,1)}, bf16[4,2,16,512]{3,2,1,0:T(8,128)(2,1)S(1)}, u32[]{:S(2)}) copy-start(bf16[4,2,16,512]{3,2,1,0:T(8,128)(2,1)S(1)} %collective-permute-done.14.refs_9_) | copy-start | bytes 393220
  120.2 4.9 %collective-permute-start.16 = (bf16[4,2,16,512]{3,2,1,0:T(8,128)(2,1)S(1)}, bf16[4,2,16,512]{3,2,1,0:T(8,128)(2,1)S(1)}, u32[]{:S(2)}, u32[]{:S(2)}) collective-permute-start(bf16[4,2,16,512]{3,2,1,0:T(8,128)(2,1)S(1)} %collective-permute-done.14.refs_9_), channel_id=1, source_target_pairs={{0,1},{1,0},{2,3},{3,2},{4,5},{5,4},{6,7},{7,6},{8,9},{9,8},{10,11... | collective-permute-start | bytes 393224 | tf_op jit(solution)/shard_map/ppermute | solution.py:23
  123.2 2.2 copy-start.19
  123.2 2.2 collective-permute-start.17
  140.2 8.4 %collective-permute-start.19 = (bf16[64,2176]{1,0:T(8,128)(2,1)}, bf16[64,2176]{1,0:T(8,128)(2,1)S(1)}, u32[]{:S(2)}, u32[]{:S(2)}) collective-permute-start(bf16[64,2176]{1,0:T(8,128)(2,1)} %get-tuple-element.94), channel_id=1, source_target_pairs={{0,8},{8,0},{1,9},{9,1},{2,10},{10,2},{3,11},{11,3},{4,12},{12,4},... | collective-permute-start | bytes 835592 | tf_op jit(solution)/shard_map/ppermute | solution.py:23
  140.5 8.6 %collective-permute-start.20 = (bf16[64,2176]{1,0:T(8,128)(2,1)}, bf16[64,2176]{1,0:T(8,128)(2,1)S(1)}, u32[]{:S(2)}, u32[]{:S(2)}) collective-permute-start(bf16[64,2176]{1,0:T(8,128)(2,1)} %get-tuple-element.101), channel_id=1, source_target_pairs={{0,6},{2,0},{4,2},{6,4},{1,7},{3,1},{5,3},{7,5},{8,14},{10,8},{12,... | collective-permute-start | bytes 835592 | tf_op jit(solution)/shard_map/ppermute | solution.py:23
  143.1 9.1 %collective-permute-start.21 = (bf16[64,2176]{1,0:T(8,128)(2,1)}, bf16[64,2176]{1,0:T(8,128)(2,1)S(1)}, u32[]{:S(2)}, u32[]{:S(2)}) collective-permute-start(bf16[64,2176]{1,0:T(8,128)(2,1)} %get-tuple-element.102), channel_id=1, source_target_pairs={{0,2},{2,4},{4,6},{6,0},{1,3},{3,5},{5,7},{7,1},{8,10},{10,12},{12... | collective-permute-start | bytes 835592 | tf_op jit(solution)/shard_map/ppermute | solution.py:23
  148.6 3.5 %copy-start.15 = (bf16[64,2176]{1,0:T(8,128)(2,1)}, bf16[64,2176]{1,0:T(8,128)(2,1)S(1)}, u32[]{:S(2)}) copy-start(bf16[64,2176]{1,0:T(8,128)(2,1)S(1)} %collective-permute-done.19.g0) | copy-start | bytes 835588
  149.1 3.0 %copy-start.16 = (bf16[64,2176]{1,0:T(8,128)(2,1)}, bf16[64,2176]{1,0:T(8,128)(2,1)S(1)}, u32[]{:S(2)}) copy-start(bf16[64,2176]{1,0:T(8,128)(2,1)S(1)} %collective-permute-done.20.g1) | copy-start | bytes 835588
  155.2 18.9 %collective-permute-start.22 = (bf16[192,2176]{1,0:T(8,128)(2,1)}, bf16[192,2176]{1,0:T(8,128)(2,1)S(1)}, u32[]{:S(2)}, u32[]{:S(2)}) collective-permute-start(bf16[192,2176]{1,0:T(8,128)(2,1)} %get-tuple-element.113), channel_id=1, source_target_pairs={{0,6},{2,0},{4,2},{6,4},{1,7},{3,1},{5,3},{7,5},{8,14},{10,8},{12,... | collective-permute-start | bytes 2506760 | tf_op jit(solution)/shard_map/ppermute | solution.py:23
  155.6 18.9 %collective-permute-start.23 = (bf16[192,2176]{1,0:T(8,128)(2,1)}, bf16[192,2176]{1,0:T(8,128)(2,1)S(1)}, u32[]{:S(2)}, u32[]{:S(2)}) collective-permute-start(bf16[192,2176]{1,0:T(8,128)(2,1)} %get-tuple-element.114), channel_id=1, source_target_pairs={{0,8},{8,0},{1,9},{9,1},{2,10},{10,2},{3,11},{11,3},{4,12},{12,4},... | collective-permute-start | bytes 2506760 | tf_op jit(solution)/shard_map/ppermute | solution.py:23
  156.7 19.9 %collective-permute-start.24 = (bf16[192,2176]{1,0:T(8,128)(2,1)}, bf16[192,2176]{1,0:T(8,128)(2,1)S(1)}, u32[]{:S(2)}, u32[]{:S(2)}) collective-permute-start(bf16[192,2176]{1,0:T(8,128)(2,1)} %get-tuple-element.103), channel_id=1, source_target_pairs={{0,2},{2,4},{4,6},{6,0},{1,3},{3,5},{5,7},{7,1},{8,10},{10,12},{12... | collective-permute-start | bytes 2506760 | tf_op jit(solution)/shard_map/ppermute | solution.py:23
  173.8 20.9 %collective-permute-start.26 = (bf16[192,2176]{1,0:T(8,128)(2,1)}, bf16[192,2176]{1,0:T(8,128)(2,1)S(1)}, u32[]{:S(2)}, u32[]{:S(2)}) collective-permute-start(bf16[192,2176]{1,0:T(8,128)(2,1)} %get-tuple-element.116), channel_id=1, source_target_pairs={{0,2},{2,4},{4,6},{6,0},{1,3},{3,5},{5,7},{7,1},{8,10},{10,12},{12... | collective-permute-start | bytes 2506760 | tf_op jit(solution)/shard_map/ppermute | solution.py:23
  174.2 2.4 %copy-start.10 = (bf16[192,2176]{1,0:T(8,128)(2,1)}, bf16[192,2176]{1,0:T(8,128)(2,1)S(1)}, u32[]{:S(2)}) copy-start(bf16[192,2176]{1,0:T(8,128)(2,1)S(1)} %collective-permute-done.22.r0) | copy-start | bytes 2506756
  177.5 4.6 %copy-start.22 = (s32[6,32]{1,0:T(8,128)S(1)}, s32[6,32]{1,0:T(8,128)}, u32[]{:S(2)}) copy-start(s32[6,32]{1,0:T(8,128)} %param.14) | copy-start | bytes 2308
  181.0 17.0 %collective-permute-start.25 = (bf16[192,2176]{1,0:T(8,128)(2,1)}, bf16[192,2176]{1,0:T(8,128)(2,1)S(1)}, u32[]{:S(2)}, u32[]{:S(2)}) collective-permute-start(bf16[192,2176]{1,0:T(8,128)(2,1)} %get-tuple-element.115), channel_id=1, source_target_pairs={{0,6},{2,0},{4,2},{6,4},{1,7},{3,1},{5,3},{7,5},{8,14},{10,8},{12,... | collective-permute-start | bytes 2506760 | tf_op jit(solution)/shard_map/ppermute | solution.py:23
  181.5 17.5 %collective-permute-start.27 = (bf16[192,2176]{1,0:T(8,128)(2,1)}, bf16[192,2176]{1,0:T(8,128)(2,1)S(1)}, u32[]{:S(2)}, u32[]{:S(2)}) collective-permute-start(bf16[192,2176]{1,0:T(8,128)(2,1)} %get-tuple-element.117), channel_id=1, source_target_pairs={{0,8},{8,0},{1,9},{9,1},{2,10},{10,2},{3,11},{11,3},{4,12},{12,4},... | collective-permute-start | bytes 2506760 | tf_op jit(solution)/shard_map/ppermute | solution.py:23
  194.7 4.3 %copy-start.7 = (bf16[192,2176]{1,0:T(8,128)(2,1)}, bf16[192,2176]{1,0:T(8,128)(2,1)S(1)}, u32[]{:S(2)}) copy-start(bf16[192,2176]{1,0:T(8,128)(2,1)S(1)} %collective-permute-done.26.m1) | copy-start | bytes 2506756
  199.9 18.3 %copy-start.23 = (s32[1024]{0:T(1024)S(1)}, s32[1024]{0:T(1024)}, u32[]{:S(2)}) copy-start(s32[1024]{0:T(1024)} %param.15) | copy-start | bytes 12292
  205.6 22.8 %all-to-all-start.3 = ((f32[128,1,256]{2,1,0:T(1,128)}), f32[128,1,256]{2,1,0:T(1,128)S(1)}, u32[]{:S(2)}, u32[]{:S(2)}) async-start(f32[128,1,256]{2,1,0:T(1,128)} %get-tuple-element.119), calls=%async_computation.3 | async-start | bytes 262144 | tf_op jit(solution)/shard_map/all_to_all | solution.py:671
  (15 other events, 14.4 us)

commit v6 on v5

--- a/solution.py
+++ b/solution.py
@@ -224,13 +224,21 @@
     )(*shards, up, their_up, down, their_down)
 
 
-def row_body(inv_root, hs, top_ref, qcol, kcol, *refs):
+def row_body(inv_root, hs, top_ref, kcol, *refs):
     cur, theirs, edges = refs[:2], refs[2:6], refs[6:10]
-    accs, dens, above = refs[10:12], refs[12:14], refs[14:]
+    accs, dens, above, qcol = refs[10:12], refs[12:14], refs[14:18], refs[18]
     r = pl.program_id(0)
     first = r == 0
     n = qcol.shape[0] // 2
-    mask = kcol[...] <= qcol[...]
+
+    @pl.when(first)
+    def _():
+        shape = (2 * n, 2 * n)
+        row, col = (lax.broadcasted_iota(jnp.int32, shape, i) for i in range(2))
+        here = jnp.where(row == col, kcol[:, : 2 * n].astype(F32), 0.0)
+        qcol[...] = jnp.broadcast_to(jnp.sum(here, axis=-1, keepdims=True), qcol.shape)
+
+    mask = kcol[...].astype(F32) <= qcol[:, 0:1]
     closed = jnp.logical_and(first, top_ref[0] == 1)
     same_one = jnp.where(mask, 1.0, 0.0)
     prev_one = jnp.where(closed, 0.0, 1.0 - same_one).astype(BF16)
@@ -269,7 +277,7 @@
         keep[...] = value
 
 
-def row_attention(top, qcol, kcol, qkv, their_qkv, edge, their_edge, hs, inv_root):
+def row_attention(top, kcol, qkv, their_qkv, edge, their_edge, hs, inv_root):
     rows = qkv[0].shape[2]
     now = pl.BlockSpec((4, 2, 1, HALF, 6 * hs), lambda r: (0, 0, r, 0, 0))
     keys = pl.BlockSpec((4, 2, 1, HALF, 2 * hs), lambda r: (0, 0, r, 0, 1))
@@ -277,19 +285,19 @@
     whole = lambda a: pl.BlockSpec(a.shape, lambda r: (0,) * a.ndim)
     out = lambda kind: jax.ShapeDtypeStruct((4, 2, rows, HALF, 2 * hs), kind)
     out_spec = pl.BlockSpec((4, 2, 1, HALF, 2 * hs), lambda r: (0, 0, r, 0, 0))
-    n = qcol.shape[0]
+    n = kcol.shape[1] // 2
     outs = pl.pallas_call(
         lambda *refs: row_body(inv_root, hs, *refs),
         grid=(rows,),
-        in_specs=[SMEM, whole(qcol), whole(kcol), now, now, keys, values, keys, values]
+        in_specs=[SMEM, whole(kcol), now, now, keys, values, keys, values]
         + [whole(e) for e in (*edge, *their_edge)],
         out_specs=[out_spec] * 4,
         out_shape=[out(BF16)] * 2 + [out(F32)] * 2,
-        scratch_shapes=[pltpu.VMEM((n // 2, 4 * hs), BF16)] * 4,
+        scratch_shapes=[pltpu.VMEM((n // 2, 4 * hs), BF16)] * 4 + [pltpu.VMEM((n, 128), F32)],
         cost_estimate=cost(rows * 32 * n * n * hs, rows * 32 * n * hs, rows * 4 * n * n),
         name="row_attention",
     )(
-        top, qcol, kcol, *qkv, their_qkv[0], their_qkv[0], their_qkv[1], their_qkv[1],
+        top, kcol, *qkv, their_qkv[0], their_qkv[0], their_qkv[1], their_qkv[1],
         *edge, *their_edge,
     )
     return outs[:2], outs[2:]
@@ -590,7 +598,7 @@
     offs = jnp.arange(cols, dtype=jnp.int32)
     mine = (starts[:, None] + core * cols + offs[None, :]).reshape(-1)
     theirs = (starts[:, None] + (1 - core) * cols + offs[None, :]).reshape(-1)
-    columns_of = (mine[:, None], jnp.concatenate([mine, theirs])[None, :])
+    columns_of = jnp.concatenate([mine, theirs])[None, :]
 
     near = (up_z(own), down_z(own), swap_x(own))
     (ff_own,) = ffn((own,), 1)
@@ -628,7 +636,7 @@
     top = (lax.axis_index(ROW) == 0).astype(jnp.int32)[None]
     acc, den = row_attention(
         after(back, top),
-        *columns_of,
+        columns_of,
         (qkv0, qkv1),
         (their_qkv0, their_qkv1),
         (edge0, edge1),

time: 232 us -> 231 us (level)
  transfers between devices with their start and end apart: 32 -> 32, of which waited for: 18 -> 18; matrix products, arithmetic and copies ran while one was open for 1% -> 1% of each run, Pallas kernels for 31% -> 32%
where the time goes in v6:
time: 231 us; the launch traced here: 230 us
  Pallas kernels  89.8 us (39%)
  starting transfers between devices  69.5 us (30%)
  waiting for transfers between devices  58.2 us (25%)
  local copies, waits for them, and re-layouts  9.43 us (4%)
    ppermute x26, waiting for transfers between devices, permuted(): return lax.ppermute(array, axis, [(i, (i + by) % n) for i in range(n)])  42.8 us
    ppermute x26, starting transfers between devices, permuted(): return lax.ppermute(array, axis, [(i, (i + by) % n) for i in range(n)])  30 us
    pallas_call x3, Pallas kernels, feed_forward(): pl.pallas_call(lambda *refs: forward_body(n, slots, slots == 4, *refs), i...  27.7 us
    pallas_call x3, Pallas kernels, terms(): pl.pallas_call(lambda *refs: term_body(hs, rows, splits, *refs), grid=(1,...  13.5 us
    pallas_call x2, Pallas kernels, project(): pl.pallas_call(lambda *refs: project_body(rows, n, *refs), grid=(3,), in_...  13.1 us
    all_to_all x2, starting transfers between devices, columns(): lax.all_to_all(qkv.reshape(row_peers, rows * HALF, 6 * hs), ROW, split_ax...  13 us
    all_to_all x1, starting transfers between devices, per_device(): lax.all_to_all(line, ALL, split_axis=0, concat_axis=0, tiled=True)  12.8 us
    all_to_all x1, waiting for transfers between devices, per_device(): lax.all_to_all(line, ALL, split_axis=0, concat_axis=0, tiled=True)  9.59 us
  transfers between devices with their start and end apart: 32, of which 18 were waited for; matrix products, arithmetic and copies ran while one was open for 1% of the time, Pallas kernels for 32%

profile of v6, /device:TPU:1, one launch (start us, length us, event | category | flops | bytes accessed | tf_op | source)
XLA Modules:
  0.0 229.9 jit_solution(122497514368113717)
XLA Ops:
  0.7 1.5 collective-permute-start.1
  2.6 2.3 %normalize.1.refs_0_ = bf16[192,2048]{1,0:T(8,128)(2,1)} custom-call(bf16[192,2048]{1,0:T(8,128)(2,1)} %bitcast.19, f32[1,2048]{1,0:T(1,128)} %bitcast.24), custom_call_target="tpu_custom_call" | custom-call | flops 1966080 | bytes 1572864 | tf_op jit(solution)/shard_map/normalize/pallas_call | solution.py:78
  4.9 1.7 collective-permute-start.4
  6.7 2.1 collective-permute-start.5
  8.9 1.3 collective-permute-start.6
  11.1 5.7 %feed_forward.3.refs_3_ = bf16[192,2176]{1,0:T(8,128)(2,1)} custom-call(bf16[192,2048]{1,0:T(8,128)(2,1)} %normalize.1.refs_0_, bf16[2048,512]{1,0:T(8,128)(2,1)} %refs_3_.3, bf16[2048,512]{1,0:T(8,128)(2,1)} %copy-done.6, bf16[512,2048]{1,0:T(8,128)(2,1)} %refs_5_.5, bf16[512,2048]{1,0:T(8,128)(2,1)} %collective-permute-done.2.refs_4_.refs_8_.refs_6_), custom_call_target="tpu_custom_call" | custom-call | flops 1610612736 | bytes 9961472 | tf_op jit(solution)/shard_map/feed_forward/pallas_call | solution.py:208
  16.7 10.1 %collective-permute-done.4.refs_1_.refs_0_ = bf16[192,2048]{1,0:T(8,128)(2,1)S(1)} collective-permute-done((bf16[192,2048]{1,0:T(8,128)(2,1)}, bf16[192,2048]{1,0:T(8,128)(2,1)S(1)}, u32[]{:S(2)}, u32[]{:S(2)}) %collective-permute-start.4) | collective-permute-done | bytes 786464 | tf_op jit(solution)/shard_map/ppermute | solution.py:23
  26.9 1.1 collective-permute-done.6.refs_3_.refs_2_
  28.0 1.2 collective-permute-start.9
  29.2 2.7 %collective-permute-start.10 = (bf16[192,2048]{1,0:T(8,128)(2,1)}, bf16[192,2048]{1,0:T(8,128)(2,1)S(1)}, u32[]{:S(2)}, u32[]{:S(2)}) collective-permute-start(bf16[192,2048]{1,0:T(8,128)(2,1)} %collective-permute-done.6.refs_3_.refs_2_), channel_id=1, source_target_pairs={{0,6},{2,0},{4,2},{6,4},{1,7},{3,1},{5,3},{7,5},{8,14},{10,8},{12,... | collective-permute-start | bytes 2359304 | tf_op jit(solution)/shard_map/ppermute | solution.py:23
  31.9 6.4 %project.2 = (bf16[4,2,6,16,768]{4,3,2,1,0:T(8,128)(2,1)}, bf16[4,2,16,512]{3,2,1,0:T(8,128)(2,1)}) custom-call(bf16[192,2048]{1,0:T(8,128)(2,1)} %normalize.1.refs_0_, bf16[192,2048]{1,0:T(8,128)(2,1)} %copy-done.26, bf16[192,2048]{1,0:T(8,128)(2,1)} %collective-permute-done.5.refs_2_.refs_1_, bf16[192,2048]{1,0:T(8,128)(2,1)} %collective-permute-done.6.refs_3_.refs_2_, ...), custom_call_target="tpu_custom_call" | custom-call | flops 2415919104 | bytes 6291456 | tf_op jit(solution)/shard_map/project/pallas_call | solution.py:108
  38.3 2.1 collective-permute-start.7
  40.4 6.4 %all-to-all-start = ((bf16[8,96,768]{2,1,0:T(8,128)(2,1)}), bf16[8,96,768]{2,1,0:T(8,128)(2,1)}, u32[]{:S(2)}, u32[]{:S(2)}) async-start(bf16[8,96,768]{2,1,0:T(8,128)(2,1)} %bitcast.17), calls=%async_computation | async-start | bytes 2359296 | tf_op jit(solution)/shard_map/all_to_all | solution.py:610
  49.0 2.1 halves.1
  51.0 2.7 %collective-permute-start.12 = (bf16[96,2048]{1,0:T(8,128)(2,1)}, bf16[96,2048]{1,0:T(8,128)(2,1)S(1)}, u32[]{:S(2)}, u32[]{:S(2)}) collective-permute-start(bf16[96,2048]{1,0:T(8,128)(2,1)} %get-tuple-element.69), channel_id=1, source_target_pairs={{0,6},{2,0},{4,2},{6,4},{1,7},{3,1},{5,3},{7,5},{8,14},{10,8},{12,... | collective-permute-start | bytes 1179656 | tf_op jit(solution)/shard_map/ppermute | solution.py:23
  53.7 7.2 %collective-permute-done.11.refs_3_ = bf16[96,2048]{1,0:T(8,128)(2,1)S(1)} collective-permute-done((bf16[96,2048]{1,0:T(8,128)(2,1)}, bf16[96,2048]{1,0:T(8,128)(2,1)S(1)}, u32[]{:S(2)}, u32[]{:S(2)}) %collective-permute-start.11) | collective-permute-done | bytes 393248 | tf_op jit(solution)/shard_map/ppermute | solution.py:23
  61.8 6.7 %project.3 = (bf16[4,2,6,16,768]{4,3,2,1,0:T(8,128)(2,1)}, bf16[4,2,16,512]{3,2,1,0:T(8,128)(2,1)}) custom-call(bf16[192,2048]{1,0:T(8,128)(2,1)} %collective-permute-done.8.refs_0_, bf16[192,2048]{1,0:T(8,128)(2,1)} %copy-done.13, bf16[192,2048]{1,0:T(8,128)(2,1)} %copy-done.14, bf16[96,2048]{1,0:T(8,128)(2,1)} %copy-done.27, bf16[96,2048]{1,0:T(8,128)(2,1)} %copy-done.28, ...), custom_call_target="tpu_custom_call" | custom-call | flops 2415919104 | bytes 6291456 | tf_op jit(solution)/shard_map/project/pallas_call | solution.py:108
  68.5 3.2 %collective-permute-start.13 = (bf16[4,2,6,16,768]{4,3,2,1,0:T(8,128)(2,1)}, bf16[4,2,6,16,768]{4,3,2,1,0:T(8,128)(2,1)S(1)}, u32[]{:S(2)}, u32[]{:S(2)}) collective-permute-start(bf16[4,2,6,16,768]{4,3,2,1,0:T(8,128)(2,1)} %get-tuple-element.75.refs_3_), channel_id=1, source_target_pairs={{0,1},{1,0},{2,3},{3,2},{4,5},{5,4},{6,7},{7,6},{8,9},{9,8},{10,11... | collective-permute-start | bytes 3538952 | tf_op jit(solution)/shard_map/ppermute | solution.py:23
  71.7 6.7 %all-to-all-start.1 = ((bf16[8,96,768]{2,1,0:T(8,128)(2,1)}), bf16[8,96,768]{2,1,0:T(8,128)(2,1)S(1)}, u32[]{:S(2)}, u32[]{:S(2)}) async-start(bf16[8,96,768]{2,1,0:T(8,128)(2,1)} %bitcast.18), calls=%async_computation.1 | async-start | bytes 2359296 | tf_op jit(solution)/shard_map/all_to_all | solution.py:610
  79.7 4.0 %column_attention.2.refs_3_ = bf16[8,2,7,16,256]{4,3,2,1,0:T(8,128)(2,1)} custom-call(f32[1]{0:T(128)S(6)} %copy.30.refs_0_, f32[1]{0:T(128)} %collective-permute-done.refs_1_, bf16[48,16,768]{2,1,0:T(8,128)(2,1)} %bitcast.4.refs_2_), custom_call_target="tpu_custom_call" | custom-call | flops 452984832 | bytes 1572864 | tf_op jit(solution)/shard_map/column_attention/pallas_call | solution.py:351
  83.7 11.6 %feed_forward.4 = (bf16[192,2176]{1,0:T(8,128)(2,1)}, bf16[192,2176]{1,0:T(8,128)(2,1)}, bf16[192,2176]{1,0:T(8,128)(2,1)}, bf16[192,2176]{1,0:T(8,128)(2,1)}) custom-call(bf16[192,2048]{1,0:T(8,128)(2,1)} %collective-permute-done.8.refs_0_, bf16[192,2048]{1,0:T(8,128)(2,1)} %copy-done.13, bf16[192,2048]{1,0:T(8,128)(2,1)} %copy-done.14, ...), custom_call_target="tpu_custom_call" | custom-call | flops 6442450944 | bytes 14680064 | tf_op jit(solution)/shard_map/feed_forward/pallas_call | solution.py:208
  95.4 1.0 copy-done.1
  96.4 4.0 %column_attention.3 = bf16[8,2,7,16,256]{4,3,2,1,0:T(8,128)(2,1)} custom-call(f32[1]{0:T(128)S(6)} %copy.30.refs_0_, f32[1]{0:T(128)} %collective-permute-done.refs_1_, bf16[48,16,768]{2,1,0:T(8,128)(2,1)} %bitcast.16, bf16[8,2,7,16,256]{4,3,2,1,0:T(8,128)(2,1)} %column_attention.2.refs_3_), custom_call_target="tpu_custom_call", output_to_operand_aliasing={{}: (3, {})} | custom-call | flops 452984832 | bytes 1572864 | tf_op jit(solution)/shard_map/column_attention/pallas_call | solution.py:351
  100.4 7.0 %all-to-all-start.2 = ((bf16[8,2,7,16,256]{4,3,2,1,0:T(8,128)(2,1)}), bf16[8,2,7,16,256]{4,3,2,1,0:T(8,128)(2,1)S(1)}, u32[]{:S(2)}, u32[]{:S(2)}) async-start(bf16[8,2,7,16,256]{4,3,2,1,0:T(8,128)(2,1)} %column_attention.3), calls=%async_computation.2 | async-start | bytes 1835008 | tf_op jit(solution)/shard_map/all_to_all | solution.py:634
  108.1 3.6 %collective-permute-start.14 = (bf16[4,2,16,512]{3,2,1,0:T(8,128)(2,1)S(1)}, bf16[4,2,16,512]{3,2,1,0:T(8,128)(2,1)S(1)}, u32[]{:S(2)}, u32[]{:S(2)}) collective-permute-start(bf16[4,2,16,512]{3,2,1,0:T(8,128)(2,1)S(1)} %copy-done.29), channel_id=1, source_target_pairs={{0,16},{16,32},{32,48},{48,64},{64,80},{80,96},{96,112},{1,17},{17... | collective-permute-start | bytes 393224 | tf_op jit(solution)/shard_map/ppermute | solution.py:44
  111.7 3.1 %collective-permute-start.15 = (bf16[4,2,16,512]{3,2,1,0:T(8,128)(2,1)S(1)}, bf16[4,2,16,512]{3,2,1,0:T(8,128)(2,1)S(1)}, u32[]{:S(2)}, u32[]{:S(2)}) collective-permute-start(bf16[4,2,16,512]{3,2,1,0:T(8,128)(2,1)S(1)} %copy-done.30), channel_id=1, source_target_pairs={{0,16},{16,32},{32,48},{48,64},{64,80},{80,96},{96,112},{1,17},{17... | collective-permute-start | bytes 393224 | tf_op jit(solution)/shard_map/ppermute | solution.py:44
  114.8 5.0 %collective-permute-done.14.refs_8_ = bf16[4,2,16,512]{3,2,1,0:T(8,128)(2,1)S(1)} collective-permute-done((bf16[4,2,16,512]{3,2,1,0:T(8,128)(2,1)S(1)}, bf16[4,2,16,512]{3,2,1,0:T(8,128)(2,1)S(1)}, u32[]{:S(2)}, u32[]{:S(2)}) %collective-permute-start.14) | collective-permute-done | bytes 131104 | tf_op jit(solution)/shard_map/ppermute | solution.py:44
  119.8 2.1 collective-permute-start.16
  122.8 1.2 collective-permute-start.17
  125.6 9.5 %row_attention.1 = (bf16[4,2,6,16,256]{4,3,2,1,0:T(8,128)(2,1)}, bf16[4,2,6,16,256]{4,3,2,1,0:T(8,128)(2,1)}, f32[4,2,6,16,256]{4,3,2,1,0:T(8,128)}, f32[4,2,6,16,256]{4,3,2,1,0:T(8,128)}) custom-call(s32[1]{0:T(128)} %bitcast.7.refs_0_, s32[1,512]{1,0:T(1,128)} %bitcast.26, bf16[4,2,6,16,768]{4,3,2,1,0:T(8,128)(2,1)} %get-tuple-element.64.refs_2_, ...), custom_call_target="tpu_custom_call" | custom-call | flops 1610612736 | bytes 6291456 | tf_op jit(solution)/shard_map/row_attention/pallas_call | solution.py:289
  136.3 3.1 %terms.3 = (bf16[64,2176]{1,0:T(8,128)(2,1)}, bf16[64,2176]{1,0:T(8,128)(2,1)}, bf16[64,2176]{1,0:T(8,128)(2,1)}) custom-call(bf16[8,2,7,16,256]{4,3,2,1,0:T(8,128)(2,1)} %copy-done, bf16[4,2,6,16,256]{4,3,2,1,0:T(8,128)(2,1)} %get-tuple-element.96.refs_1_, f32[4,2,6,16,256]{4,3,2,1,0:T(8,128)} %get-tuple-element.97.refs_2_, ...), custom_call_target="tpu_custom_call" | custom-call | flops 213909504 | bytes 2088960 | tf_op jit(solution)/shard_map/terms/pallas_call | solution.py:407
  139.7 2.6 %collective-permute-start.20 = (bf16[64,2176]{1,0:T(8,128)(2,1)}, bf16[64,2176]{1,0:T(8,128)(2,1)S(1)}, u32[]{:S(2)}, u32[]{:S(2)}) collective-permute-start(bf16[64,2176]{1,0:T(8,128)(2,1)} %get-tuple-element.101), channel_id=1, source_target_pairs={{0,6},{2,0},{4,2},{6,4},{1,7},{3,1},{5,3},{7,5},{8,14},{10,8},{12,... | collective-permute-start | bytes 835592 | tf_op jit(solution)/shard_map/ppermute | solution.py:23
  142.2 4.7 %terms.4 = (bf16[192,2176]{1,0:T(8,128)(2,1)}, bf16[192,2176]{1,0:T(8,128)(2,1)}, bf16[192,2176]{1,0:T(8,128)(2,1)}) custom-call(bf16[8,2,7,16,256]{4,3,2,1,0:T(8,128)(2,1)} %copy-done, bf16[4,2,6,16,256]{4,3,2,1,0:T(8,128)(2,1)} %get-tuple-element.96.refs_1_, f32[4,2,6,16,256]{4,3,2,1,0:T(8,128)} %get-tuple-element.97.refs_2_, ...), custom_call_target="tpu_custom_call" | custom-call | flops 641728512 | bytes 6266880 | tf_op jit(solution)/shard_map/terms/pallas_call | solution.py:407
  147.9 3.0 %collective-permute-done.21.g2 = bf16[64,2176]{1,0:T(8,128)(2,1)S(1)} collective-permute-done((bf16[64,2176]{1,0:T(8,128)(2,1)}, bf16[64,2176]{1,0:T(8,128)(2,1)S(1)}, u32[]{:S(2)}, u32[]{:S(2)}) %collective-permute-start.21) | collective-permute-done | bytes 278560 | tf_op jit(solution)/shard_map/ppermute | solution.py:23
  151.6 2.4 %add_far.1 = (bf16[192,2176]{1,0:T(8,128)(2,1)}, bf16[192,2176]{1,0:T(8,128)(2,1)}, bf16[192,2176]{1,0:T(8,128)(2,1)}) custom-call(bf16[192,2176]{1,0:T(8,128)(2,1)} %get-tuple-element.98.t0, bf16[192,2176]{1,0:T(8,128)(2,1)} %get-tuple-element.99.t1, ...), custom_call_target="tpu_custom_call", output_to_operand_aliasing={{0}: (0, {}), {1}: (1, {}), {2}: (2, {})} | custom-call | flops 835584 | bytes 2506752 | tf_op jit(solution)/shard_map/add_far/pallas_call | solution.py:453
  154.4 1.1 collective-permute-start.23
  155.5 1.1 collective-permute-start.24
  156.6 10.5 %feed_forward.5 = (bf16[192,2176]{1,0:T(8,128)(2,1)}, bf16[192,2176]{1,0:T(8,128)(2,1)}, bf16[192,2176]{1,0:T(8,128)(2,1)}) custom-call(bf16[192,2048]{1,0:T(8,128)(2,1)} %copy-done.26, bf16[192,2048]{1,0:T(8,128)(2,1)} %collective-permute-done.5.refs_2_.refs_1_, bf16[192,2048]{1,0:T(8,128)(2,1)} %collective-permute-done.6.refs_3_.refs_2_, ...), custom_call_target="tpu_custom_call" | custom-call | flops 4831838208 | bytes 13107200 | tf_op jit(solution)/shard_map/feed_forward/pallas_call | solution.py:208
  167.1 5.7 %terms.5 = (bf16[192,2176]{1,0:T(8,128)(2,1)}, bf16[192,2176]{1,0:T(8,128)(2,1)}, bf16[192,2176]{1,0:T(8,128)(2,1)}, bf16[192,2176]{1,0:T(8,128)(2,1)}) custom-call(bf16[8,2,7,16,256]{4,3,2,1,0:T(8,128)(2,1)} %copy-done, bf16[4,2,6,16,256]{4,3,2,1,0:T(8,128)(2,1)} %get-tuple-element.90.refs_1_, f32[4,2,6,16,256]{4,3,2,1,0:T(8,128)} %get-tuple-element.91.refs_2_, ...), custom_call_target="tpu_custom_call" | custom-call | flops 855638016 | bytes 8355840 | tf_op jit(solution)/shard_map/terms/pallas_call | solution.py:407
  173.0 2.1 collective-permute-done.24.r2
  175.9 3.5 %add_near.1 = (bf16[192,2176]{1,0:T(8,128)(2,1)}, bf16[192,2176]{1,0:T(8,128)(2,1)}) custom-call(bf16[192,2176]{1,0:T(8,128)(2,1)} %get-tuple-element.111.t0, bf16[192,2176]{1,0:T(8,128)(2,1)} %get-tuple-element.112.t1, bf16[192,2176]{1,0:T(8,128)(2,1)} %copy-done.10, bf16[192,2176]{1,0:T(8,128)(2,1)} %copy-done.11, bf16[192,2176]{1,0:T(8,128)(2,1)} %copy-done.12), custom_call_target="tpu_custom_call" | custom-call | flops 1253376 | bytes 5849088 | tf_op jit(solution)/shard_map/add_near/pallas_call | solution.py:472
  181.4 11.7 %collective-permute-done.26.m1 = bf16[192,2176]{1,0:T(8,128)(2,1)S(1)} collective-permute-done((bf16[192,2176]{1,0:T(8,128)(2,1)}, bf16[192,2176]{1,0:T(8,128)(2,1)S(1)}, u32[]{:S(2)}, u32[]{:S(2)}) %collective-permute-start.26) | collective-permute-done | bytes 835616 | tf_op jit(solution)/shard_map/ppermute | solution.py:23
  193.1 3.0 %collective-permute-done.25.m0 = bf16[192,2176]{1,0:T(8,128)(2,1)S(1)} collective-permute-done((bf16[192,2176]{1,0:T(8,128)(2,1)}, bf16[192,2176]{1,0:T(8,128)(2,1)S(1)}, u32[]{:S(2)}, u32[]{:S(2)}) %collective-permute-start.25) | collective-permute-done | bytes 835616 | tf_op jit(solution)/shard_map/ppermute | solution.py:23
  196.1 1.4 collective-permute-done.27.m2
  198.4 5.7 %head.1 = (bf16[192,2048]{1,0:T(8,128)(2,1)}, f32[128,1,256]{2,1,0:T(1,128)}) custom-call(bf16[192,2048]{1,0:T(8,128)(2,1)} %bitcast.20, bf16[192,2176]{1,0:T(8,128)(2,1)} %get-tuple-element.110.mine, bf16[192,2176]{1,0:T(8,128)(2,1)} %copy-done.8, bf16[192,2176]{1,0:T(8,128)(2,1)} %copy-done.7, bf16[192,2176]{1,0:T(8,128)(2,1)} %copy-done.9, ...), custom_call_target="tpu_custom_call" | custom-call | tf_op jit(solution)/shard_map/head/pallas_call | solution.py:510
  204.1 12.8 %all-to-all-start.3 = ((f32[128,1,256]{2,1,0:T(1,128)}), f32[128,1,256]{2,1,0:T(1,128)S(1)}, u32[]{:S(2)}, u32[]{:S(2)}) async-start(f32[128,1,256]{2,1,0:T(1,128)} %get-tuple-element.119), calls=%async_computation.3 | async-start | bytes 262144 | tf_op jit(solution)/shard_map/all_to_all | solution.py:679
  217.5 9.6 %all-to-all-done.3 = f32[128,1,256]{2,1,0:T(1,128)S(1)} async-done(((f32[128,1,256]{2,1,0:T(1,128)}), f32[128,1,256]{2,1,0:T(1,128)S(1)}, u32[]{:S(2)}, u32[]{:S(2)}) %all-to-all-start.3) | async-done | bytes 131104 | tf_op jit(solution)/shard_map/all_to_all | solution.py:679
  227.8 2.1 pick.1
  (105 shorter events, 17.3 us)
Async XLA Ops:
  0.6 8.2 %copy-start.24 = (s32[8]{0:T(128)S(1)}, s32[8]{0:T(128)}, u32[]{:S(2)}) copy-start(s32[8]{0:T(128)} %constant.117.clone) | copy-start | bytes 100
  0.6 8.2 %copy-start.25 = (s32[8]{0:T(128)S(1)}, s32[8]{0:T(128)}, u32[]{:S(2)}) copy-start(s32[8]{0:T(128)} %constant.118.clone) | copy-start | bytes 100
  0.7 8.2 %collective-permute-start.1 = (bf16[2048,512]{1,0:T(8,128)(2,1)}, bf16[2048,512]{1,0:T(8,128)(2,1)S(1)}, u32[]{:S(2)}, u32[]{:S(2)}) collective-permute-start(bf16[2048,512]{1,0:T(8,128)(2,1)} %refs_3_.3), channel_id=1, source_target_pairs={{0,1},{1,0},{2,3},{3,2},{4,5},{5,4},{6,7},{7,6},{8,9},{9,8},{10,11... | collective-permute-start | bytes 6291464 | tf_op jit(solution)/shard_map/ppermute | solution.py:23
  2.1 8.9 %collective-permute-start.2 = (bf16[512,2048]{1,0:T(8,128)(2,1)}, bf16[512,2048]{1,0:T(8,128)(2,1)}, u32[]{:S(2)}, u32[]{:S(2)}) collective-permute-start(bf16[512,2048]{1,0:T(8,128)(2,1)} %refs_5_.5), channel_id=1, source_target_pairs={{0,1},{1,0},{2,3},{3,2},{4,5},{5,4},{6,7},{7,6},{8,9},{9,8},{10,11... | collective-permute-start | bytes 6291464 | tf_op jit(solution)/shard_map/ppermute | solution.py:23
  2.2 25.8 %collective-permute-start.3 = (bf16[3,2048,128]{2,1,0:T(8,128)(2,1)}, bf16[3,2048,128]{2,1,0:T(8,128)(2,1)}, u32[]{:S(2)}, u32[]{:S(2)}) collective-permute-start(bf16[3,2048,128]{2,1,0:T(8,128)(2,1)} %refs_5_.3), channel_id=1, source_target_pairs={{0,1},{1,0},{2,3},{3,2},{4,5},{5,4},{6,7},{7,6},{8,9},{9,8},{10,11... | collective-permute-start | bytes 4718600 | tf_op jit(solution)/shard_map/ppermute | solution.py:23
  4.9 21.9 %collective-permute-start.4 = (bf16[192,2048]{1,0:T(8,128)(2,1)}, bf16[192,2048]{1,0:T(8,128)(2,1)S(1)}, u32[]{:S(2)}, u32[]{:S(2)}) collective-permute-start(bf16[192,2048]{1,0:T(8,128)(2,1)} %normalize.1.refs_0_), channel_id=1, source_target_pairs={{0,2},{2,4},{4,6},{6,0},{1,3},{3,5},{5,7},{7,1},{8,10},{10,12},{12... | collective-permute-start | bytes 2359304 | tf_op jit(solution)/shard_map/ppermute | solution.py:23
  6.7 20.2 %collective-permute-start.5 = (bf16[192,2048]{1,0:T(8,128)(2,1)}, bf16[192,2048]{1,0:T(8,128)(2,1)}, u32[]{:S(2)}, u32[]{:S(2)}) collective-permute-start(bf16[192,2048]{1,0:T(8,128)(2,1)} %normalize.1.refs_0_), channel_id=1, source_target_pairs={{0,6},{2,0},{4,2},{6,4},{1,7},{3,1},{5,3},{7,5},{8,14},{10,8},{12,... | collective-permute-start | bytes 2359304 | tf_op jit(solution)/shard_map/ppermute | solution.py:23
  8.9 2.2 copy-start.6
  8.9 19.1 %collective-permute-start.6 = (bf16[192,2048]{1,0:T(8,128)(2,1)}, bf16[192,2048]{1,0:T(8,128)(2,1)}, u32[]{:S(2)}, u32[]{:S(2)}) collective-permute-start(bf16[192,2048]{1,0:T(8,128)(2,1)} %normalize.1.refs_0_), channel_id=1, source_target_pairs={{0,8},{8,0},{1,9},{9,1},{2,10},{10,2},{3,11},{11,3},{4,12},{12,4},... | collective-permute-start | bytes 2359304 | tf_op jit(solution)/shard_map/ppermute | solution.py:23
  26.8 5.0 %copy-start.26 = (bf16[192,2048]{1,0:T(8,128)(2,1)}, bf16[192,2048]{1,0:T(8,128)(2,1)S(1)}, u32[]{:S(2)}) copy-start(bf16[192,2048]{1,0:T(8,128)(2,1)S(1)} %collective-permute-done.4.refs_1_.refs_0_) | copy-start | bytes 2359300
  28.0 19.2 %collective-permute-start.8 = (bf16[192,2048]{1,0:T(8,128)(2,1)S(1)}, bf16[192,2048]{1,0:T(8,128)(2,1)}, u32[]{:S(2)}, u32[]{:S(2)}) collective-permute-start(bf16[192,2048]{1,0:T(8,128)(2,1)S(1)} %collective-permute-done.4.refs_1_.refs_0_), channel_id=1, source_target_pairs={{0,2},{2,4},{4,6},{6,0},{1,3},{3,5},{5,7},{7,1},{8,10},{10,12},{12... | collective-permute-start | bytes 2359304 | tf_op jit(solution)/shard_map/ppermute | solution.py:23
  28.0 19.2 %collective-permute-start.9 = (bf16[192,2048]{1,0:T(8,128)(2,1)S(1)}, bf16[192,2048]{1,0:T(8,128)(2,1)S(1)}, u32[]{:S(2)}, u32[]{:S(2)}) collective-permute-start(bf16[192,2048]{1,0:T(8,128)(2,1)S(1)} %collective-permute-done.4.refs_1_.refs_0_), channel_id=1, source_target_pairs={{0,8},{8,0},{1,9},{9,1},{2,10},{10,2},{3,11},{11,3},{4,12},{12,4},... | collective-permute-start | bytes 2359304 | tf_op jit(solution)/shard_map/ppermute | solution.py:23
  29.2 18.1 %collective-permute-start.10 = (bf16[192,2048]{1,0:T(8,128)(2,1)}, bf16[192,2048]{1,0:T(8,128)(2,1)S(1)}, u32[]{:S(2)}, u32[]{:S(2)}) collective-permute-start(bf16[192,2048]{1,0:T(8,128)(2,1)} %collective-permute-done.6.refs_3_.refs_2_), channel_id=1, source_target_pairs={{0,6},{2,0},{4,2},{6,4},{1,7},{3,1},{5,3},{7,5},{8,14},{10,8},{12,... | collective-permute-start | bytes 2359304 | tf_op jit(solution)/shard_map/ppermute | solution.py:23
  38.3 22.6 %collective-permute-start.7 = (bf16[4,2,6,16,768]{4,3,2,1,0:T(8,128)(2,1)}, bf16[4,2,6,16,768]{4,3,2,1,0:T(8,128)(2,1)S(1)}, u32[]{:S(2)}, u32[]{:S(2)}) collective-permute-start(bf16[4,2,6,16,768]{4,3,2,1,0:T(8,128)(2,1)} %get-tuple-element.64.refs_2_), channel_id=1, source_target_pairs={{0,1},{1,0},{2,3},{3,2},{4,5},{5,4},{6,7},{7,6},{8,9},{9,8},{10,11... | collective-permute-start | bytes 3538952 | tf_op jit(solution)/shard_map/ppermute | solution.py:23
  40.4 31.3 %all-to-all-start = ((bf16[8,96,768]{2,1,0:T(8,128)(2,1)}), bf16[8,96,768]{2,1,0:T(8,128)(2,1)}, u32[]{:S(2)}, u32[]{:S(2)}) async-start(bf16[8,96,768]{2,1,0:T(8,128)(2,1)} %bitcast.17), calls=%async_computation | async-start | bytes 2359296 | tf_op jit(solution)/shard_map/all_to_all | solution.py:610
  51.0 9.8 %collective-permute-start.11 = (bf16[96,2048]{1,0:T(8,128)(2,1)}, bf16[96,2048]{1,0:T(8,128)(2,1)S(1)}, u32[]{:S(2)}, u32[]{:S(2)}) collective-permute-start(bf16[96,2048]{1,0:T(8,128)(2,1)} %get-tuple-element.68), channel_id=1, source_target_pairs={{0,2},{2,4},{4,6},{6,0},{1,3},{3,5},{5,7},{7,1},{8,10},{10,12},{12... | collective-permute-start | bytes 1179656 | tf_op jit(solution)/shard_map/ppermute | solution.py:23
  51.0 9.8 %collective-permute-start.12 = (bf16[96,2048]{1,0:T(8,128)(2,1)}, bf16[96,2048]{1,0:T(8,128)(2,1)S(1)}, u32[]{:S(2)}, u32[]{:S(2)}) collective-permute-start(bf16[96,2048]{1,0:T(8,128)(2,1)} %get-tuple-element.69), channel_id=1, source_target_pairs={{0,6},{2,0},{4,2},{6,4},{1,7},{3,1},{5,3},{7,5},{8,14},{10,8},{12,... | collective-permute-start | bytes 1179656 | tf_op jit(solution)/shard_map/ppermute | solution.py:23
  61.8 6.7 %copy-start.4 = (bf16[4,2,6,16,768]{4,3,2,1,0:T(8,128)(2,1)}, bf16[4,2,6,16,768]{4,3,2,1,0:T(8,128)(2,1)S(1)}, u32[]{:S(2)}) copy-start(bf16[4,2,6,16,768]{4,3,2,1,0:T(8,128)(2,1)S(1)} %collective-permute-done.7.refs_4_.refs_5_) | copy-start | bytes 3538948
  68.5 26.9 %collective-permute-start.13 = (bf16[4,2,6,16,768]{4,3,2,1,0:T(8,128)(2,1)}, bf16[4,2,6,16,768]{4,3,2,1,0:T(8,128)(2,1)S(1)}, u32[]{:S(2)}, u32[]{:S(2)}) collective-permute-start(bf16[4,2,6,16,768]{4,3,2,1,0:T(8,128)(2,1)} %get-tuple-element.75.refs_3_), channel_id=1, source_target_pairs={{0,1},{1,0},{2,3},{3,2},{4,5},{5,4},{6,7},{7,6},{8,9},{9,8},{10,11... | collective-permute-start | bytes 3538952 | tf_op jit(solution)/shard_map/ppermute | solution.py:23
  71.7 23.7 %all-to-all-start.1 = ((bf16[8,96,768]{2,1,0:T(8,128)(2,1)}), bf16[8,96,768]{2,1,0:T(8,128)(2,1)S(1)}, u32[]{:S(2)}, u32[]{:S(2)}) async-start(bf16[8,96,768]{2,1,0:T(8,128)(2,1)} %bitcast.18), calls=%async_computation.1 | async-start | bytes 2359296 | tf_op jit(solution)/shard_map/all_to_all | solution.py:610
  78.3 1.4 collective-permute-start
  95.4 5.0 %copy-start.5 = (bf16[4,2,6,16,768]{4,3,2,1,0:T(8,128)(2,1)}, bf16[4,2,6,16,768]{4,3,2,1,0:T(8,128)(2,1)S(1)}, u32[]{:S(2)}) copy-start(bf16[4,2,6,16,768]{4,3,2,1,0:T(8,128)(2,1)S(1)} %collective-permute-done.13.refs_6_.refs_7_) | copy-start | bytes 3538948
  100.4 7.1 %copy-start.2 = (bf16[128,2048]{1,0:T(8,128)(2,1)S(1)}, bf16[128,2048]{1,0:T(8,128)(2,1)}, u32[]{:S(2)}) copy-start(bf16[128,2048]{1,0:T(8,128)(2,1)} %refs_7_.3) | copy-start | bytes 1572868
  100.4 7.8 %copy-start.29 = (bf16[4,2,16,512]{3,2,1,0:T(8,128)(2,1)S(1)}, bf16[4,2,16,512]{3,2,1,0:T(8,128)(2,1)}, u32[]{:S(2)}) copy-start(bf16[4,2,16,512]{3,2,1,0:T(8,128)(2,1)} %get-tuple-element.88) | copy-start | bytes 393220
  100.4 11.3 %copy-start.30 = (bf16[4,2,16,512]{3,2,1,0:T(8,128)(2,1)S(1)}, bf16[4,2,16,512]{3,2,1,0:T(8,128)(2,1)}, u32[]{:S(2)}) copy-start(bf16[4,2,16,512]{3,2,1,0:T(8,128)(2,1)} %get-tuple-element.89) | copy-start | bytes 393220
  100.4 34.8 %all-to-all-start.2 = ((bf16[8,2,7,16,256]{4,3,2,1,0:T(8,128)(2,1)}), bf16[8,2,7,16,256]{4,3,2,1,0:T(8,128)(2,1)S(1)}, u32[]{:S(2)}, u32[]{:S(2)}) async-start(bf16[8,2,7,16,256]{4,3,2,1,0:T(8,128)(2,1)} %column_attention.3), calls=%async_computation.2 | async-start | bytes 1835008 | tf_op jit(solution)/shard_map/all_to_all | solution.py:634
  107.4 27.7 %collective-permute-start.18 = (bf16[128,2048]{1,0:T(8,128)(2,1)S(1)}, bf16[128,2048]{1,0:T(8,128)(2,1)S(1)}, u32[]{:S(2)}, u32[]{:S(2)}) collective-permute-start(bf16[128,2048]{1,0:T(8,128)(2,1)S(1)} %copy-done.2), channel_id=1, source_target_pairs={{0,1},{1,0},{2,3},{3,2},{4,5},{5,4},{6,7},{7,6},{8,9},{9,8},{10,11... | collective-permute-start | bytes 1572872 | tf_op jit(solution)/shard_map/ppermute | solution.py:23
  108.1 11.7 %collective-permute-start.14 = (bf16[4,2,16,512]{3,2,1,0:T(8,128)(2,1)S(1)}, bf16[4,2,16,512]{3,2,1,0:T(8,128)(2,1)S(1)}, u32[]{:S(2)}, u32[]{:S(2)}) collective-permute-start(bf16[4,2,16,512]{3,2,1,0:T(8,128)(2,1)S(1)} %copy-done.29), channel_id=1, source_target_pairs={{0,16},{16,32},{32,48},{48,64},{64,80},{80,96},{96,112},{1,17},{17... | collective-permute-start | bytes 393224 | tf_op jit(solution)/shard_map/ppermute | solution.py:44
  111.7 11.1 %collective-permute-start.15 = (bf16[4,2,16,512]{3,2,1,0:T(8,128)(2,1)S(1)}, bf16[4,2,16,512]{3,2,1,0:T(8,128)(2,1)S(1)}, u32[]{:S(2)}, u32[]{:S(2)}) collective-permute-start(bf16[4,2,16,512]{3,2,1,0:T(8,128)(2,1)S(1)} %copy-done.30), channel_id=1, source_target_pairs={{0,16},{16,32},{32,48},{48,64},{64,80},{80,96},{96,112},{1,17},{17... | collective-permute-start | bytes 393224 | tf_op jit(solution)/shard_map/ppermute | solution.py:44
  119.8 5.1 %copy-start.18 = (bf16[4,2,16,512]{3,2,1,0:T(8,128)(2,1)}, bf16[4,2,16,512]{3,2,1,0:T(8,128)(2,1)S(1)}, u32[]{:S(2)}) copy-start(bf16[4,2,16,512]{3,2,1,0:T(8,128)(2,1)S(1)} %collective-permute-done.14.refs_8_) | copy-start | bytes 393220
  119.8 4.2 %collective-permute-start.16 = (bf16[4,2,16,512]{3,2,1,0:T(8,128)(2,1)S(1)}, bf16[4,2,16,512]{3,2,1,0:T(8,128)(2,1)S(1)}, u32[]{:S(2)}, u32[]{:S(2)}) collective-permute-start(bf16[4,2,16,512]{3,2,1,0:T(8,128)(2,1)S(1)} %collective-permute-done.14.refs_8_), channel_id=1, source_target_pairs={{0,1},{1,0},{2,3},{3,2},{4,5},{5,4},{6,7},{7,6},{8,9},{9,8},{10,11... | collective-permute-start | bytes 393224 | tf_op jit(solution)/shard_map/ppermute | solution.py:23
  122.8 2.2 collective-permute-start.17
  139.4 8.1 %collective-permute-start.19 = (bf16[64,2176]{1,0:T(8,128)(2,1)}, bf16[64,2176]{1,0:T(8,128)(2,1)S(1)}, u32[]{:S(2)}, u32[]{:S(2)}) collective-permute-start(bf16[64,2176]{1,0:T(8,128)(2,1)} %get-tuple-element.94), channel_id=1, source_target_pairs={{0,8},{8,0},{1,9},{9,1},{2,10},{10,2},{3,11},{11,3},{4,12},{12,4},... | collective-permute-start | bytes 835592 | tf_op jit(solution)/shard_map/ppermute | solution.py:23
  139.7 8.2 %collective-permute-start.20 = (bf16[64,2176]{1,0:T(8,128)(2,1)}, bf16[64,2176]{1,0:T(8,128)(2,1)S(1)}, u32[]{:S(2)}, u32[]{:S(2)}) collective-permute-start(bf16[64,2176]{1,0:T(8,128)(2,1)} %get-tuple-element.101), channel_id=1, source_target_pairs={{0,6},{2,0},{4,2},{6,4},{1,7},{3,1},{5,3},{7,5},{8,14},{10,8},{12,... | collective-permute-start | bytes 835592 | tf_op jit(solution)/shard_map/ppermute | solution.py:23
  142.2 8.7 %collective-permute-start.21 = (bf16[64,2176]{1,0:T(8,128)(2,1)}, bf16[64,2176]{1,0:T(8,128)(2,1)S(1)}, u32[]{:S(2)}, u32[]{:S(2)}) collective-permute-start(bf16[64,2176]{1,0:T(8,128)(2,1)} %get-tuple-element.102), channel_id=1, source_target_pairs={{0,2},{2,4},{4,6},{6,0},{1,3},{3,5},{5,7},{7,1},{8,10},{10,12},{12... | collective-permute-start | bytes 835592 | tf_op jit(solution)/shard_map/ppermute | solution.py:23
  147.4 3.5 %copy-start.15 = (bf16[64,2176]{1,0:T(8,128)(2,1)}, bf16[64,2176]{1,0:T(8,128)(2,1)S(1)}, u32[]{:S(2)}) copy-start(bf16[64,2176]{1,0:T(8,128)(2,1)S(1)} %collective-permute-done.19.g0) | copy-start | bytes 835588
  147.9 3.0 %copy-start.16 = (bf16[64,2176]{1,0:T(8,128)(2,1)}, bf16[64,2176]{1,0:T(8,128)(2,1)S(1)}, u32[]{:S(2)}) copy-start(bf16[64,2176]{1,0:T(8,128)(2,1)S(1)} %collective-permute-done.20.g1) | copy-start | bytes 835588
  154.0 18.7 %collective-permute-start.22 = (bf16[192,2176]{1,0:T(8,128)(2,1)}, bf16[192,2176]{1,0:T(8,128)(2,1)S(1)}, u32[]{:S(2)}, u32[]{:S(2)}) collective-permute-start(bf16[192,2176]{1,0:T(8,128)(2,1)} %get-tuple-element.113), channel_id=1, source_target_pairs={{0,6},{2,0},{4,2},{6,4},{1,7},{3,1},{5,3},{7,5},{8,14},{10,8},{12,... | collective-permute-start | bytes 2506760 | tf_op jit(solution)/shard_map/ppermute | solution.py:23
  154.4 18.6 %collective-permute-start.23 = (bf16[192,2176]{1,0:T(8,128)(2,1)}, bf16[192,2176]{1,0:T(8,128)(2,1)S(1)}, u32[]{:S(2)}, u32[]{:S(2)}) collective-permute-start(bf16[192,2176]{1,0:T(8,128)(2,1)} %get-tuple-element.114), channel_id=1, source_target_pairs={{0,8},{8,0},{1,9},{9,1},{2,10},{10,2},{3,11},{11,3},{4,12},{12,4},... | collective-permute-start | bytes 2506760 | tf_op jit(solution)/shard_map/ppermute | solution.py:23
  155.5 19.5 %collective-permute-start.24 = (bf16[192,2176]{1,0:T(8,128)(2,1)}, bf16[192,2176]{1,0:T(8,128)(2,1)S(1)}, u32[]{:S(2)}, u32[]{:S(2)}) collective-permute-start(bf16[192,2176]{1,0:T(8,128)(2,1)} %get-tuple-element.103), channel_id=1, source_target_pairs={{0,2},{2,4},{4,6},{6,0},{1,3},{3,5},{5,7},{7,1},{8,10},{10,12},{12... | collective-permute-start | bytes 2506760 | tf_op jit(solution)/shard_map/ppermute | solution.py:23
  172.7 20.4 %collective-permute-start.26 = (bf16[192,2176]{1,0:T(8,128)(2,1)}, bf16[192,2176]{1,0:T(8,128)(2,1)S(1)}, u32[]{:S(2)}, u32[]{:S(2)}) collective-permute-start(bf16[192,2176]{1,0:T(8,128)(2,1)} %get-tuple-element.116), channel_id=1, source_target_pairs={{0,2},{2,4},{4,6},{6,0},{1,3},{3,5},{5,7},{7,1},{8,10},{10,12},{12... | collective-permute-start | bytes 2506760 | tf_op jit(solution)/shard_map/ppermute | solution.py:23
  172.7 2.3 %copy-start.10 = (bf16[192,2176]{1,0:T(8,128)(2,1)}, bf16[192,2176]{1,0:T(8,128)(2,1)S(1)}, u32[]{:S(2)}) copy-start(bf16[192,2176]{1,0:T(8,128)(2,1)S(1)} %collective-permute-done.22.r0) | copy-start | bytes 2506756
  175.9 4.7 %copy-start.22 = (s32[6,32]{1,0:T(8,128)S(1)}, s32[6,32]{1,0:T(8,128)}, u32[]{:S(2)}) copy-start(s32[6,32]{1,0:T(8,128)} %param.14) | copy-start | bytes 2308
  179.4 16.7 %collective-permute-start.25 = (bf16[192,2176]{1,0:T(8,128)(2,1)}, bf16[192,2176]{1,0:T(8,128)(2,1)S(1)}, u32[]{:S(2)}, u32[]{:S(2)}) collective-permute-start(bf16[192,2176]{1,0:T(8,128)(2,1)} %get-tuple-element.115), channel_id=1, source_target_pairs={{0,6},{2,0},{4,2},{6,4},{1,7},{3,1},{5,3},{7,5},{8,14},{10,8},{12,... | collective-permute-start | bytes 2506760 | tf_op jit(solution)/shard_map/ppermute | solution.py:23
  180.3 17.2 %collective-permute-start.27 = (bf16[192,2176]{1,0:T(8,128)(2,1)}, bf16[192,2176]{1,0:T(8,128)(2,1)S(1)}, u32[]{:S(2)}, u32[]{:S(2)}) collective-permute-start(bf16[192,2176]{1,0:T(8,128)(2,1)} %get-tuple-element.117), channel_id=1, source_target_pairs={{0,8},{8,0},{1,9},{9,1},{2,10},{10,2},{3,11},{11,3},{4,12},{12,4},... | collective-permute-start | bytes 2506760 | tf_op jit(solution)/shard_map/ppermute | solution.py:23
  193.1 4.4 %copy-start.7 = (bf16[192,2176]{1,0:T(8,128)(2,1)}, bf16[192,2176]{1,0:T(8,128)(2,1)S(1)}, u32[]{:S(2)}) copy-start(bf16[192,2176]{1,0:T(8,128)(2,1)S(1)} %collective-permute-done.26.m1) | copy-start | bytes 2506756
  198.4 18.5 %copy-start.23 = (s32[1024]{0:T(1024)S(1)}, s32[1024]{0:T(1024)}, u32[]{:S(2)}) copy-start(s32[1024]{0:T(1024)} %param.15) | copy-start | bytes 12292
  204.1 23.0 %all-to-all-start.3 = ((f32[128,1,256]{2,1,0:T(1,128)}), f32[128,1,256]{2,1,0:T(1,128)S(1)}, u32[]{:S(2)}, u32[]{:S(2)}) async-start(f32[128,1,256]{2,1,0:T(1,128)} %get-tuple-element.119), calls=%async_computation.3 | async-start | bytes 262144 | tf_op jit(solution)/shard_map/all_to_all | solution.py:679
  (15 other events, 16.1 us)
